TPU v7x, 256 devices: a whole 4x4x8 slice. The times are simulated.
256 devices in a mesh: row: 8 (over y, core), col: 32 (over x, z).
Axes of the slice: x: 4, y: 4, z: 8, core: 2. Of those that a mesh axis runs over, the one named last changes fastest.
Arguments:
- transmission: float32 [2, 2, 4096, 8192], P(None, None, 'row', 'col'), may hold values from -5 to 5
- probe_field: float32 [2, 256, 256], replicated, may hold values from -6 to 6
- prop_phase: float32 [256, 256], replicated, may hold values from -3.140625 to 3.140625
- amplitude: float32 [8, 32, 4, 256, 256], P('row', 'col'), may hold values from 0 to 2
- window_count: int32 [8, 32], P('row', 'col'), may hold values from 1 to 4
- offset_row: int32 [8, 32, 4], P('row', 'col'), may hold values from 0 to 384
- offset_col: int32 [8, 32, 4], P('row', 'col'), may hold values from 0 to 128
- window_batch: int32 [8, 32, 4], P('row', 'col'), may hold values from 0 to 2
Outputs:
- updated: float32 [2, 2, 4096, 8192], P(None, None, 'row', 'col')
All inputs are finite; a program needn't handle non-finite values.
Results may differ from a plain program's by a relative error of at most 0.0003.
Values sent between devices are 32-bit elements; how exact they have to be, the bound alone decides.
No kernel may reach another device: no remote copies, remote signals or barrier semaphores. Data moves between devices by JAX's collectives and lax.ppermute only.
A program may use at most 64 MiB of HBM per device.

v0:
```python
import math

import jax
import jax.numpy as jnp
import numpy as np
from jax import lax
from jax.experimental import pallas as pl
from jax.experimental.pallas import tpu as pltpu
from jax.sharding import PartitionSpec as P

BATCHES = 3
WIN = 256
HALF = 128
SLOTS = 4
ROWS = 512
COLS = 256
EXT_R = 640
EXT_C = 384


cc = jnp.concatenate
f32 = jnp.float32
bf16 = jnp.bfloat16


def dft_tables():
    n = np.arange(HALF)
    even = np.exp(-2j * np.pi * (np.outer(n, n) % HALF) / HALF) / math.sqrt(WIN)
    odd = np.exp(-2j * np.pi * n / WIN)[:, None] * even
    out = []
    for m in (even, odd):
        full = np.block([[m.real, m.imag], [-m.imag, m.real]]).astype(np.float32)
        for t in (full, full.T):
            hi = t.astype(bf16)
            lo = (t - hi.astype(np.float32)).astype(bf16)
            out.append(np.stack([hi, lo]))
    return np.stack(out).reshape(2, 2, 2, WIN, WIN)


def order_matrix():
    source = np.concatenate([np.arange(0, WIN, 2), np.arange(1, WIN, 2)])
    m = np.zeros((WIN, WIN), np.float32)
    m[source, np.arange(WIN)] = 1.0
    return np.stack([m, m.T]).astype(bf16)


def halves(x):
    hi = x.astype(bf16)
    lo = (x - hi.astype(f32)).astype(bf16)
    return hi, lo


def dot_r(x, tab, which, trans):
    hi, lo = halves(x)
    th = tab[which, trans, 0]
    t = cc([th, th, tab[which, trans, 1]], 0)
    return jnp.dot(cc([hi, lo, hi], 1), t, preferred_element_type=f32)


def dot_l(tab, which, trans, x):
    hi, lo = halves(x)
    th = tab[which, trans, 0]
    t = cc([th, th, tab[which, trans, 1]], 1)
    return jnp.dot(t, cc([hi, lo, hi], 0), preferred_element_type=f32)


def forward_two(z, tab):
    re, im = z
    h = HALF
    a = dot_r(cc([re[:, :h] + re[:, h:], im[:, :h] + im[:, h:]], 1), tab, 0, 0)
    b = dot_r(cc([re[:, :h] - re[:, h:], im[:, :h] - im[:, h:]], 1), tab, 1, 0)
    re, im = cc([a[:, :h], b[:, :h]], 1), cc([a[:, h:], b[:, h:]], 1)
    a = dot_l(tab, 0, 1, cc([re[:h] + re[h:], im[:h] + im[h:]], 0))
    b = dot_l(tab, 1, 1, cc([re[:h] - re[h:], im[:h] - im[h:]], 0))
    return cc([a[:h], b[:h]], 0), cc([a[h:], b[h:]], 0)


def inverse_two(z, tab):
    re, im = z
    h = HALF
    a = dot_l(tab, 0, 0, cc([re[:h], im[:h]], 0))
    b = dot_l(tab, 1, 0, cc([re[h:], im[h:]], 0))
    s, d = a + b, a - b
    re, im = cc([s[:h], d[:h]], 0), cc([s[h:], d[h:]], 0)
    a = dot_r(cc([re[:, :h], im[:, :h]], 1), tab, 0, 1)
    b = dot_r(cc([re[:, h:], im[:, h:]], 1), tab, 1, 1)
    s, d = a + b, a - b
    return cc([s[:, :h], d[:, :h]], 1), cc([s[:, h:], d[:, h:]], 1)


def cmul(a, b):
    return a[0] * b[0] - a[1] * b[1], a[0] * b[1] + a[1] * b[0]


def cjmul(a, b):
    return a[0] * b[0] + a[1] * b[1], a[0] * b[1] - a[1] * b[0]


def place(r):
    base = pl.multiple_of(jnp.minimum(r // 8 * 8, EXT_R - WIN - 8), 8)
    return base, r - base


def load_window(ref, first, r, c):
    base, shift = place(r)
    out = []
    for p in (first, first + 1):
        t = ref[p, pl.ds(base, WIN + 8), :]
        t = pltpu.roll(t, lax.rem(EXT_C - c, EXT_C), 1)[:, :WIN]
        out.append(pltpu.roll(t, lax.rem(WIN + 8 - shift, WIN + 8), 0)[:WIN])
    return out


def add_window(ref, first, r, c, g):
    base, shift = place(r)
    for p in (first, first + 1):
        t = pltpu.roll(cc([g[p - first], jnp.zeros((8, WIN), f32)], 0), shift, 0)
        t = pltpu.roll(cc([t, jnp.zeros((WIN + 8, EXT_C - WIN), f32)], 1), c, 1)
        ref[p, pl.ds(base, WIN + 8), :] = ref[p, pl.ds(base, WIN + 8), :] + t


def reorder(x, order):
    a = x.astype(bf16)
    rest = x - a.astype(f32)
    b = rest.astype(bf16)
    c = (rest - b.astype(f32)).astype(bf16)
    m = order[0]
    y = jnp.dot(a, m, preferred_element_type=f32)
    y = y + jnp.dot(b, m, preferred_element_type=f32)
    y = y + jnp.dot(c, m, preferred_element_type=f32)
    a = y.astype(bf16)
    rest = y - a.astype(f32)
    b = rest.astype(bf16)
    c = (rest - b.astype(f32)).astype(bf16)
    m = order[1]
    y = jnp.dot(m, a, preferred_element_type=f32)
    y = y + jnp.dot(m, b, preferred_element_type=f32)
    return y + jnp.dot(m, c, preferred_element_type=f32)


def prep_kernel(amp, phase, order, amp_out, prop_out):
    def step(s, _):
        amp_out[s] = reorder(amp[0, 0, s], order)
        return 0

    lax.fori_loop(0, SLOTS, step, 0)
    ph = reorder(phase[...], order)
    prop_out[0] = jnp.cos(ph)
    prop_out[1] = jnp.sin(ph)


def inside(axis):
    return lax.axis_index(axis) < lax.axis_size(axis) - 1


def assemble_kernel(main, right_top, right_rest, bottom, state):
    for p in range(4):
        q = (p // 2, p % 2)
        state[p, :ROWS, :COLS] = main[q]
        state[p, :HALF, COLS:] = right_top[p]
        state[p, HALF:ROWS, COLS:] = right_rest[p]
        state[p, ROWS:, :] = bottom[p]


def batch_kernel(batch, first):
    def run(count, orow, ocol, wbatch, tab, probe, prop, amp, *rest):
        if first:
            (old,) = rest[:1]
            state, grad, side_l, side_r, top, bottom = rest[1:]
            state = old
        else:
            old, mid_l, mid_r, end_l, end_r = rest[:5]
            state, grad, side_l, side_r, top, bottom = rest[5:]
            scale = jnp.where(inside("col"), 0.5, 0.0).astype(f32)
            drop = jnp.where(inside("row"), 1.0, 0.0).astype(f32)
            for p in range(4):
                for cols, fac, mid, end in (
                    (pl.ds(0, HALF), jnp.float32(0.5), mid_l, end_l),
                    (pl.ds(COLS, HALF), scale, mid_r, end_r),
                ):
                    state[p, :HALF, cols] = old[p, :HALF, cols] - fac * end[p, :HALF]
                    state[p, HALF:ROWS, cols] = old[p, HALF:ROWS, cols] - fac * mid[p]
                    state[p, ROWS:, cols] = old[p, ROWS:, cols] - (fac * drop) * end[p, HALF:]
        grad[...] = jnp.zeros_like(grad)

        def step(s, _):
            @pl.when((s < count[0, 0]) & (wbatch[0, 0, s] == batch))
            def _():
                r = orow[0, 0, s]
                c = ocol[0, 0, s]
                psi = cmul((probe[0], probe[1]), load_window(state, 0, r, c))
                f = forward_two(psi, tab)
                bt = inverse_two(cmul((prop[0], prop[1]), f), tab)
                w2 = load_window(state, 2, r, c)
                far = forward_two(cmul(bt, w2), tab)
                power = far[0] * far[0] + far[1] * far[1]
                factor = 1.0 - amp[s] * lax.rsqrt(jnp.maximum(power, 1.0))
                back = inverse_two((far[0] * factor, far[1] * factor), tab)
                add_window(grad, 2, r, c, cjmul(bt, back))
                f = forward_two(cjmul(w2, back), tab)
                back = inverse_two(cjmul((prop[0], prop[1]), f), tab)
                add_window(grad, 0, r, c, cjmul((probe[0], probe[1]), back))

            return 0

        lax.fori_loop(0, SLOTS, step, 0)
        side_l[...] = grad[:, HALF:ROWS, :HALF]
        side_r[...] = grad[:, HALF:ROWS, COLS:]
        top[...] = grad[:, :HALF, :]
        bottom[...] = grad[:, ROWS:, :]

    return run


def settle_kernel(state, grad, above, below, out, end_l, end_r):
    in_r = jnp.where(inside("row"), 0.5, 0.0).astype(f32)
    in_c = jnp.where(inside("col"), 1.0, 0.0).astype(f32)
    h = HALF
    for p in range(4):
        for at in range(0, EXT_R, h):
            rows = pl.ds(at, h)
            g = grad[p, rows, :]
            if at == 0:
                g = g + above[p]
                end_l[p, :h] = g[:, :h]
                end_r[p, :h] = g[:, COLS:]
            if at == ROWS:
                g = g + below[p]
                end_l[p, h:] = g[:, :h]
                end_r[p, h:] = g[:, COLS:]
            scale = in_r if at == ROWS else jnp.float32(0.5)
            out[p, rows, :COLS] = state[p, rows, :COLS] - scale * g[:, :COLS]
            out[p, rows, COLS:] = state[p, rows, COLS:] - (scale * in_c) * g[:, COLS:]


def final_settle_kernel(state, grad, above, out, end_r):
    h = HALF
    for p in range(4):
        for at in range(0, ROWS, h):
            rows = pl.ds(at, h)
            g = grad[p, rows, :]
            if at == 0:
                g = g + above[p]
                end_r[p] = g[:, COLS:]
            out[p, rows] = state[p, rows, :COLS] - 0.5 * g[:, :COLS]


def last_kernel(state, mid, end, out):
    h = HALF
    for p in range(4):
        q = (p // 2, p % 2)
        out[(*q, slice(0, h), slice(0, h))] = state[p, :h, :h] - 0.5 * end[p]
        out[(*q, slice(h, ROWS), slice(0, h))] = state[p, h:, :h] - 0.5 * mid[p]
        out[(*q, slice(0, ROWS), slice(h, COLS))] = state[p, :, h:]


VM = pl.BlockSpec(memory_space=pltpu.VMEM)
SM = pl.BlockSpec(memory_space=pltpu.SMEM)
EXT = (4, EXT_R, EXT_C)
FLAT = (4, HALF, EXT_C)
MIDS = (4, ROWS - HALF, HALF)
ENDS = (4, 2 * HALF, HALF)


def call(kernel, scalars, arrays, outs, alias=None, limit=24):
    return pl.pallas_call(
        kernel,
        in_specs=[SM] * len(scalars) + [VM] * len(arrays),
        out_specs=[VM] * len(outs),
        out_shape=[jax.ShapeDtypeStruct(s, f32) for s in outs],
        input_output_aliases=alias or {},
        compiler_params=pltpu.CompilerParams(vmem_limit_bytes=limit * 2**20),
    )(*scalars, *arrays)


def from_behind(array, axis, by):
    size = lax.axis_size(axis)
    pairs = [(i, i + by) for i in range(size) if 0 <= i + by < size]
    return lax.ppermute(array, axis, pairs)


def body(transmission, probe, phase, amplitude, count, orow, ocol, wbatch):
    tab = jnp.asarray(dft_tables())
    order = jnp.asarray(order_matrix())
    scalars = (count, orow, ocol, wbatch)
    h = HALF
    planes = transmission.reshape(4, ROWS, COLS)
    right_top = from_behind(planes[:, :h, :h], "col", -1)
    right_rest = from_behind(planes[:, h:, :h], "col", -1)
    amp, prop = call(
        prep_kernel, (), (amplitude, phase, order), [(SLOTS, WIN, WIN), (2, WIN, WIN)]
    )
    low = cc([planes[:, :h, :], right_top], 2)
    bottom = from_behind(low, "row", -1)
    (state,) = call(
        assemble_kernel, (), (transmission, right_top, right_rest, bottom), [EXT]
    )
    parts = ()
    for b in range(BATCHES):
        state, grad, side_l, side_r, top, low = call(
            batch_kernel(b, b == 0),
            scalars,
            (tab, probe, prop, amp, state, *parts),
            [EXT, EXT, MIDS, MIDS, FLAT, FLAT],
            {8: 0},
        )
        mid_l = from_behind(side_r, "col", 1)
        above = from_behind(low, "row", 1)
        if b == BATCHES - 1:
            break
        mid_r = from_behind(side_l, "col", -1)
        below = from_behind(top, "row", -1)
        state, end_l, end_r = call(
            settle_kernel, (), (state, grad, above, below), [EXT, ENDS, ENDS], {0: 0}
        )
        parts = (
            mid_l, mid_r, from_behind(end_r, "col", 1), from_behind(end_l, "col", -1)
        )
    main, end_r = call(
        final_settle_kernel, (), (state, grad, above), [(4, ROWS, COLS), (4, h, h)]
    )
    end_l = from_behind(end_r, "col", 1)
    return call(last_kernel, (), (main, mid_l, end_l), [(2, 2, ROWS, COLS)])[0]


def solution(mesh):
    in_specs = (
        P(None, None, "row", "col"),
        P(),
        P(),
        P("row", "col", None, None, None),
        P("row", "col"),
        P("row", "col", None),
        P("row", "col", None),
        P("row", "col", None),
    )
    out_specs = P(None, None, "row", "col")
    return jax.shard_map(body, mesh=mesh, in_specs=in_specs, out_specs=out_specs, check_vma=False)
```

profile of v0, /device:TPU:22, one launch (start us, length us, event | category | flops | bytes accessed | tf_op | source)
XLA Modules:
  0.0 193.2 jit_solution(7651040499168262704)
XLA Ops:
  1.2 8.2 %collective-permute-start = (f32[4,128,128]{2,1,0:T(8,128)S(1)}, f32[4,128,128]{2,1,0:T(8,128)S(1)}, u32[]{:S(2)}, u32[]{:S(2)}) collective-permute-start(f32[4,128,128]{2,1,0:T(8,128)S(1)} %slice.12), channel_id=1, source_target_pairs={{1,0},{2,1},{3,2},{4,3},{5,4},{6,5},{7,6},{8,7},{9,8},{10,9},{11,1... | collective-permute-start | bytes 786440 | tf_op jit(solution)/shard_map/ppermute | solution.py:279
  10.5 2.9 %collective-permute-start.1 = (f32[4,384,128]{2,1,0:T(8,128)S(1)}, f32[4,384,128]{2,1,0:T(8,128)S(1)}, u32[]{:S(2)}, u32[]{:S(2)}) collective-permute-start(f32[4,384,128]{2,1,0:T(8,128)S(1)} %slice.13), channel_id=1, source_target_pairs={{1,0},{2,1},{3,2},{4,3},{5,4},{6,5},{7,6},{8,7},{9,8},{10,9},{11,1... | collective-permute-start | bytes 2359304 | tf_op jit(solution)/shard_map/ppermute | solution.py:279
  16.1 1.9 collective-permute-start.2
  18.7 4.2 %shard_map.100 = (f32[4,256,256]{2,1,0:T(8,128)S(1)}, f32[2,256,256]{2,1,0:T(8,128)S(1)}) custom-call(f32[1,1,4,256,256]{4,3,2,1,0:T(8,128)S(1)} %copy-done.3, f32[256,256]{1,0:T(8,128)S(1)} %copy-done.4, bf16[2,256,256]{2,1,0:T(8,128)(2,1)S(1)} %copy-done.5), custom_call_target="tpu_custom_call" | custom-call | tf_op jit(solution)/shard_map/pallas_call | solution.py:266
  22.9 8.8 %collective-permute-done.1.right_rest = f32[4,384,128]{2,1,0:T(8,128)S(1)} collective-permute-done((f32[4,384,128]{2,1,0:T(8,128)S(1)}, f32[4,384,128]{2,1,0:T(8,128)S(1)}, u32[]{:S(2)}, u32[]{:S(2)}) %collective-permute-start.1) | collective-permute-done | bytes 786464 | tf_op jit(solution)/shard_map/ppermute | solution.py:279
  32.0 6.4 %shard_map.102 = (f32[4,640,384]{2,1,0:T(8,128)S(1)}, f32[4,640,384]{2,1,0:T(8,128)S(1)}, f32[4,384,128]{2,1,0:T(8,128)S(1)}, f32[4,384,128]{2,1,0:T(8,128)S(1)}...) custom-call(s32[1,1]{1,0:T(1,128)S(6)} %copy.21.count, ...), custom_call_target="tpu_custom_call", output_to_operand_aliasing={{0}: (8, {})} | custom-call | tf_op jit(solution)/shard_map/pallas_call | solution.py:266
  38.5 1.9 collective-permute-start.3
  40.4 3.6 %collective-permute-start.4 = (f32[4,128,384]{2,1,0:T(8,128)S(1)}, f32[4,128,384]{2,1,0:T(8,128)S(1)}, u32[]{:S(2)}, u32[]{:S(2)}) collective-permute-start(f32[4,128,384]{2,1,0:T(8,128)S(1)} %get-tuple-element.36), channel_id=1, source_target_pairs={{32,0},{64,32},{96,64},{128,96},{160,128},{192,160},{224,192},{33,... | collective-permute-start | bytes 2359304 | tf_op jit(solution)/shard_map/ppermute | solution.py:279
  44.1 14.1 %collective-permute-start.5 = (f32[4,384,128]{2,1,0:T(8,128)S(1)}, f32[4,384,128]{2,1,0:T(8,128)S(1)}, u32[]{:S(2)}, u32[]{:S(2)}) collective-permute-start(f32[4,384,128]{2,1,0:T(8,128)S(1)} %get-tuple-element.38), channel_id=1, source_target_pairs={{0,1},{1,2},{2,3},{3,4},{4,5},{5,6},{6,7},{7,8},{8,9},{9,10},{10,1... | collective-permute-start | bytes 2359304 | tf_op jit(solution)/shard_map/ppermute | solution.py:279
  58.1 1.9 collective-permute-start.6
  61.1 7.5 %collective-permute-start.7 = (f32[4,256,128]{2,1,0:T(8,128)S(1)}, f32[4,256,128]{2,1,0:T(8,128)S(1)}, u32[]{:S(2)}, u32[]{:S(2)}) collective-permute-start(f32[4,256,128]{2,1,0:T(8,128)S(1)} %get-tuple-element.40), channel_id=1, source_target_pairs={{0,1},{1,2},{2,3},{3,4},{4,5},{5,6},{6,7},{7,8},{8,9},{9,10},{10,1... | collective-permute-start | bytes 1572872 | tf_op jit(solution)/shard_map/ppermute | solution.py:279
  68.6 2.1 %collective-permute-start.8 = (f32[4,256,128]{2,1,0:T(8,128)S(1)}, f32[4,256,128]{2,1,0:T(8,128)S(1)}, u32[]{:S(2)}, u32[]{:S(2)}) collective-permute-start(f32[4,256,128]{2,1,0:T(8,128)S(1)} %get-tuple-element.41), channel_id=1, source_target_pairs={{1,0},{2,1},{3,2},{4,3},{5,4},{6,5},{7,6},{8,7},{9,8},{10,9},{11,1... | collective-permute-start | bytes 1572872 | tf_op jit(solution)/shard_map/ppermute | solution.py:279
  70.7 5.3 %collective-permute-done.5.rest_1_ = f32[4,384,128]{2,1,0:T(8,128)S(1)} collective-permute-done((f32[4,384,128]{2,1,0:T(8,128)S(1)}, f32[4,384,128]{2,1,0:T(8,128)S(1)}, u32[]{:S(2)}, u32[]{:S(2)}) %collective-permute-start.5) | collective-permute-done | bytes 786464 | tf_op jit(solution)/shard_map/ppermute | solution.py:279
  76.1 4.4 %collective-permute-done.6.rest_2_ = f32[4,384,128]{2,1,0:T(8,128)S(1)} collective-permute-done((f32[4,384,128]{2,1,0:T(8,128)S(1)}, f32[4,384,128]{2,1,0:T(8,128)S(1)}, u32[]{:S(2)}, u32[]{:S(2)}) %collective-permute-start.6) | collective-permute-done | bytes 786464 | tf_op jit(solution)/shard_map/ppermute | solution.py:279
  80.5 6.4 %collective-permute-done.7.rest_3_ = f32[4,256,128]{2,1,0:T(8,128)S(1)} collective-permute-done((f32[4,256,128]{2,1,0:T(8,128)S(1)}, f32[4,256,128]{2,1,0:T(8,128)S(1)}, u32[]{:S(2)}, u32[]{:S(2)}) %collective-permute-start.7) | collective-permute-done | bytes 524320 | tf_op jit(solution)/shard_map/ppermute | solution.py:279
  86.8 4.1 %collective-permute-done.8.rest_4_ = f32[4,256,128]{2,1,0:T(8,128)S(1)} collective-permute-done((f32[4,256,128]{2,1,0:T(8,128)S(1)}, f32[4,256,128]{2,1,0:T(8,128)S(1)}, u32[]{:S(2)}, u32[]{:S(2)}) %collective-permute-start.8) | collective-permute-done | bytes 524320 | tf_op jit(solution)/shard_map/ppermute | solution.py:279
  90.9 12.3 %shard_map.104 = (f32[4,640,384]{2,1,0:T(8,128)S(1)}, f32[4,640,384]{2,1,0:T(8,128)S(1)}, f32[4,384,128]{2,1,0:T(8,128)S(1)}, f32[4,384,128]{2,1,0:T(8,128)S(1)}...) custom-call(s32[1,1]{1,0:T(1,128)S(6)} %copy.21.count, ...), custom_call_target="tpu_custom_call", output_to_operand_aliasing={{0}: (8, {})} | custom-call | tf_op jit(solution)/shard_map/pallas_call | solution.py:266
  103.3 1.9 collective-permute-start.9
  105.2 3.6 %collective-permute-start.10 = (f32[4,128,384]{2,1,0:T(8,128)S(1)}, f32[4,128,384]{2,1,0:T(8,128)S(1)}, u32[]{:S(2)}, u32[]{:S(2)}) collective-permute-start(f32[4,128,384]{2,1,0:T(8,128)S(1)} %get-tuple-element.45), channel_id=1, source_target_pairs={{32,0},{64,32},{96,64},{128,96},{160,128},{192,160},{224,192},{33,... | collective-permute-start | bytes 2359304 | tf_op jit(solution)/shard_map/ppermute | solution.py:279
  108.9 1.9 collective-permute-start.11
  110.8 6.0 %collective-permute-start.12 = (f32[4,384,128]{2,1,0:T(8,128)S(1)}, f32[4,384,128]{2,1,0:T(8,128)S(1)}, u32[]{:S(2)}, u32[]{:S(2)}) collective-permute-start(f32[4,384,128]{2,1,0:T(8,128)S(1)} %get-tuple-element.48), channel_id=1, source_target_pairs={{1,0},{2,1},{3,2},{4,3},{5,4},{6,5},{7,6},{8,7},{9,8},{10,9},{11,1... | collective-permute-start | bytes 2359304 | tf_op jit(solution)/shard_map/ppermute | solution.py:279
  121.2 6.0 %collective-permute-start.14 = (f32[4,256,128]{2,1,0:T(8,128)S(1)}, f32[4,256,128]{2,1,0:T(8,128)S(1)}, u32[]{:S(2)}, u32[]{:S(2)}) collective-permute-start(f32[4,256,128]{2,1,0:T(8,128)S(1)} %get-tuple-element.50), channel_id=1, source_target_pairs={{1,0},{2,1},{3,2},{4,3},{5,4},{6,5},{7,6},{8,7},{9,8},{10,9},{11,1... | collective-permute-start | bytes 1572872 | tf_op jit(solution)/shard_map/ppermute | solution.py:279
  127.3 6.0 %collective-permute-done.11.rest_1_ = f32[4,384,128]{2,1,0:T(8,128)S(1)} collective-permute-done((f32[4,384,128]{2,1,0:T(8,128)S(1)}, f32[4,384,128]{2,1,0:T(8,128)S(1)}, u32[]{:S(2)}, u32[]{:S(2)}) %collective-permute-start.11) | collective-permute-done | bytes 786464 | tf_op jit(solution)/shard_map/ppermute | solution.py:279
  133.3 2.9 %collective-permute-done.12.rest_2_ = f32[4,384,128]{2,1,0:T(8,128)S(1)} collective-permute-done((f32[4,384,128]{2,1,0:T(8,128)S(1)}, f32[4,384,128]{2,1,0:T(8,128)S(1)}, u32[]{:S(2)}, u32[]{:S(2)}) %collective-permute-start.12) | collective-permute-done | bytes 786464 | tf_op jit(solution)/shard_map/ppermute | solution.py:279
  136.2 6.1 %collective-permute-done.13.rest_3_ = f32[4,256,128]{2,1,0:T(8,128)S(1)} collective-permute-done((f32[4,256,128]{2,1,0:T(8,128)S(1)}, f32[4,256,128]{2,1,0:T(8,128)S(1)}, u32[]{:S(2)}, u32[]{:S(2)}) %collective-permute-start.13) | collective-permute-done | bytes 524320 | tf_op jit(solution)/shard_map/ppermute | solution.py:279
  142.3 2.9 %collective-permute-done.14.rest_4_ = f32[4,256,128]{2,1,0:T(8,128)S(1)} collective-permute-done((f32[4,256,128]{2,1,0:T(8,128)S(1)}, f32[4,256,128]{2,1,0:T(8,128)S(1)}, u32[]{:S(2)}, u32[]{:S(2)}) %collective-permute-start.14) | collective-permute-done | bytes 524320 | tf_op jit(solution)/shard_map/ppermute | solution.py:279
  145.3 8.1 %shard_map.106 = (f32[4,640,384]{2,1,0:T(8,128)S(1)}, f32[4,640,384]{2,1,0:T(8,128)S(1)}, f32[4,384,128]{2,1,0:T(8,128)}, f32[4,384,128]{2,1,0:T(8,128)S(1)}, f3...) custom-call(s32[1,1]{1,0:T(1,128)S(6)} %copy.21.count, ...), custom_call_target="tpu_custom_call", output_to_operand_aliasing={{0}: (8, {})} | custom-call | tf_op jit(solution)/shard_map/pallas_call | solution.py:266
  155.3 3.6 %collective-permute-start.16 = (f32[4,384,128]{2,1,0:T(8,128)S(1)}, f32[4,384,128]{2,1,0:T(8,128)S(1)}, u32[]{:S(2)}, u32[]{:S(2)}) collective-permute-start(f32[4,384,128]{2,1,0:T(8,128)S(1)} %get-tuple-element.55), channel_id=1, source_target_pairs={{0,1},{1,2},{2,3},{3,4},{4,5},{5,6},{6,7},{7,8},{8,9},{9,10},{10,1... | collective-permute-start | bytes 2359304 | tf_op jit(solution)/shard_map/ppermute | solution.py:279
  159.0 7.7 %collective-permute-done.15.above = f32[4,128,384]{2,1,0:T(8,128)S(1)} collective-permute-done((f32[4,128,384]{2,1,0:T(8,128)S(1)}, f32[4,128,384]{2,1,0:T(8,128)S(1)}, u32[]{:S(2)}, u32[]{:S(2)}) %collective-permute-start.15) | collective-permute-done | bytes 786464 | tf_op jit(solution)/shard_map/ppermute | solution.py:279
  167.0 3.6 %collective-permute-start.17 = (f32[4,128,128]{2,1,0:T(8,128)S(1)}, f32[4,128,128]{2,1,0:T(8,128)S(1)}, u32[]{:S(2)}, u32[]{:S(2)}) collective-permute-start(f32[4,128,128]{2,1,0:T(8,128)S(1)} %get-tuple-element.56), channel_id=1, source_target_pairs={{0,1},{1,2},{2,3},{3,4},{4,5},{5,6},{6,7},{7,8},{8,9},{9,10},{10,1... | collective-permute-start | bytes 786440 | tf_op jit(solution)/shard_map/ppermute | solution.py:279
  170.6 16.1 %collective-permute-done.16.mid = f32[4,384,128]{2,1,0:T(8,128)S(1)} collective-permute-done((f32[4,384,128]{2,1,0:T(8,128)S(1)}, f32[4,384,128]{2,1,0:T(8,128)S(1)}, u32[]{:S(2)}, u32[]{:S(2)}) %collective-permute-start.16) | collective-permute-done | bytes 786464 | tf_op jit(solution)/shard_map/ppermute | solution.py:279
  186.8 4.9 %collective-permute-done.17.end = f32[4,128,128]{2,1,0:T(8,128)S(1)} collective-permute-done((f32[4,128,128]{2,1,0:T(8,128)S(1)}, f32[4,128,128]{2,1,0:T(8,128)S(1)}, u32[]{:S(2)}, u32[]{:S(2)}) %collective-permute-start.17) | collective-permute-done | bytes 262176 | tf_op jit(solution)/shard_map/ppermute | solution.py:279
  (35 shorter events, 14.3 us)
Async XLA Ops:
  0.0 18.6 %copy-start.5 = (bf16[2,256,256]{2,1,0:T(8,128)(2,1)S(1)}, bf16[2,256,256]{2,1,0:T(8,128)(2,1)}, u32[]{:S(2)}) copy-start(bf16[2,256,256]{2,1,0:T(8,128)(2,1)} %constant.5.clone.order) | copy-start | bytes 786436
  0.0 31.7 %copy-start.1 = (f32[2,2,512,256]{3,2,1,0:T(8,128)S(1)}, f32[2,2,512,256]{3,2,1,0:T(8,128)}, u32[]{:S(2)}) copy-start(f32[2,2,512,256]{3,2,1,0:T(8,128)} %main.1) | copy-start | bytes 6291460
  0.0 18.6 %copy-start.3 = (f32[1,1,4,256,256]{4,3,2,1,0:T(8,128)S(1)}, f32[1,1,4,256,256]{4,3,2,1,0:T(8,128)}, u32[]{:S(2)}) copy-start(f32[1,1,4,256,256]{4,3,2,1,0:T(8,128)} %amp.1) | copy-start | bytes 3145732
  0.0 18.6 %copy-start.4 = (f32[256,256]{1,0:T(8,128)S(1)}, f32[256,256]{1,0:T(8,128)}, u32[]{:S(2)}) copy-start(f32[256,256]{1,0:T(8,128)} %phase.1) | copy-start | bytes 786436
  1.2 14.8 %collective-permute-start = (f32[4,128,128]{2,1,0:T(8,128)S(1)}, f32[4,128,128]{2,1,0:T(8,128)S(1)}, u32[]{:S(2)}, u32[]{:S(2)}) collective-permute-start(f32[4,128,128]{2,1,0:T(8,128)S(1)} %slice.12), channel_id=1, source_target_pairs={{1,0},{2,1},{3,2},{4,3},{5,4},{6,5},{7,6},{8,7},{9,8},{10,9},{11,1... | collective-permute-start | bytes 786440 | tf_op jit(solution)/shard_map/ppermute | solution.py:279
  10.5 21.2 %collective-permute-start.1 = (f32[4,384,128]{2,1,0:T(8,128)S(1)}, f32[4,384,128]{2,1,0:T(8,128)S(1)}, u32[]{:S(2)}, u32[]{:S(2)}) collective-permute-start(f32[4,384,128]{2,1,0:T(8,128)S(1)} %slice.13), channel_id=1, source_target_pairs={{1,0},{2,1},{3,2},{4,3},{5,4},{6,5},{7,6},{8,7},{9,8},{10,9},{11,1... | collective-permute-start | bytes 2359304 | tf_op jit(solution)/shard_map/ppermute | solution.py:279
  16.1 15.7 %collective-permute-start.2 = (f32[4,128,384]{2,1,0:T(8,128)S(1)}, f32[4,128,384]{2,1,0:T(8,128)S(1)}, u32[]{:S(2)}, u32[]{:S(2)}) collective-permute-start(f32[4,128,384]{2,1,0:T(8,128)S(1)} %pad_maximum_fusion), channel_id=1, source_target_pairs={{32,0},{64,32},{96,64},{128,96},{160,128},{192,160},{224,192},{33,... | collective-permute-start | bytes 2359304 | tf_op jit(solution)/shard_map/ppermute | solution.py:279
  22.8 9.1 %copy-start = (bf16[2,2,2,256,256]{4,3,2,1,0:T(8,128)(2,1)S(1)}, bf16[2,2,2,256,256]{4,3,2,1,0:T(8,128)(2,1)}, u32[]{:S(2)}) copy-start(bf16[2,2,2,256,256]{4,3,2,1,0:T(8,128)(2,1)} %constant.4.clone.tab) | copy-start | bytes 3145732
  22.9 9.1 %copy-start.2 = (f32[2,256,256]{2,1,0:T(8,128)S(1)}, f32[2,256,256]{2,1,0:T(8,128)}, u32[]{:S(2)}) copy-start(f32[2,256,256]{2,1,0:T(8,128)} %probe.5) | copy-start | bytes 1572868
  22.9 9.1 %copy-start.6 = (s32[1,1,4]{2,1,0:T(1,128)S(1)}, s32[1,1,4]{2,1,0:T(1,128)}, u32[]{:S(2)}) copy-start(s32[1,1,4]{2,1,0:T(1,128)} %orow.5) | copy-start | bytes 52
  22.9 9.1 %copy-start.7 = (s32[1,1,4]{2,1,0:T(1,128)S(1)}, s32[1,1,4]{2,1,0:T(1,128)}, u32[]{:S(2)}) copy-start(s32[1,1,4]{2,1,0:T(1,128)} %ocol.5) | copy-start | bytes 52
  22.9 9.1 %copy-start.8 = (s32[1,1,4]{2,1,0:T(1,128)S(1)}, s32[1,1,4]{2,1,0:T(1,128)}, u32[]{:S(2)}) copy-start(s32[1,1,4]{2,1,0:T(1,128)} %wbatch.5) | copy-start | bytes 52
  38.5 21.6 %collective-permute-start.3 = (f32[4,128,384]{2,1,0:T(8,128)S(1)}, f32[4,128,384]{2,1,0:T(8,128)S(1)}, u32[]{:S(2)}, u32[]{:S(2)}) collective-permute-start(f32[4,128,384]{2,1,0:T(8,128)S(1)} %get-tuple-element.35), channel_id=1, source_target_pairs={{0,32},{32,64},{64,96},{96,128},{128,160},{160,192},{192,224},{1,3... | collective-permute-start | bytes 2359304 | tf_op jit(solution)/shard_map/ppermute | solution.py:279
  40.4 19.7 %collective-permute-start.4 = (f32[4,128,384]{2,1,0:T(8,128)S(1)}, f32[4,128,384]{2,1,0:T(8,128)S(1)}, u32[]{:S(2)}, u32[]{:S(2)}) collective-permute-start(f32[4,128,384]{2,1,0:T(8,128)S(1)} %get-tuple-element.36), channel_id=1, source_target_pairs={{32,0},{64,32},{96,64},{128,96},{160,128},{192,160},{224,192},{33,... | collective-permute-start | bytes 2359304 | tf_op jit(solution)/shard_map/ppermute | solution.py:279
  44.1 32.0 %collective-permute-start.5 = (f32[4,384,128]{2,1,0:T(8,128)S(1)}, f32[4,384,128]{2,1,0:T(8,128)S(1)}, u32[]{:S(2)}, u32[]{:S(2)}) collective-permute-start(f32[4,384,128]{2,1,0:T(8,128)S(1)} %get-tuple-element.38), channel_id=1, source_target_pairs={{0,1},{1,2},{2,3},{3,4},{4,5},{5,6},{6,7},{7,8},{8,9},{9,10},{10,1... | collective-permute-start | bytes 2359304 | tf_op jit(solution)/shard_map/ppermute | solution.py:279
  58.1 22.3 %collective-permute-start.6 = (f32[4,384,128]{2,1,0:T(8,128)S(1)}, f32[4,384,128]{2,1,0:T(8,128)S(1)}, u32[]{:S(2)}, u32[]{:S(2)}) collective-permute-start(f32[4,384,128]{2,1,0:T(8,128)S(1)} %get-tuple-element.39), channel_id=1, source_target_pairs={{1,0},{2,1},{3,2},{4,3},{5,4},{6,5},{7,6},{8,7},{9,8},{10,9},{11,1... | collective-permute-start | bytes 2359304 | tf_op jit(solution)/shard_map/ppermute | solution.py:279
  61.1 25.7 %collective-permute-start.7 = (f32[4,256,128]{2,1,0:T(8,128)S(1)}, f32[4,256,128]{2,1,0:T(8,128)S(1)}, u32[]{:S(2)}, u32[]{:S(2)}) collective-permute-start(f32[4,256,128]{2,1,0:T(8,128)S(1)} %get-tuple-element.40), channel_id=1, source_target_pairs={{0,1},{1,2},{2,3},{3,4},{4,5},{5,6},{6,7},{7,8},{8,9},{9,10},{10,1... | collective-permute-start | bytes 1572872 | tf_op jit(solution)/shard_map/ppermute | solution.py:279
  68.6 22.3 %collective-permute-start.8 = (f32[4,256,128]{2,1,0:T(8,128)S(1)}, f32[4,256,128]{2,1,0:T(8,128)S(1)}, u32[]{:S(2)}, u32[]{:S(2)}) collective-permute-start(f32[4,256,128]{2,1,0:T(8,128)S(1)} %get-tuple-element.41), channel_id=1, source_target_pairs={{1,0},{2,1},{3,2},{4,3},{5,4},{6,5},{7,6},{8,7},{9,8},{10,9},{11,1... | collective-permute-start | bytes 1572872 | tf_op jit(solution)/shard_map/ppermute | solution.py:279
  103.3 13.5 %collective-permute-start.9 = (f32[4,128,384]{2,1,0:T(8,128)S(1)}, f32[4,128,384]{2,1,0:T(8,128)S(1)}, u32[]{:S(2)}, u32[]{:S(2)}) collective-permute-start(f32[4,128,384]{2,1,0:T(8,128)S(1)} %get-tuple-element.44), channel_id=1, source_target_pairs={{0,32},{32,64},{64,96},{96,128},{128,160},{160,192},{192,224},{1,3... | collective-permute-start | bytes 2359304 | tf_op jit(solution)/shard_map/ppermute | solution.py:279
  105.2 13.1 %collective-permute-start.10 = (f32[4,128,384]{2,1,0:T(8,128)S(1)}, f32[4,128,384]{2,1,0:T(8,128)S(1)}, u32[]{:S(2)}, u32[]{:S(2)}) collective-permute-start(f32[4,128,384]{2,1,0:T(8,128)S(1)} %get-tuple-element.45), channel_id=1, source_target_pairs={{32,0},{64,32},{96,64},{128,96},{160,128},{192,160},{224,192},{33,... | collective-permute-start | bytes 2359304 | tf_op jit(solution)/shard_map/ppermute | solution.py:279
  108.9 24.4 %collective-permute-start.11 = (f32[4,384,128]{2,1,0:T(8,128)S(1)}, f32[4,384,128]{2,1,0:T(8,128)S(1)}, u32[]{:S(2)}, u32[]{:S(2)}) collective-permute-start(f32[4,384,128]{2,1,0:T(8,128)S(1)} %get-tuple-element.47), channel_id=1, source_target_pairs={{0,1},{1,2},{2,3},{3,4},{4,5},{5,6},{6,7},{7,8},{8,9},{9,10},{10,1... | collective-permute-start | bytes 2359304 | tf_op jit(solution)/shard_map/ppermute | solution.py:279
  110.8 25.4 %collective-permute-start.12 = (f32[4,384,128]{2,1,0:T(8,128)S(1)}, f32[4,384,128]{2,1,0:T(8,128)S(1)}, u32[]{:S(2)}, u32[]{:S(2)}) collective-permute-start(f32[4,384,128]{2,1,0:T(8,128)S(1)} %get-tuple-element.48), channel_id=1, source_target_pairs={{1,0},{2,1},{3,2},{4,3},{5,4},{6,5},{7,6},{8,7},{9,8},{10,9},{11,1... | collective-permute-start | bytes 2359304 | tf_op jit(solution)/shard_map/ppermute | solution.py:279
  119.3 23.0 %collective-permute-start.13 = (f32[4,256,128]{2,1,0:T(8,128)S(1)}, f32[4,256,128]{2,1,0:T(8,128)S(1)}, u32[]{:S(2)}, u32[]{:S(2)}) collective-permute-start(f32[4,256,128]{2,1,0:T(8,128)S(1)} %get-tuple-element.49), channel_id=1, source_target_pairs={{0,1},{1,2},{2,3},{3,4},{4,5},{5,6},{6,7},{7,8},{8,9},{9,10},{10,1... | collective-permute-start | bytes 1572872 | tf_op jit(solution)/shard_map/ppermute | solution.py:279
  121.2 24.0 %collective-permute-start.14 = (f32[4,256,128]{2,1,0:T(8,128)S(1)}, f32[4,256,128]{2,1,0:T(8,128)S(1)}, u32[]{:S(2)}, u32[]{:S(2)}) collective-permute-start(f32[4,256,128]{2,1,0:T(8,128)S(1)} %get-tuple-element.50), channel_id=1, source_target_pairs={{1,0},{2,1},{3,2},{4,3},{5,4},{6,5},{7,6},{8,7},{9,8},{10,9},{11,1... | collective-permute-start | bytes 1572872 | tf_op jit(solution)/shard_map/ppermute | solution.py:279
  153.4 13.3 %collective-permute-start.15 = (f32[4,128,384]{2,1,0:T(8,128)S(1)}, f32[4,128,384]{2,1,0:T(8,128)S(1)}, u32[]{:S(2)}, u32[]{:S(2)}) collective-permute-start(f32[4,128,384]{2,1,0:T(8,128)S(1)} %get-tuple-element.53), channel_id=1, source_target_pairs={{0,32},{32,64},{64,96},{96,128},{128,160},{160,192},{192,224},{1,3... | collective-permute-start | bytes 2359304 | tf_op jit(solution)/shard_map/ppermute | solution.py:279
  155.3 31.5 %collective-permute-start.16 = (f32[4,384,128]{2,1,0:T(8,128)S(1)}, f32[4,384,128]{2,1,0:T(8,128)S(1)}, u32[]{:S(2)}, u32[]{:S(2)}) collective-permute-start(f32[4,384,128]{2,1,0:T(8,128)S(1)} %get-tuple-element.55), channel_id=1, source_target_pairs={{0,1},{1,2},{2,3},{3,4},{4,5},{5,6},{6,7},{7,8},{8,9},{9,10},{10,1... | collective-permute-start | bytes 2359304 | tf_op jit(solution)/shard_map/ppermute | solution.py:279
  167.0 24.7 %collective-permute-start.17 = (f32[4,128,128]{2,1,0:T(8,128)S(1)}, f32[4,128,128]{2,1,0:T(8,128)S(1)}, u32[]{:S(2)}, u32[]{:S(2)}) collective-permute-start(f32[4,128,128]{2,1,0:T(8,128)S(1)} %get-tuple-element.56), channel_id=1, source_target_pairs={{0,1},{1,2},{2,3},{3,4},{4,5},{5,6},{6,7},{7,8},{8,9},{9,10},{10,1... | collective-permute-start | bytes 786440 | tf_op jit(solution)/shard_map/ppermute | solution.py:279
where the time goes:
time: 194 us; the launch traced here: 193 us
  waiting for transfers between devices  78.8 us (41%)
  starting transfers between devices  74.9 us (39%)
  Pallas kernels  35.1 us (18%)
  local copies, waits for them, and re-layouts  3.48 us (2%)
    ppermute x18, waiting for transfers between devices, from_behind(): return lax.ppermute(array, axis, pairs)  78.8 us
    ppermute x18, starting transfers between devices, from_behind(): return lax.ppermute(array, axis, pairs)  74.9 us
    pallas_call x9, Pallas kernels, call(): pl.pallas_call(kernel, in_specs=[SM] * len(scalars) + [VM] * len(arrays),...  35.1 us
  transfers between devices with their start and end apart: 18, of which 14 were waited for; matrix products, arithmetic and copies ran while one was open for 1% of the time, Pallas kernels for 3%

commit v1 on v0

--- a/solution.py
+++ b/solution.py
@@ -101,21 +101,49 @@
     return base, r - base
 
 
+def lanes_left(x, c):
+    keep = lax.broadcasted_iota(jnp.int32, (x.shape[0], HALF), 1) < HALF - c
+    turn = lax.rem(HALF - c, HALF)
+    a, b, d = [pltpu.roll(x[:, i * HALF : (i + 1) * HALF], turn, 1) for i in range(3)]
+    return cc([jnp.where(keep, a, b), jnp.where(keep, b, d)], 1)
+
+
+def lanes_right(x, c):
+    keep = lax.broadcasted_iota(jnp.int32, (x.shape[0], HALF), 1) >= c
+    turn = lax.rem(c, HALF)
+    a, b = [pltpu.roll(x[:, i * HALF : (i + 1) * HALF], turn, 1) for i in range(2)]
+    none = jnp.zeros_like(a)
+    return cc([jnp.where(keep, a, none), jnp.where(keep, b, a), jnp.where(keep, none, b)], 1)
+
+
+def rows_up(x, shift):
+    y = x.reshape(WIN // 8 + 1, 8, x.shape[1])
+    y = pltpu.roll(y, lax.rem(8 - shift, 8), 1)
+    keep = lax.broadcasted_iota(jnp.int32, (WIN // 8, 8, x.shape[1]), 1) < 8 - shift
+    return jnp.where(keep, y[:-1], y[1:]).reshape(WIN, x.shape[1])
+
+
+def rows_down(x, shift):
+    y = x.reshape(WIN // 8, 8, x.shape[1])
+    y = pltpu.roll(y, lax.rem(shift, 8), 1)
+    none = jnp.zeros((1, 8, x.shape[1]), f32)
+    keep = lax.broadcasted_iota(jnp.int32, (WIN // 8 + 1, 8, x.shape[1]), 1) >= shift
+    return jnp.where(keep, cc([y, none], 0), cc([none, y], 0)).reshape(WIN + 8, x.shape[1])
+
+
 def load_window(ref, first, r, c):
     base, shift = place(r)
     out = []
     for p in (first, first + 1):
-        t = ref[p, pl.ds(base, WIN + 8), :]
-        t = pltpu.roll(t, lax.rem(EXT_C - c, EXT_C), 1)[:, :WIN]
-        out.append(pltpu.roll(t, lax.rem(WIN + 8 - shift, WIN + 8), 0)[:WIN])
+        t = lanes_left(ref[p, pl.ds(base, WIN + 8), :], c)
+        out.append(rows_up(t, shift))
     return out
 
 
 def add_window(ref, first, r, c, g):
     base, shift = place(r)
     for p in (first, first + 1):
-        t = pltpu.roll(cc([g[p - first], jnp.zeros((8, WIN), f32)], 0), shift, 0)
-        t = pltpu.roll(cc([t, jnp.zeros((WIN + 8, EXT_C - WIN), f32)], 1), c, 1)
+        t = lanes_right(rows_down(g[p - first], shift), c)
         ref[p, pl.ds(base, WIN + 8), :] = ref[p, pl.ds(base, WIN + 8), :] + t
 
 
@@ -162,15 +190,14 @@
         state[p, ROWS:, :] = bottom[p]
 
 
-def batch_kernel(batch, first):
+def batch_kernel(batch, first, final):
     def run(count, orow, ocol, wbatch, tab, probe, prop, amp, *rest):
         if first:
-            (old,) = rest[:1]
-            state, grad, side_l, side_r, top, bottom = rest[1:]
-            state = old
+            state, grad, side_l, side_r, *edges = rest[1:]
         else:
-            old, mid_l, mid_r, end_l, end_r = rest[:5]
-            state, grad, side_l, side_r, top, bottom = rest[5:]
+            old, mid_l, mid_r, end_l, end_r, core_a, core_b = rest[:7]
+            outs = rest[7:]
+            state, grad, side_l, side_r, *edges = (*outs[:2], None, *outs[2:]) if final else outs
             scale = jnp.where(inside("col"), 0.5, 0.0).astype(f32)
             drop = jnp.where(inside("row"), 1.0, 0.0).astype(f32)
             for p in range(4):
@@ -181,6 +208,9 @@
                     state[p, :HALF, cols] = old[p, :HALF, cols] - fac * end[p, :HALF]
                     state[p, HALF:ROWS, cols] = old[p, HALF:ROWS, cols] - fac * mid[p]
                     state[p, ROWS:, cols] = old[p, ROWS:, cols] - (fac * drop) * end[p, HALF:]
+                cols = pl.ds(HALF, HALF)
+                state[p, :HALF, cols] = old[p, :HALF, cols] - 0.5 * core_a[p]
+                state[p, ROWS:, cols] = old[p, ROWS:, cols] - (0.5 * drop) * core_b[p]
         grad[...] = jnp.zeros_like(grad)
 
         def step(s, _):
@@ -204,10 +234,18 @@
             return 0
 
         lax.fori_loop(0, SLOTS, step, 0)
-        side_l[...] = grad[:, HALF:ROWS, :HALF]
         side_r[...] = grad[:, HALF:ROWS, COLS:]
-        top[...] = grad[:, :HALF, :]
-        bottom[...] = grad[:, ROWS:, :]
+        if final:
+            corner, low = edges
+            corner[...] = grad[:, ROWS:, COLS:]
+            low[...] = grad[:, ROWS:, :COLS]
+        else:
+            side_l[...] = grad[:, HALF:ROWS, :HALF]
+            top, bottom, top_core, bottom_core = edges
+            for out, core, rows in ((top, top_core, pl.ds(0, HALF)), (bottom, bottom_core, pl.ds(ROWS, HALF))):
+                out[:, :, :HALF] = grad[:, rows, :HALF]
+                out[:, :, HALF:] = grad[:, rows, COLS:]
+                core[...] = grad[:, rows, HALF:COLS]
 
     return run
 
@@ -217,47 +255,41 @@
     in_c = jnp.where(inside("col"), 1.0, 0.0).astype(f32)
     h = HALF
     for p in range(4):
-        for at in range(0, EXT_R, h):
-            rows = pl.ds(at, h)
-            g = grad[p, rows, :]
-            if at == 0:
-                g = g + above[p]
-                end_l[p, :h] = g[:, :h]
-                end_r[p, :h] = g[:, COLS:]
-            if at == ROWS:
-                g = g + below[p]
-                end_l[p, h:] = g[:, :h]
-                end_r[p, h:] = g[:, COLS:]
+        for at, near, ends in ((0, above, pl.ds(0, h)), (h, None, None), (ROWS, below, pl.ds(h, h))):
+            rows = pl.ds(at, ROWS - h if near is None else h)
+            left, mid, right = grad[p, rows, :h], grad[p, rows, h:COLS], grad[p, rows, COLS:]
+            if near is not None:
+                left = left + near[p, :, :h]
+                right = right + near[p, :, h:]
+                end_l[p, ends] = left
+                end_r[p, ends] = right
             scale = in_r if at == ROWS else jnp.float32(0.5)
-            out[p, rows, :COLS] = state[p, rows, :COLS] - scale * g[:, :COLS]
-            out[p, rows, COLS:] = state[p, rows, COLS:] - (scale * in_c) * g[:, COLS:]
-
-
-def final_settle_kernel(state, grad, above, out, end_r):
-    h = HALF
+            out[p, rows, :h] = state[p, rows, :h] - scale * left
+            out[p, rows, h:COLS] = state[p, rows, h:COLS] - scale * mid
+            out[p, rows, COLS:] = state[p, rows, COLS:] - (scale * in_c) * right
+
+
+def final_settle_kernel(state, grad, corner, out, end_r):
     for p in range(4):
-        for at in range(0, ROWS, h):
-            rows = pl.ds(at, h)
-            g = grad[p, rows, :]
-            if at == 0:
-                g = g + above[p]
-                end_r[p] = g[:, COLS:]
-            out[p, rows] = state[p, rows, :COLS] - 0.5 * g[:, :COLS]
-
-
-def last_kernel(state, mid, end, out):
+        end_r[p] = grad[p, :HALF, COLS:] + corner[p]
+        out[p] = state[p, :ROWS, :COLS] - 0.5 * grad[p, :ROWS, :COLS]
+
+
+def last_kernel(state, mid, end, low, out):
     h = HALF
     for p in range(4):
         q = (p // 2, p % 2)
-        out[(*q, slice(0, h), slice(0, h))] = state[p, :h, :h] - 0.5 * end[p]
+        out[(*q, slice(0, h), slice(0, h))] = state[p, :h, :h] - 0.5 * (end[p] + low[p, :, :h])
         out[(*q, slice(h, ROWS), slice(0, h))] = state[p, h:, :h] - 0.5 * mid[p]
-        out[(*q, slice(0, ROWS), slice(h, COLS))] = state[p, :, h:]
+        out[(*q, slice(0, h), slice(h, COLS))] = state[p, :h, h:] - 0.5 * low[p, :, h:]
+        out[(*q, slice(h, ROWS), slice(h, COLS))] = state[p, h:, h:]
 
 
 VM = pl.BlockSpec(memory_space=pltpu.VMEM)
 SM = pl.BlockSpec(memory_space=pltpu.SMEM)
 EXT = (4, EXT_R, EXT_C)
-FLAT = (4, HALF, EXT_C)
+EDGE = (4, HALF, 2 * HALF)
+CORE = (4, HALF, HALF)
 MIDS = (4, ROWS - HALF, HALF)
 ENDS = (4, 2 * HALF, HALF)
 
@@ -287,40 +319,48 @@
     planes = transmission.reshape(4, ROWS, COLS)
     right_top = from_behind(planes[:, :h, :h], "col", -1)
     right_rest = from_behind(planes[:, h:, :h], "col", -1)
-    amp, prop = call(
-        prep_kernel, (), (amplitude, phase, order), [(SLOTS, WIN, WIN), (2, WIN, WIN)]
-    )
+    amp, prop = call(prep_kernel, (), (amplitude, phase, order), [(SLOTS, WIN, WIN), (2, WIN, WIN)])
     low = cc([planes[:, :h, :], right_top], 2)
     bottom = from_behind(low, "row", -1)
-    (state,) = call(
-        assemble_kernel, (), (transmission, right_top, right_rest, bottom), [EXT]
-    )
+    (state,) = call(assemble_kernel, (), (transmission, right_top, right_rest, bottom), [EXT])
     parts = ()
     for b in range(BATCHES):
-        state, grad, side_l, side_r, top, low = call(
-            batch_kernel(b, b == 0),
+        final = b == BATCHES - 1
+        outs = [MIDS, CORE, EDGE] if final else [MIDS, MIDS, EDGE, EDGE, CORE, CORE]
+        state, grad, *sent = call(
+            batch_kernel(b, b == 0, final),
             scalars,
             (tab, probe, prop, amp, state, *parts),
-            [EXT, EXT, MIDS, MIDS, FLAT, FLAT],
+            [EXT, EXT, *outs],
             {8: 0},
         )
+        if final:
+            side_r, corner, low = sent
+            mid_l = from_behind(side_r, "col", 1)
+            corner = from_behind(corner, "row", 1)
+            main, end_r = call(
+                final_settle_kernel, (), (state, grad, corner), [(4, ROWS, COLS), CORE]
+            )
+            end_l = from_behind(end_r, "col", 1)
+            low = from_behind(low, "row", 1)
+            break
+        side_l, side_r, top, bottom, top_core, bottom_core = sent
         mid_l = from_behind(side_r, "col", 1)
-        above = from_behind(low, "row", 1)
-        if b == BATCHES - 1:
-            break
         mid_r = from_behind(side_l, "col", -1)
+        above = from_behind(bottom, "row", 1)
         below = from_behind(top, "row", -1)
         state, end_l, end_r = call(
             settle_kernel, (), (state, grad, above, below), [EXT, ENDS, ENDS], {0: 0}
         )
         parts = (
-            mid_l, mid_r, from_behind(end_r, "col", 1), from_behind(end_l, "col", -1)
+            mid_l,
+            mid_r,
+            from_behind(end_r, "col", 1),
+            from_behind(end_l, "col", -1),
+            from_behind(bottom_core, "row", 1),
+            from_behind(top_core, "row", -1),
         )
-    main, end_r = call(
-        final_settle_kernel, (), (state, grad, above), [(4, ROWS, COLS), (4, h, h)]
-    )
-    end_l = from_behind(end_r, "col", 1)
-    return call(last_kernel, (), (main, mid_l, end_l), [(2, 2, ROWS, COLS)])[0]
+    return call(last_kernel, (), (main, mid_l, end_l, low), [(2, 2, ROWS, COLS)])[0]
 
 
 def solution(mesh):

time: 194 us -> 183 us (0.943)
  the two profiles are of different devices: /device:TPU:22 before, /device:TPU:147 now
where the time goes in v1:
time: 183 us
  starting transfers between devices  96.4 us (53%)
  waiting for transfers between devices  49.6 us (27%)
  Pallas kernels  32 us (17%)
  local copies, waits for them, and re-layouts  3.48 us (2%)
    ppermute x23, starting transfers between devices, from_behind(): return lax.ppermute(array, axis, pairs)  96.4 us
    ppermute x23, waiting for transfers between devices, from_behind(): return lax.ppermute(array, axis, pairs)  49.6 us
    pallas_call x9, Pallas kernels, call(): pl.pallas_call(kernel, in_specs=[SM] * len(scalars) + [VM] * len(arrays),...  32 us
  transfers between devices with their start and end apart: 23, of which 10 were waited for; matrix products, arithmetic and copies ran while one was open for 1% of the time, Pallas kernels for 3%

profile of v1, /device:TPU:147, one launch (start us, length us, event | category | flops | bytes accessed | tf_op | source)
XLA Modules:
  0.0 182.6 jit_solution(7541320657612852880)
XLA Ops:
  1.2 2.1 %collective-permute-start = (f32[4,128,128]{2,1,0:T(8,128)S(1)}, f32[4,128,128]{2,1,0:T(8,128)S(1)}, u32[]{:S(2)}, u32[]{:S(2)}) collective-permute-start(f32[4,128,128]{2,1,0:T(8,128)S(1)} %slice.12), channel_id=1, source_target_pairs={{1,0},{2,1},{3,2},{4,3},{5,4},{6,5},{7,6},{8,7},{9,8},{10,9},{11,1... | collective-permute-start | bytes 786440 | tf_op jit(solution)/shard_map/ppermute | solution.py:311
  4.4 1.9 %collective-permute-start.1 = (f32[4,384,128]{2,1,0:T(8,128)S(1)}, f32[4,384,128]{2,1,0:T(8,128)S(1)}, u32[]{:S(2)}, u32[]{:S(2)}) collective-permute-start(f32[4,384,128]{2,1,0:T(8,128)S(1)} %slice.13), channel_id=1, source_target_pairs={{1,0},{2,1},{3,2},{4,3},{5,4},{6,5},{7,6},{8,7},{9,8},{10,9},{11,1... | collective-permute-start | bytes 2359304 | tf_op jit(solution)/shard_map/ppermute | solution.py:311
  7.4 2.9 %collective-permute-done.right_top = f32[4,128,128]{2,1,0:T(8,128)S(1)} collective-permute-done((f32[4,128,128]{2,1,0:T(8,128)S(1)}, f32[4,128,128]{2,1,0:T(8,128)S(1)}, u32[]{:S(2)}, u32[]{:S(2)}) %collective-permute-start) | collective-permute-done | bytes 262176 | tf_op jit(solution)/shard_map/ppermute | solution.py:311
  10.4 4.6 %collective-permute-start.2 = (f32[4,128,384]{2,1,0:T(8,128)S(1)}, f32[4,128,384]{2,1,0:T(8,128)S(1)}, u32[]{:S(2)}, u32[]{:S(2)}) collective-permute-start(f32[4,128,384]{2,1,0:T(8,128)S(1)} %pad_maximum_fusion), channel_id=1, source_target_pairs={{32,0},{64,32},{96,64},{128,96},{160,128},{192,160},{224,192},{33,... | collective-permute-start | bytes 2359304 | tf_op jit(solution)/shard_map/ppermute | solution.py:311
  15.7 4.2 %shard_map.100 = (f32[4,256,256]{2,1,0:T(8,128)S(1)}, f32[2,256,256]{2,1,0:T(8,128)S(1)}) custom-call(f32[1,1,4,256,256]{4,3,2,1,0:T(8,128)S(1)} %copy-done.3, f32[256,256]{1,0:T(8,128)S(1)} %copy-done.4, bf16[2,256,256]{2,1,0:T(8,128)(2,1)S(1)} %copy-done.5), custom_call_target="tpu_custom_call" | custom-call | tf_op jit(solution)/shard_map/pallas_call | solution.py:298
  19.9 7.3 %collective-permute-done.1.right_rest = f32[4,384,128]{2,1,0:T(8,128)S(1)} collective-permute-done((f32[4,384,128]{2,1,0:T(8,128)S(1)}, f32[4,384,128]{2,1,0:T(8,128)S(1)}, u32[]{:S(2)}, u32[]{:S(2)}) %collective-permute-start.1) | collective-permute-done | bytes 786464 | tf_op jit(solution)/shard_map/ppermute | solution.py:311
  28.6 23.9 %collective-permute-start.3 = (f32[4,128,256]{2,1,0:T(8,128)S(1)}, f32[4,128,256]{2,1,0:T(8,128)S(1)}, u32[]{:S(2)}, u32[]{:S(2)}) collective-permute-start(f32[4,128,256]{2,1,0:T(8,128)S(1)} %get-tuple-element.40), channel_id=1, source_target_pairs={{0,32},{32,64},{64,96},{96,128},{128,160},{160,192},{192,224},{1,3... | collective-permute-start | bytes 1572872 | tf_op jit(solution)/shard_map/ppermute | solution.py:311
  52.5 1.9 %collective-permute-start.4 = (f32[4,128,256]{2,1,0:T(8,128)S(1)}, f32[4,128,256]{2,1,0:T(8,128)S(1)}, u32[]{:S(2)}, u32[]{:S(2)}) collective-permute-start(f32[4,128,256]{2,1,0:T(8,128)S(1)} %get-tuple-element.41), channel_id=1, source_target_pairs={{32,0},{64,32},{96,64},{128,96},{160,128},{192,160},{224,192},{33,... | collective-permute-start | bytes 1572872 | tf_op jit(solution)/shard_map/ppermute | solution.py:311
  54.5 1.9 %collective-permute-start.5 = (f32[4,384,128]{2,1,0:T(8,128)S(1)}, f32[4,384,128]{2,1,0:T(8,128)S(1)}, u32[]{:S(2)}, u32[]{:S(2)}) collective-permute-start(f32[4,384,128]{2,1,0:T(8,128)S(1)} %get-tuple-element.43), channel_id=1, source_target_pairs={{0,1},{1,2},{2,3},{3,4},{4,5},{5,6},{6,7},{7,8},{8,9},{9,10},{10,1... | collective-permute-start | bytes 2359304 | tf_op jit(solution)/shard_map/ppermute | solution.py:311
  56.4 4.6 %collective-permute-start.6 = (f32[4,384,128]{2,1,0:T(8,128)S(1)}, f32[4,384,128]{2,1,0:T(8,128)S(1)}, u32[]{:S(2)}, u32[]{:S(2)}) collective-permute-start(f32[4,384,128]{2,1,0:T(8,128)S(1)} %get-tuple-element.44), channel_id=1, source_target_pairs={{1,0},{2,1},{3,2},{4,3},{5,4},{6,5},{7,6},{8,7},{9,8},{10,9},{11,1... | collective-permute-start | bytes 2359304 | tf_op jit(solution)/shard_map/ppermute | solution.py:311
  61.0 4.2 %collective-permute-start.9 = (f32[4,128,128]{2,1,0:T(8,128)S(1)}, f32[4,128,128]{2,1,0:T(8,128)S(1)}, u32[]{:S(2)}, u32[]{:S(2)}) collective-permute-start(f32[4,128,128]{2,1,0:T(8,128)S(1)} %get-tuple-element.47), channel_id=1, source_target_pairs={{0,32},{32,64},{64,96},{96,128},{128,160},{160,192},{192,224},{1,3... | collective-permute-start | bytes 786440 | tf_op jit(solution)/shard_map/ppermute | solution.py:311
  66.1 1.9 %collective-permute-start.7 = (f32[4,256,128]{2,1,0:T(8,128)S(1)}, f32[4,256,128]{2,1,0:T(8,128)S(1)}, u32[]{:S(2)}, u32[]{:S(2)}) collective-permute-start(f32[4,256,128]{2,1,0:T(8,128)S(1)} %get-tuple-element.45), channel_id=1, source_target_pairs={{0,1},{1,2},{2,3},{3,4},{4,5},{5,6},{6,7},{7,8},{8,9},{9,10},{10,1... | collective-permute-start | bytes 1572872 | tf_op jit(solution)/shard_map/ppermute | solution.py:311
  68.0 4.6 %collective-permute-start.8 = (f32[4,256,128]{2,1,0:T(8,128)S(1)}, f32[4,256,128]{2,1,0:T(8,128)S(1)}, u32[]{:S(2)}, u32[]{:S(2)}) collective-permute-start(f32[4,256,128]{2,1,0:T(8,128)S(1)} %get-tuple-element.46), channel_id=1, source_target_pairs={{1,0},{2,1},{3,2},{4,3},{5,4},{6,5},{7,6},{8,7},{9,8},{10,9},{11,1... | collective-permute-start | bytes 1572872 | tf_op jit(solution)/shard_map/ppermute | solution.py:311
  72.6 2.1 %collective-permute-start.10 = (f32[4,128,128]{2,1,0:T(8,128)S(1)}, f32[4,128,128]{2,1,0:T(8,128)S(1)}, u32[]{:S(2)}, u32[]{:S(2)}) collective-permute-start(f32[4,128,128]{2,1,0:T(8,128)S(1)} %get-tuple-element.48), channel_id=1, source_target_pairs={{32,0},{64,32},{96,64},{128,96},{160,128},{192,160},{224,192},{33,... | collective-permute-start | bytes 786440 | tf_op jit(solution)/shard_map/ppermute | solution.py:311
  74.7 5.9 %collective-permute-done.10.rest_6_ = f32[4,128,128]{2,1,0:T(8,128)S(1)} collective-permute-done((f32[4,128,128]{2,1,0:T(8,128)S(1)}, f32[4,128,128]{2,1,0:T(8,128)S(1)}, u32[]{:S(2)}, u32[]{:S(2)}) %collective-permute-start.10) | collective-permute-done | bytes 262176 | tf_op jit(solution)/shard_map/ppermute | solution.py:311
  83.3 6.6 %shard_map.104 = (f32[4,640,384]{2,1,0:T(8,128)S(1)}, f32[4,640,384]{2,1,0:T(8,128)S(1)}, f32[4,384,128]{2,1,0:T(8,128)S(1)}, f32[4,384,128]{2,1,0:T(8,128)S(1)}...) custom-call(s32[1,1]{1,0:T(1,128)S(6)} %copy.21.count, ...), custom_call_target="tpu_custom_call", output_to_operand_aliasing={{0}: (8, {})} | custom-call | tf_op jit(solution)/shard_map/pallas_call | solution.py:298
  89.9 3.7 %collective-permute-start.11 = (f32[4,128,256]{2,1,0:T(8,128)S(1)}, f32[4,128,256]{2,1,0:T(8,128)S(1)}, u32[]{:S(2)}, u32[]{:S(2)}) collective-permute-start(f32[4,128,256]{2,1,0:T(8,128)S(1)} %get-tuple-element.51), channel_id=1, source_target_pairs={{0,32},{32,64},{64,96},{96,128},{128,160},{160,192},{192,224},{1,3... | collective-permute-start | bytes 1572872 | tf_op jit(solution)/shard_map/ppermute | solution.py:311
  93.6 1.9 %collective-permute-start.12 = (f32[4,128,256]{2,1,0:T(8,128)S(1)}, f32[4,128,256]{2,1,0:T(8,128)S(1)}, u32[]{:S(2)}, u32[]{:S(2)}) collective-permute-start(f32[4,128,256]{2,1,0:T(8,128)S(1)} %get-tuple-element.52), channel_id=1, source_target_pairs={{32,0},{64,32},{96,64},{128,96},{160,128},{192,160},{224,192},{33,... | collective-permute-start | bytes 1572872 | tf_op jit(solution)/shard_map/ppermute | solution.py:311
  95.6 5.6 %collective-permute-start.13 = (f32[4,384,128]{2,1,0:T(8,128)S(1)}, f32[4,384,128]{2,1,0:T(8,128)S(1)}, u32[]{:S(2)}, u32[]{:S(2)}) collective-permute-start(f32[4,384,128]{2,1,0:T(8,128)S(1)} %get-tuple-element.54), channel_id=1, source_target_pairs={{0,1},{1,2},{2,3},{3,4},{4,5},{5,6},{6,7},{7,8},{8,9},{9,10},{10,1... | collective-permute-start | bytes 2359304 | tf_op jit(solution)/shard_map/ppermute | solution.py:311
  101.2 11.5 %collective-permute-start.14 = (f32[4,384,128]{2,1,0:T(8,128)S(1)}, f32[4,384,128]{2,1,0:T(8,128)S(1)}, u32[]{:S(2)}, u32[]{:S(2)}) collective-permute-start(f32[4,384,128]{2,1,0:T(8,128)S(1)} %get-tuple-element.55), channel_id=1, source_target_pairs={{1,0},{2,1},{3,2},{4,3},{5,4},{6,5},{7,6},{8,7},{9,8},{10,9},{11,1... | collective-permute-start | bytes 2359304 | tf_op jit(solution)/shard_map/ppermute | solution.py:311
  112.7 3.9 %collective-permute-start.17 = (f32[4,128,128]{2,1,0:T(8,128)S(1)}, f32[4,128,128]{2,1,0:T(8,128)S(1)}, u32[]{:S(2)}, u32[]{:S(2)}) collective-permute-start(f32[4,128,128]{2,1,0:T(8,128)S(1)} %get-tuple-element.58), channel_id=1, source_target_pairs={{0,32},{32,64},{64,96},{96,128},{128,160},{160,192},{192,224},{1,3... | collective-permute-start | bytes 786440 | tf_op jit(solution)/shard_map/ppermute | solution.py:311
  117.5 1.9 %collective-permute-start.15 = (f32[4,256,128]{2,1,0:T(8,128)S(1)}, f32[4,256,128]{2,1,0:T(8,128)S(1)}, u32[]{:S(2)}, u32[]{:S(2)}) collective-permute-start(f32[4,256,128]{2,1,0:T(8,128)S(1)} %get-tuple-element.56), channel_id=1, source_target_pairs={{0,1},{1,2},{2,3},{3,4},{4,5},{5,6},{6,7},{7,8},{8,9},{9,10},{10,1... | collective-permute-start | bytes 1572872 | tf_op jit(solution)/shard_map/ppermute | solution.py:311
  119.4 4.6 %collective-permute-start.16 = (f32[4,256,128]{2,1,0:T(8,128)S(1)}, f32[4,256,128]{2,1,0:T(8,128)S(1)}, u32[]{:S(2)}, u32[]{:S(2)}) collective-permute-start(f32[4,256,128]{2,1,0:T(8,128)S(1)} %get-tuple-element.57), channel_id=1, source_target_pairs={{1,0},{2,1},{3,2},{4,3},{5,4},{6,5},{7,6},{8,7},{9,8},{10,9},{11,1... | collective-permute-start | bytes 1572872 | tf_op jit(solution)/shard_map/ppermute | solution.py:311
  124.0 1.9 %collective-permute-start.18 = (f32[4,128,128]{2,1,0:T(8,128)S(1)}, f32[4,128,128]{2,1,0:T(8,128)S(1)}, u32[]{:S(2)}, u32[]{:S(2)}) collective-permute-start(f32[4,128,128]{2,1,0:T(8,128)S(1)} %get-tuple-element.59), channel_id=1, source_target_pairs={{32,0},{64,32},{96,64},{128,96},{160,128},{192,160},{224,192},{33,... | collective-permute-start | bytes 786440 | tf_op jit(solution)/shard_map/ppermute | solution.py:311
  125.9 6.1 %collective-permute-done.18.rest_6_ = f32[4,128,128]{2,1,0:T(8,128)S(1)} collective-permute-done((f32[4,128,128]{2,1,0:T(8,128)S(1)}, f32[4,128,128]{2,1,0:T(8,128)S(1)}, u32[]{:S(2)}, u32[]{:S(2)}) %collective-permute-start.18) | collective-permute-done | bytes 262176 | tf_op jit(solution)/shard_map/ppermute | solution.py:311
  132.0 7.3 %collective-permute-done.15.rest_3_ = f32[4,256,128]{2,1,0:T(8,128)S(1)} collective-permute-done((f32[4,256,128]{2,1,0:T(8,128)S(1)}, f32[4,256,128]{2,1,0:T(8,128)S(1)}, u32[]{:S(2)}, u32[]{:S(2)}) %collective-permute-start.15) | collective-permute-done | bytes 524320 | tf_op jit(solution)/shard_map/ppermute | solution.py:311
  141.0 16.4 %shard_map.106 = (f32[4,640,384]{2,1,0:T(8,128)S(1)}, f32[4,640,384]{2,1,0:T(8,128)S(1)}, f32[4,384,128]{2,1,0:T(8,128)S(1)}, f32[4,128,128]{2,1,0:T(8,128)S(1)}, f32[4,128,256]{2,1,0:T(8,128)S(1)}) custom-call(s32[1,1]{1,0:T(1,128)S(6)} %copy.21.count, s32[1,1,4]{2,1,0:T(1,128)S(1)} %copy-done.6, ...), custom_call_target="tpu_custom_call", output_to_operand_aliasing={{0}: (8, {})} | custom-call | tf_op jit(solution)/shard_map/pallas_call | solution.py:298
  157.4 1.9 %collective-permute-start.20 = (f32[4,384,128]{2,1,0:T(8,128)S(1)}, f32[4,384,128]{2,1,0:T(8,128)S(1)}, u32[]{:S(2)}, u32[]{:S(2)}) collective-permute-start(f32[4,384,128]{2,1,0:T(8,128)S(1)} %get-tuple-element.64), channel_id=1, source_target_pairs={{0,1},{1,2},{2,3},{3,4},{4,5},{5,6},{6,7},{7,8},{8,9},{9,10},{10,1... | collective-permute-start | bytes 2359304 | tf_op jit(solution)/shard_map/ppermute | solution.py:311
  159.3 1.9 %collective-permute-start.19 = (f32[4,128,128]{2,1,0:T(8,128)S(1)}, f32[4,128,128]{2,1,0:T(8,128)S(1)}, u32[]{:S(2)}, u32[]{:S(2)}) collective-permute-start(f32[4,128,128]{2,1,0:T(8,128)S(1)} %get-tuple-element.62), channel_id=1, source_target_pairs={{0,32},{32,64},{64,96},{96,128},{128,160},{160,192},{192,224},{1,3... | collective-permute-start | bytes 786440 | tf_op jit(solution)/shard_map/ppermute | solution.py:311
  161.3 1.9 %collective-permute-start.22 = (f32[4,128,256]{2,1,0:T(8,128)S(1)}, f32[4,128,256]{2,1,0:T(8,128)S(1)}, u32[]{:S(2)}, u32[]{:S(2)}) collective-permute-start(f32[4,128,256]{2,1,0:T(8,128)S(1)} %get-tuple-element.66), channel_id=1, source_target_pairs={{0,32},{32,64},{64,96},{96,128},{128,160},{160,192},{192,224},{1,3... | collective-permute-start | bytes 1572872 | tf_op jit(solution)/shard_map/ppermute | solution.py:311
  164.8 1.9 %collective-permute-start.21 = (f32[4,128,128]{2,1,0:T(8,128)S(1)}, f32[4,128,128]{2,1,0:T(8,128)S(1)}, u32[]{:S(2)}, u32[]{:S(2)}) collective-permute-start(f32[4,128,128]{2,1,0:T(8,128)S(1)} %get-tuple-element.65), channel_id=1, source_target_pairs={{0,1},{1,2},{2,3},{3,4},{4,5},{5,6},{6,7},{7,8},{8,9},{9,10},{10,1... | collective-permute-start | bytes 786440 | tf_op jit(solution)/shard_map/ppermute | solution.py:311
  166.8 14.3 %collective-permute-done.21.end = f32[4,128,128]{2,1,0:T(8,128)S(1)} collective-permute-done((f32[4,128,128]{2,1,0:T(8,128)S(1)}, f32[4,128,128]{2,1,0:T(8,128)S(1)}, u32[]{:S(2)}, u32[]{:S(2)}) %collective-permute-start.21) | collective-permute-done | bytes 262176 | tf_op jit(solution)/shard_map/ppermute | solution.py:311
  (45 shorter events, 14.2 us)
Async XLA Ops:
  0.0 15.7 %copy-start.5 = (bf16[2,256,256]{2,1,0:T(8,128)(2,1)S(1)}, bf16[2,256,256]{2,1,0:T(8,128)(2,1)}, u32[]{:S(2)}) copy-start(bf16[2,256,256]{2,1,0:T(8,128)(2,1)} %constant.5.clone.order) | copy-start | bytes 786436
  0.0 27.2 %copy-start.1 = (f32[2,2,512,256]{3,2,1,0:T(8,128)S(1)}, f32[2,2,512,256]{3,2,1,0:T(8,128)}, u32[]{:S(2)}) copy-start(f32[2,2,512,256]{3,2,1,0:T(8,128)} %main.1) | copy-start | bytes 6291460
  0.0 15.7 %copy-start.3 = (f32[1,1,4,256,256]{4,3,2,1,0:T(8,128)S(1)}, f32[1,1,4,256,256]{4,3,2,1,0:T(8,128)}, u32[]{:S(2)}) copy-start(f32[1,1,4,256,256]{4,3,2,1,0:T(8,128)} %amp.1) | copy-start | bytes 3145732
  0.0 15.7 %copy-start.4 = (f32[256,256]{1,0:T(8,128)S(1)}, f32[256,256]{1,0:T(8,128)}, u32[]{:S(2)}) copy-start(f32[256,256]{1,0:T(8,128)} %phase.1) | copy-start | bytes 786436
  1.2 9.2 %collective-permute-start = (f32[4,128,128]{2,1,0:T(8,128)S(1)}, f32[4,128,128]{2,1,0:T(8,128)S(1)}, u32[]{:S(2)}, u32[]{:S(2)}) collective-permute-start(f32[4,128,128]{2,1,0:T(8,128)S(1)} %slice.12), channel_id=1, source_target_pairs={{1,0},{2,1},{3,2},{4,3},{5,4},{6,5},{7,6},{8,7},{9,8},{10,9},{11,1... | collective-permute-start | bytes 786440 | tf_op jit(solution)/shard_map/ppermute | solution.py:311
  4.4 22.8 %collective-permute-start.1 = (f32[4,384,128]{2,1,0:T(8,128)S(1)}, f32[4,384,128]{2,1,0:T(8,128)S(1)}, u32[]{:S(2)}, u32[]{:S(2)}) collective-permute-start(f32[4,384,128]{2,1,0:T(8,128)S(1)} %slice.13), channel_id=1, source_target_pairs={{1,0},{2,1},{3,2},{4,3},{5,4},{6,5},{7,6},{8,7},{9,8},{10,9},{11,1... | collective-permute-start | bytes 2359304 | tf_op jit(solution)/shard_map/ppermute | solution.py:311
  10.4 16.8 %collective-permute-start.2 = (f32[4,128,384]{2,1,0:T(8,128)S(1)}, f32[4,128,384]{2,1,0:T(8,128)S(1)}, u32[]{:S(2)}, u32[]{:S(2)}) collective-permute-start(f32[4,128,384]{2,1,0:T(8,128)S(1)} %pad_maximum_fusion), channel_id=1, source_target_pairs={{32,0},{64,32},{96,64},{128,96},{160,128},{192,160},{224,192},{33,... | collective-permute-start | bytes 2359304 | tf_op jit(solution)/shard_map/ppermute | solution.py:311
  19.9 7.6 %copy-start = (bf16[2,2,2,256,256]{4,3,2,1,0:T(8,128)(2,1)S(1)}, bf16[2,2,2,256,256]{4,3,2,1,0:T(8,128)(2,1)}, u32[]{:S(2)}) copy-start(bf16[2,2,2,256,256]{4,3,2,1,0:T(8,128)(2,1)} %constant.4.clone.tab) | copy-start | bytes 3145732
  19.9 7.6 %copy-start.2 = (f32[2,256,256]{2,1,0:T(8,128)S(1)}, f32[2,256,256]{2,1,0:T(8,128)}, u32[]{:S(2)}) copy-start(f32[2,256,256]{2,1,0:T(8,128)} %probe.5) | copy-start | bytes 1572868
  19.9 7.6 %copy-start.6 = (s32[1,1,4]{2,1,0:T(1,128)S(1)}, s32[1,1,4]{2,1,0:T(1,128)}, u32[]{:S(2)}) copy-start(s32[1,1,4]{2,1,0:T(1,128)} %orow.5) | copy-start | bytes 52
  19.9 7.6 %copy-start.7 = (s32[1,1,4]{2,1,0:T(1,128)S(1)}, s32[1,1,4]{2,1,0:T(1,128)}, u32[]{:S(2)}) copy-start(s32[1,1,4]{2,1,0:T(1,128)} %ocol.5) | copy-start | bytes 52
  19.9 7.6 %copy-start.8 = (s32[1,1,4]{2,1,0:T(1,128)S(1)}, s32[1,1,4]{2,1,0:T(1,128)}, u32[]{:S(2)}) copy-start(s32[1,1,4]{2,1,0:T(1,128)} %wbatch.5) | copy-start | bytes 52
  28.6 36.6 %collective-permute-start.3 = (f32[4,128,256]{2,1,0:T(8,128)S(1)}, f32[4,128,256]{2,1,0:T(8,128)S(1)}, u32[]{:S(2)}, u32[]{:S(2)}) collective-permute-start(f32[4,128,256]{2,1,0:T(8,128)S(1)} %get-tuple-element.40), channel_id=1, source_target_pairs={{0,32},{32,64},{64,96},{96,128},{128,160},{160,192},{192,224},{1,3... | collective-permute-start | bytes 1572872 | tf_op jit(solution)/shard_map/ppermute | solution.py:311
  52.5 12.7 %collective-permute-start.4 = (f32[4,128,256]{2,1,0:T(8,128)S(1)}, f32[4,128,256]{2,1,0:T(8,128)S(1)}, u32[]{:S(2)}, u32[]{:S(2)}) collective-permute-start(f32[4,128,256]{2,1,0:T(8,128)S(1)} %get-tuple-element.41), channel_id=1, source_target_pairs={{32,0},{64,32},{96,64},{128,96},{160,128},{192,160},{224,192},{33,... | collective-permute-start | bytes 1572872 | tf_op jit(solution)/shard_map/ppermute | solution.py:311
  54.5 26.1 %collective-permute-start.5 = (f32[4,384,128]{2,1,0:T(8,128)S(1)}, f32[4,384,128]{2,1,0:T(8,128)S(1)}, u32[]{:S(2)}, u32[]{:S(2)}) collective-permute-start(f32[4,384,128]{2,1,0:T(8,128)S(1)} %get-tuple-element.43), channel_id=1, source_target_pairs={{0,1},{1,2},{2,3},{3,4},{4,5},{5,6},{6,7},{7,8},{8,9},{9,10},{10,1... | collective-permute-start | bytes 2359304 | tf_op jit(solution)/shard_map/ppermute | solution.py:311
  56.4 24.2 %collective-permute-start.6 = (f32[4,384,128]{2,1,0:T(8,128)S(1)}, f32[4,384,128]{2,1,0:T(8,128)S(1)}, u32[]{:S(2)}, u32[]{:S(2)}) collective-permute-start(f32[4,384,128]{2,1,0:T(8,128)S(1)} %get-tuple-element.44), channel_id=1, source_target_pairs={{1,0},{2,1},{3,2},{4,3},{5,4},{6,5},{7,6},{8,7},{9,8},{10,9},{11,1... | collective-permute-start | bytes 2359304 | tf_op jit(solution)/shard_map/ppermute | solution.py:311
  61.0 11.6 %collective-permute-start.9 = (f32[4,128,128]{2,1,0:T(8,128)S(1)}, f32[4,128,128]{2,1,0:T(8,128)S(1)}, u32[]{:S(2)}, u32[]{:S(2)}) collective-permute-start(f32[4,128,128]{2,1,0:T(8,128)S(1)} %get-tuple-element.47), channel_id=1, source_target_pairs={{0,32},{32,64},{64,96},{96,128},{128,160},{160,192},{192,224},{1,3... | collective-permute-start | bytes 786440 | tf_op jit(solution)/shard_map/ppermute | solution.py:311
  66.1 15.4 %collective-permute-start.7 = (f32[4,256,128]{2,1,0:T(8,128)S(1)}, f32[4,256,128]{2,1,0:T(8,128)S(1)}, u32[]{:S(2)}, u32[]{:S(2)}) collective-permute-start(f32[4,256,128]{2,1,0:T(8,128)S(1)} %get-tuple-element.45), channel_id=1, source_target_pairs={{0,1},{1,2},{2,3},{3,4},{4,5},{5,6},{6,7},{7,8},{8,9},{9,10},{10,1... | collective-permute-start | bytes 1572872 | tf_op jit(solution)/shard_map/ppermute | solution.py:311
  68.0 15.3 %collective-permute-start.8 = (f32[4,256,128]{2,1,0:T(8,128)S(1)}, f32[4,256,128]{2,1,0:T(8,128)S(1)}, u32[]{:S(2)}, u32[]{:S(2)}) collective-permute-start(f32[4,256,128]{2,1,0:T(8,128)S(1)} %get-tuple-element.46), channel_id=1, source_target_pairs={{1,0},{2,1},{3,2},{4,3},{5,4},{6,5},{7,6},{8,7},{9,8},{10,9},{11,1... | collective-permute-start | bytes 1572872 | tf_op jit(solution)/shard_map/ppermute | solution.py:311
  72.6 8.0 %collective-permute-start.10 = (f32[4,128,128]{2,1,0:T(8,128)S(1)}, f32[4,128,128]{2,1,0:T(8,128)S(1)}, u32[]{:S(2)}, u32[]{:S(2)}) collective-permute-start(f32[4,128,128]{2,1,0:T(8,128)S(1)} %get-tuple-element.48), channel_id=1, source_target_pairs={{32,0},{64,32},{96,64},{128,96},{160,128},{192,160},{224,192},{33,... | collective-permute-start | bytes 786440 | tf_op jit(solution)/shard_map/ppermute | solution.py:311
  89.9 26.7 %collective-permute-start.11 = (f32[4,128,256]{2,1,0:T(8,128)S(1)}, f32[4,128,256]{2,1,0:T(8,128)S(1)}, u32[]{:S(2)}, u32[]{:S(2)}) collective-permute-start(f32[4,128,256]{2,1,0:T(8,128)S(1)} %get-tuple-element.51), channel_id=1, source_target_pairs={{0,32},{32,64},{64,96},{96,128},{128,160},{160,192},{192,224},{1,3... | collective-permute-start | bytes 1572872 | tf_op jit(solution)/shard_map/ppermute | solution.py:311
  93.6 23.0 %collective-permute-start.12 = (f32[4,128,256]{2,1,0:T(8,128)S(1)}, f32[4,128,256]{2,1,0:T(8,128)S(1)}, u32[]{:S(2)}, u32[]{:S(2)}) collective-permute-start(f32[4,128,256]{2,1,0:T(8,128)S(1)} %get-tuple-element.52), channel_id=1, source_target_pairs={{32,0},{64,32},{96,64},{128,96},{160,128},{192,160},{224,192},{33,... | collective-permute-start | bytes 1572872 | tf_op jit(solution)/shard_map/ppermute | solution.py:311
  95.6 36.4 %collective-permute-start.13 = (f32[4,384,128]{2,1,0:T(8,128)S(1)}, f32[4,384,128]{2,1,0:T(8,128)S(1)}, u32[]{:S(2)}, u32[]{:S(2)}) collective-permute-start(f32[4,384,128]{2,1,0:T(8,128)S(1)} %get-tuple-element.54), channel_id=1, source_target_pairs={{0,1},{1,2},{2,3},{3,4},{4,5},{5,6},{6,7},{7,8},{8,9},{9,10},{10,1... | collective-permute-start | bytes 2359304 | tf_op jit(solution)/shard_map/ppermute | solution.py:311
  101.2 30.8 %collective-permute-start.14 = (f32[4,384,128]{2,1,0:T(8,128)S(1)}, f32[4,384,128]{2,1,0:T(8,128)S(1)}, u32[]{:S(2)}, u32[]{:S(2)}) collective-permute-start(f32[4,384,128]{2,1,0:T(8,128)S(1)} %get-tuple-element.55), channel_id=1, source_target_pairs={{1,0},{2,1},{3,2},{4,3},{5,4},{6,5},{7,6},{8,7},{9,8},{10,9},{11,1... | collective-permute-start | bytes 2359304 | tf_op jit(solution)/shard_map/ppermute | solution.py:311
  112.7 11.3 %collective-permute-start.17 = (f32[4,128,128]{2,1,0:T(8,128)S(1)}, f32[4,128,128]{2,1,0:T(8,128)S(1)}, u32[]{:S(2)}, u32[]{:S(2)}) collective-permute-start(f32[4,128,128]{2,1,0:T(8,128)S(1)} %get-tuple-element.58), channel_id=1, source_target_pairs={{0,32},{32,64},{64,96},{96,128},{128,160},{160,192},{192,224},{1,3... | collective-permute-start | bytes 786440 | tf_op jit(solution)/shard_map/ppermute | solution.py:311
  117.5 21.8 %collective-permute-start.15 = (f32[4,256,128]{2,1,0:T(8,128)S(1)}, f32[4,256,128]{2,1,0:T(8,128)S(1)}, u32[]{:S(2)}, u32[]{:S(2)}) collective-permute-start(f32[4,256,128]{2,1,0:T(8,128)S(1)} %get-tuple-element.56), channel_id=1, source_target_pairs={{0,1},{1,2},{2,3},{3,4},{4,5},{5,6},{6,7},{7,8},{8,9},{9,10},{10,1... | collective-permute-start | bytes 1572872 | tf_op jit(solution)/shard_map/ppermute | solution.py:311
  119.4 21.6 %collective-permute-start.16 = (f32[4,256,128]{2,1,0:T(8,128)S(1)}, f32[4,256,128]{2,1,0:T(8,128)S(1)}, u32[]{:S(2)}, u32[]{:S(2)}) collective-permute-start(f32[4,256,128]{2,1,0:T(8,128)S(1)} %get-tuple-element.57), channel_id=1, source_target_pairs={{1,0},{2,1},{3,2},{4,3},{5,4},{6,5},{7,6},{8,7},{9,8},{10,9},{11,1... | collective-permute-start | bytes 1572872 | tf_op jit(solution)/shard_map/ppermute | solution.py:311
  124.0 8.0 %collective-permute-start.18 = (f32[4,128,128]{2,1,0:T(8,128)S(1)}, f32[4,128,128]{2,1,0:T(8,128)S(1)}, u32[]{:S(2)}, u32[]{:S(2)}) collective-permute-start(f32[4,128,128]{2,1,0:T(8,128)S(1)} %get-tuple-element.59), channel_id=1, source_target_pairs={{32,0},{64,32},{96,64},{128,96},{160,128},{192,160},{224,192},{33,... | collective-permute-start | bytes 786440 | tf_op jit(solution)/shard_map/ppermute | solution.py:311
  157.4 23.6 %collective-permute-start.20 = (f32[4,384,128]{2,1,0:T(8,128)S(1)}, f32[4,384,128]{2,1,0:T(8,128)S(1)}, u32[]{:S(2)}, u32[]{:S(2)}) collective-permute-start(f32[4,384,128]{2,1,0:T(8,128)S(1)} %get-tuple-element.64), channel_id=1, source_target_pairs={{0,1},{1,2},{2,3},{3,4},{4,5},{5,6},{6,7},{7,8},{8,9},{9,10},{10,1... | collective-permute-start | bytes 2359304 | tf_op jit(solution)/shard_map/ppermute | solution.py:311
  159.3 5.2 %collective-permute-start.19 = (f32[4,128,128]{2,1,0:T(8,128)S(1)}, f32[4,128,128]{2,1,0:T(8,128)S(1)}, u32[]{:S(2)}, u32[]{:S(2)}) collective-permute-start(f32[4,128,128]{2,1,0:T(8,128)S(1)} %get-tuple-element.62), channel_id=1, source_target_pairs={{0,32},{32,64},{64,96},{96,128},{128,160},{160,192},{192,224},{1,3... | collective-permute-start | bytes 786440 | tf_op jit(solution)/shard_map/ppermute | solution.py:311
  161.3 19.8 %collective-permute-start.22 = (f32[4,128,256]{2,1,0:T(8,128)S(1)}, f32[4,128,256]{2,1,0:T(8,128)S(1)}, u32[]{:S(2)}, u32[]{:S(2)}) collective-permute-start(f32[4,128,256]{2,1,0:T(8,128)S(1)} %get-tuple-element.66), channel_id=1, source_target_pairs={{0,32},{32,64},{64,96},{96,128},{128,160},{160,192},{192,224},{1,3... | collective-permute-start | bytes 1572872 | tf_op jit(solution)/shard_map/ppermute | solution.py:311
  164.8 16.2 %collective-permute-start.21 = (f32[4,128,128]{2,1,0:T(8,128)S(1)}, f32[4,128,128]{2,1,0:T(8,128)S(1)}, u32[]{:S(2)}, u32[]{:S(2)}) collective-permute-start(f32[4,128,128]{2,1,0:T(8,128)S(1)} %get-tuple-element.65), channel_id=1, source_target_pairs={{0,1},{1,2},{2,3},{3,4},{4,5},{5,6},{6,7},{7,8},{8,9},{9,10},{10,1... | collective-permute-start | bytes 786440 | tf_op jit(solution)/shard_map/ppermute | solution.py:311

commit v2 on v1

--- a/solution.py
+++ b/solution.py
@@ -181,73 +181,113 @@
     return lax.axis_index(axis) < lax.axis_size(axis) - 1
 
 
-def assemble_kernel(main, right_top, right_rest, bottom, state):
+def assemble_kernel(main, right_top, right_rest, bottom, *rest):
+    state = rest[-1]
+    first = 0 if len(rest) == 1 else 2
+    for k in range(2):
+        p = first + k
+        state[p, :ROWS, :COLS] = main[first // 2, k]
+        state[p, :HALF, COLS:] = right_top[p]
+        state[p, HALF:ROWS, COLS:] = right_rest[k]
+        state[p, ROWS:, :] = bottom[p]
+
+
+def fold_sides(old, state, mid_l, mid_r, end_l, end_r, core):
+    scale = jnp.where(inside("col"), 0.5, 0.0).astype(f32)
+    drop = jnp.where(inside("row"), 1.0, 0.0).astype(f32)
     for p in range(4):
-        q = (p // 2, p % 2)
-        state[p, :ROWS, :COLS] = main[q]
-        state[p, :HALF, COLS:] = right_top[p]
-        state[p, HALF:ROWS, COLS:] = right_rest[p]
-        state[p, ROWS:, :] = bottom[p]
-
-
-def batch_kernel(batch, first, final):
-    def run(count, orow, ocol, wbatch, tab, probe, prop, amp, *rest):
-        if first:
-            state, grad, side_l, side_r, *edges = rest[1:]
-        else:
-            old, mid_l, mid_r, end_l, end_r, core_a, core_b = rest[:7]
-            outs = rest[7:]
-            state, grad, side_l, side_r, *edges = (*outs[:2], None, *outs[2:]) if final else outs
-            scale = jnp.where(inside("col"), 0.5, 0.0).astype(f32)
-            drop = jnp.where(inside("row"), 1.0, 0.0).astype(f32)
-            for p in range(4):
-                for cols, fac, mid, end in (
-                    (pl.ds(0, HALF), jnp.float32(0.5), mid_l, end_l),
-                    (pl.ds(COLS, HALF), scale, mid_r, end_r),
-                ):
-                    state[p, :HALF, cols] = old[p, :HALF, cols] - fac * end[p, :HALF]
-                    state[p, HALF:ROWS, cols] = old[p, HALF:ROWS, cols] - fac * mid[p]
-                    state[p, ROWS:, cols] = old[p, ROWS:, cols] - (fac * drop) * end[p, HALF:]
-                cols = pl.ds(HALF, HALF)
-                state[p, :HALF, cols] = old[p, :HALF, cols] - 0.5 * core_a[p]
-                state[p, ROWS:, cols] = old[p, ROWS:, cols] - (0.5 * drop) * core_b[p]
-        grad[...] = jnp.zeros_like(grad)
-
-        def step(s, _):
-            @pl.when((s < count[0, 0]) & (wbatch[0, 0, s] == batch))
-            def _():
-                r = orow[0, 0, s]
-                c = ocol[0, 0, s]
+        for cols, fac, mid, end in (
+            (pl.ds(0, HALF), jnp.float32(0.5), mid_l, end_l),
+            (pl.ds(COLS, HALF), scale, mid_r, end_r),
+        ):
+            state[p, :HALF, cols] = old[p, :HALF, cols] - fac * end[p, :HALF]
+            state[p, HALF:ROWS, cols] = old[p, HALF:ROWS, cols] - fac * mid[p]
+            state[p, ROWS:, cols] = old[p, ROWS:, cols] - (fac * drop) * end[p, HALF:]
+        cols = pl.ds(HALF, HALF)
+        state[p, ROWS:, cols] = old[p, ROWS:, cols] - (0.5 * drop) * core[p]
+
+
+def windows(batch, stages, count, orow, ocol, wbatch, tab, probe, prop, amp, state, grad, between, mid):
+    def step(s, _):
+        @pl.when((s < count[0, 0]) & (wbatch[0, 0, s] == batch))
+        def _():
+            r = orow[0, 0, s]
+            c = ocol[0, 0, s]
+            if "a" in stages:
                 psi = cmul((probe[0], probe[1]), load_window(state, 0, r, c))
                 f = forward_two(psi, tab)
                 bt = inverse_two(cmul((prop[0], prop[1]), f), tab)
+                if "b" not in stages:
+                    between[s, 0] = bt[0]
+                    between[s, 1] = bt[1]
+            if "b" in stages:
+                if "a" not in stages:
+                    bt = (between[s, 0], between[s, 1])
                 w2 = load_window(state, 2, r, c)
                 far = forward_two(cmul(bt, w2), tab)
                 power = far[0] * far[0] + far[1] * far[1]
                 factor = 1.0 - amp[s] * lax.rsqrt(jnp.maximum(power, 1.0))
                 back = inverse_two((far[0] * factor, far[1] * factor), tab)
                 add_window(grad, 2, r, c, cjmul(bt, back))
-                f = forward_two(cjmul(w2, back), tab)
+                m = cjmul(w2, back)
+                if "c" not in stages:
+                    mid[s, 0] = m[0]
+                    mid[s, 1] = m[1]
+            if "c" in stages:
+                if "b" not in stages:
+                    m = (mid[s, 0], mid[s, 1])
+                f = forward_two(m, tab)
                 back = inverse_two(cjmul((prop[0], prop[1]), f), tab)
                 add_window(grad, 0, r, c, cjmul((probe[0], probe[1]), back))
 
-            return 0
-
-        lax.fori_loop(0, SLOTS, step, 0)
-        side_r[...] = grad[:, HALF:ROWS, COLS:]
-        if final:
-            corner, low = edges
-            corner[...] = grad[:, ROWS:, COLS:]
-            low[...] = grad[:, ROWS:, :COLS]
-        else:
-            side_l[...] = grad[:, HALF:ROWS, :HALF]
-            top, bottom, top_core, bottom_core = edges
-            for out, core, rows in ((top, top_core, pl.ds(0, HALF)), (bottom, bottom_core, pl.ds(ROWS, HALF))):
-                out[:, :, :HALF] = grad[:, rows, :HALF]
-                out[:, :, HALF:] = grad[:, rows, COLS:]
-                core[...] = grad[:, rows, HALF:COLS]
+        return 0
+
+    lax.fori_loop(0, SLOTS, step, 0)
+
+
+def edges_of(grad, side_l, side_r, top, top_core, bottom):
+    side_l[...] = grad[:, HALF:ROWS, :HALF]
+    side_r[...] = grad[:, HALF:ROWS, COLS:]
+    top[:, :, :HALF] = grad[:, :HALF, :HALF]
+    top[:, :, HALF:] = grad[:, :HALF, COLS:]
+    top_core[...] = grad[:, :HALF, HALF:COLS]
+    bottom[...] = grad[:, ROWS:, :]
+
+
+def early_kernel(count, orow, ocol, wbatch, tab, probe, prop, state, between):
+    windows(0, "a", count, orow, ocol, wbatch, tab, probe, prop, None, state, None, between, None)
+
+
+def first_kernel(count, orow, ocol, wbatch, tab, probe, prop, amp, state, between, grad, *out):
+    grad[...] = jnp.zeros_like(grad)
+    windows(0, "bc", count, orow, ocol, wbatch, tab, probe, prop, amp, state, grad, between, None)
+    edges_of(grad, *out)
+
+
+def batch_kernel(batch):
+    def run(count, orow, ocol, wbatch, tab, probe, prop, amp, old, *rest):
+        sides, (state, grad), out = rest[:5], rest[5:7], rest[7:]
+        fold_sides(old, state, *sides)
+        grad[...] = jnp.zeros_like(grad)
+        windows(batch, "abc", count, orow, ocol, wbatch, tab, probe, prop, amp, state, grad, None, None)
+        edges_of(grad, *out)
 
     return run
+
+
+def final_kernel(count, orow, ocol, wbatch, tab, probe, prop, amp, old, *rest):
+    sides, (state, grad, mid, side_r) = rest[:5], rest[5:]
+    fold_sides(old, state, *sides)
+    grad[...] = jnp.zeros_like(grad)
+    windows(BATCHES - 1, "ab", count, orow, ocol, wbatch, tab, probe, prop, amp, state, grad, None, mid)
+    side_r[...] = grad[2:, HALF:ROWS, COLS:]
+
+
+def late_kernel(count, orow, ocol, wbatch, tab, probe, prop, mid, old, grad, side_r, corner, low):
+    windows(BATCHES - 1, "c", count, orow, ocol, wbatch, tab, probe, prop, None, None, grad, None, mid)
+    side_r[...] = grad[:2, HALF:ROWS, COLS:]
+    corner[...] = grad[:, ROWS:, COLS:]
+    low[...] = grad[:, ROWS:, :COLS]
 
 
 def settle_kernel(state, grad, above, below, out, end_l, end_r):
@@ -260,7 +300,9 @@
             left, mid, right = grad[p, rows, :h], grad[p, rows, h:COLS], grad[p, rows, COLS:]
             if near is not None:
                 left = left + near[p, :, :h]
-                right = right + near[p, :, h:]
+                right = right + near[p, :, -h:]
+                if at == 0:
+                    mid = mid + near[p, :, h:COLS]
                 end_l[p, ends] = left
                 end_r[p, ends] = right
             scale = in_r if at == ROWS else jnp.float32(0.5)
@@ -275,12 +317,13 @@
         out[p] = state[p, :ROWS, :COLS] - 0.5 * grad[p, :ROWS, :COLS]
 
 
-def last_kernel(state, mid, end, low, out):
+def last_kernel(state, mid1, mid2, end, low, out):
     h = HALF
     for p in range(4):
         q = (p // 2, p % 2)
+        mid = (mid1, mid2)[p // 2]
         out[(*q, slice(0, h), slice(0, h))] = state[p, :h, :h] - 0.5 * (end[p] + low[p, :, :h])
-        out[(*q, slice(h, ROWS), slice(0, h))] = state[p, h:, :h] - 0.5 * mid[p]
+        out[(*q, slice(h, ROWS), slice(0, h))] = state[p, h:, :h] - 0.5 * mid[p % 2]
         out[(*q, slice(0, h), slice(h, COLS))] = state[p, :h, h:] - 0.5 * low[p, :, h:]
         out[(*q, slice(h, ROWS), slice(h, COLS))] = state[p, h:, h:]
 
@@ -290,6 +333,9 @@
 EXT = (4, EXT_R, EXT_C)
 EDGE = (4, HALF, 2 * HALF)
 CORE = (4, HALF, HALF)
+FLAT = (4, HALF, EXT_C)
+SIDE = (2, ROWS - HALF, HALF)
+PLANES = (SLOTS, 2, WIN, WIN)
 MIDS = (4, ROWS - HALF, HALF)
 ENDS = (4, 2 * HALF, HALF)
 
@@ -318,49 +364,52 @@
     h = HALF
     planes = transmission.reshape(4, ROWS, COLS)
     right_top = from_behind(planes[:, :h, :h], "col", -1)
-    right_rest = from_behind(planes[:, h:, :h], "col", -1)
+    right_1 = from_behind(planes[:2, h:, :h], "col", -1)
+    right_2 = from_behind(planes[2:, h:, :h], "col", -1)
     amp, prop = call(prep_kernel, (), (amplitude, phase, order), [(SLOTS, WIN, WIN), (2, WIN, WIN)])
     low = cc([planes[:, :h, :], right_top], 2)
     bottom = from_behind(low, "row", -1)
-    (state,) = call(assemble_kernel, (), (transmission, right_top, right_rest, bottom), [EXT])
-    parts = ()
-    for b in range(BATCHES):
-        final = b == BATCHES - 1
-        outs = [MIDS, CORE, EDGE] if final else [MIDS, MIDS, EDGE, EDGE, CORE, CORE]
-        state, grad, *sent = call(
-            batch_kernel(b, b == 0, final),
-            scalars,
-            (tab, probe, prop, amp, state, *parts),
-            [EXT, EXT, *outs],
-            {8: 0},
-        )
-        if final:
-            side_r, corner, low = sent
-            mid_l = from_behind(side_r, "col", 1)
-            corner = from_behind(corner, "row", 1)
-            main, end_r = call(
-                final_settle_kernel, (), (state, grad, corner), [(4, ROWS, COLS), CORE]
+    (state,) = call(assemble_kernel, (), (transmission, right_top, right_1, bottom), [EXT])
+    (between,) = call(early_kernel, scalars, (tab, probe, prop, state), [PLANES])
+    (state,) = call(
+        assemble_kernel, (), (transmission, right_top, right_2, bottom, state), [EXT], {4: 0}
+    )
+    edges = [MIDS, MIDS, EDGE, CORE, FLAT]
+    for b in range(BATCHES - 1):
+        common = (tab, probe, prop, amp, state)
+        if b == 0:
+            grad, *sent = call(first_kernel, scalars, (*common, between), [EXT, *edges])
+        else:
+            state, grad, *sent = call(
+                batch_kernel(b), scalars, (*common, *parts), [EXT, EXT, *edges], {8: 0}
             )
-            end_l = from_behind(end_r, "col", 1)
-            low = from_behind(low, "row", 1)
-            break
-        side_l, side_r, top, bottom, top_core, bottom_core = sent
+        side_l, side_r, top, top_core, bottom = sent
         mid_l = from_behind(side_r, "col", 1)
         mid_r = from_behind(side_l, "col", -1)
         above = from_behind(bottom, "row", 1)
         below = from_behind(top, "row", -1)
+        core = from_behind(top_core, "row", -1)
         state, end_l, end_r = call(
             settle_kernel, (), (state, grad, above, below), [EXT, ENDS, ENDS], {0: 0}
         )
-        parts = (
-            mid_l,
-            mid_r,
-            from_behind(end_r, "col", 1),
-            from_behind(end_l, "col", -1),
-            from_behind(bottom_core, "row", 1),
-            from_behind(top_core, "row", -1),
-        )
-    return call(last_kernel, (), (main, mid_l, end_l, low), [(2, 2, ROWS, COLS)])[0]
+        parts = (mid_l, mid_r, from_behind(end_r, "col", 1), from_behind(end_l, "col", -1), core)
+    state, grad, mid, side_2 = call(
+        final_kernel,
+        scalars,
+        (tab, probe, prop, amp, state, *parts),
+        [EXT, EXT, PLANES, SIDE],
+        {8: 0},
+    )
+    mid_2 = from_behind(side_2, "col", 1)
+    grad, side_1, corner, low = call(
+        late_kernel, scalars, (tab, probe, prop, mid, grad), [EXT, SIDE, CORE, EDGE], {8: 0}
+    )
+    mid_1 = from_behind(side_1, "col", 1)
+    corner = from_behind(corner, "row", 1)
+    main, end_r = call(final_settle_kernel, (), (state, grad, corner), [(4, ROWS, COLS), CORE])
+    end = from_behind(end_r, "col", 1)
+    low = from_behind(low, "row", 1)
+    return call(last_kernel, (), (main, mid_1, mid_2, end, low), [(2, 2, ROWS, COLS)])[0]
 
 
 def solution(mesh):

time: 183 us -> 199 us (1.087)
  the two profiles are of different devices: /device:TPU:147 before, /device:TPU:12 now
where the time goes in v2:
time: 199 us; the launch traced here: 198 us
  starting transfers between devices  97.7 us (49%)
  waiting for transfers between devices  77.2 us (39%)
  Pallas kernels  18.4 us (9%)
  local copies, waits for them, and re-layouts  3.45 us (2%)
    ppermute x23, starting transfers between devices, from_behind(): return lax.ppermute(array, axis, pairs)  97.7 us
    ppermute x23, waiting for transfers between devices, from_behind(): return lax.ppermute(array, axis, pairs)  77.2 us
    pallas_call x12, Pallas kernels, call(): pl.pallas_call(kernel, in_specs=[SM] * len(scalars) + [VM] * len(arrays),...  18.4 us
  transfers between devices with their start and end apart: 23, of which 16 were waited for; matrix products, arithmetic and copies ran while one was open for 1% of the time, Pallas kernels for 4%

profile of v2, /device:TPU:12, one launch (start us, length us, event | category | flops | bytes accessed | tf_op | source)
XLA Modules:
  0.0 198.0 jit_solution(8720327589182596332)
XLA Ops:
  1.2 7.9 %collective-permute-start = (f32[4,128,128]{2,1,0:T(8,128)S(1)}, f32[4,128,128]{2,1,0:T(8,128)S(1)}, u32[]{:S(2)}, u32[]{:S(2)}) collective-permute-start(f32[4,128,128]{2,1,0:T(8,128)S(1)} %slice.16), channel_id=1, source_target_pairs={{1,0},{2,1},{3,2},{4,3},{5,4},{6,5},{7,6},{8,7},{9,8},{10,9},{11,1... | collective-permute-start | bytes 786440 | tf_op jit(solution)/shard_map/ppermute | solution.py:357
  10.1 4.5 %collective-permute-done.right_top = f32[4,128,128]{2,1,0:T(8,128)S(1)} collective-permute-done((f32[4,128,128]{2,1,0:T(8,128)S(1)}, f32[4,128,128]{2,1,0:T(8,128)S(1)}, u32[]{:S(2)}, u32[]{:S(2)}) %collective-permute-start) | collective-permute-done | bytes 262176 | tf_op jit(solution)/shard_map/ppermute | solution.py:357
  17.8 6.5 %collective-permute-start.3 = (f32[2,384,128]{2,1,0:T(8,128)S(1)}, f32[2,384,128]{2,1,0:T(8,128)S(1)}, u32[]{:S(2)}, u32[]{:S(2)}) collective-permute-start(f32[2,384,128]{2,1,0:T(8,128)S(1)} %get-tuple-element.67), channel_id=1, source_target_pairs={{1,0},{2,1},{3,2},{4,3},{5,4},{6,5},{7,6},{8,7},{9,8},{10,9},{11,1... | collective-permute-start | bytes 1179656 | tf_op jit(solution)/shard_map/ppermute | solution.py:357
  24.3 1.9 collective-permute-start.1
  26.9 4.2 %shard_map.100 = (f32[4,256,256]{2,1,0:T(8,128)S(1)}, f32[2,256,256]{2,1,0:T(8,128)S(1)}) custom-call(f32[1,1,4,256,256]{4,3,2,1,0:T(8,128)S(1)} %copy-done.3, f32[256,256]{1,0:T(8,128)S(1)} %copy-done.4, bf16[2,256,256]{2,1,0:T(8,128)(2,1)S(1)} %copy-done.5), custom_call_target="tpu_custom_call" | custom-call | tf_op jit(solution)/shard_map/pallas_call | solution.py:344
  31.1 2.6 %collective-permute-done.3.right_rest = f32[2,384,128]{2,1,0:T(8,128)S(1)} collective-permute-done((f32[2,384,128]{2,1,0:T(8,128)S(1)}, f32[2,384,128]{2,1,0:T(8,128)S(1)}, u32[]{:S(2)}, u32[]{:S(2)}) %collective-permute-start.3) | collective-permute-done | bytes 393248 | tf_op jit(solution)/shard_map/ppermute | solution.py:357
  34.6 7.1 %collective-permute-done.1.right_rest = f32[2,384,128]{2,1,0:T(8,128)S(1)} collective-permute-done((f32[2,384,128]{2,1,0:T(8,128)S(1)}, f32[2,384,128]{2,1,0:T(8,128)S(1)}, u32[]{:S(2)}, u32[]{:S(2)}) %collective-permute-start.1) | collective-permute-done | bytes 393248 | tf_op jit(solution)/shard_map/ppermute | solution.py:357
  44.8 3.6 %collective-permute-start.5 = (f32[4,128,256]{2,1,0:T(8,128)S(1)}, f32[4,128,256]{2,1,0:T(8,128)S(1)}, u32[]{:S(2)}, u32[]{:S(2)}) collective-permute-start(f32[4,128,256]{2,1,0:T(8,128)S(1)} %get-tuple-element.40), channel_id=1, source_target_pairs={{32,0},{64,32},{96,64},{128,96},{160,128},{192,160},{224,192},{33,... | collective-permute-start | bytes 1572872 | tf_op jit(solution)/shard_map/ppermute | solution.py:357
  48.5 6.2 %collective-permute-start.6 = (f32[4,384,128]{2,1,0:T(8,128)S(1)}, f32[4,384,128]{2,1,0:T(8,128)S(1)}, u32[]{:S(2)}, u32[]{:S(2)}) collective-permute-start(f32[4,384,128]{2,1,0:T(8,128)S(1)} %get-tuple-element.42), channel_id=1, source_target_pairs={{0,1},{1,2},{2,3},{3,4},{4,5},{5,6},{6,7},{7,8},{8,9},{9,10},{10,1... | collective-permute-start | bytes 2359304 | tf_op jit(solution)/shard_map/ppermute | solution.py:357
  54.7 5.7 %collective-permute-start.7 = (f32[4,384,128]{2,1,0:T(8,128)S(1)}, f32[4,384,128]{2,1,0:T(8,128)S(1)}, u32[]{:S(2)}, u32[]{:S(2)}) collective-permute-start(f32[4,384,128]{2,1,0:T(8,128)S(1)} %get-tuple-element.43), channel_id=1, source_target_pairs={{1,0},{2,1},{3,2},{4,3},{5,4},{6,5},{7,6},{8,7},{9,8},{10,9},{11,1... | collective-permute-start | bytes 2359304 | tf_op jit(solution)/shard_map/ppermute | solution.py:357
  61.3 4.1 %collective-permute-start.8 = (f32[4,256,128]{2,1,0:T(8,128)S(1)}, f32[4,256,128]{2,1,0:T(8,128)S(1)}, u32[]{:S(2)}, u32[]{:S(2)}) collective-permute-start(f32[4,256,128]{2,1,0:T(8,128)S(1)} %get-tuple-element.44), channel_id=1, source_target_pairs={{0,1},{1,2},{2,3},{3,4},{4,5},{5,6},{6,7},{7,8},{8,9},{9,10},{10,1... | collective-permute-start | bytes 1572872 | tf_op jit(solution)/shard_map/ppermute | solution.py:357
  65.4 3.9 %collective-permute-start.9 = (f32[4,256,128]{2,1,0:T(8,128)S(1)}, f32[4,256,128]{2,1,0:T(8,128)S(1)}, u32[]{:S(2)}, u32[]{:S(2)}) collective-permute-start(f32[4,256,128]{2,1,0:T(8,128)S(1)} %get-tuple-element.45), channel_id=1, source_target_pairs={{1,0},{2,1},{3,2},{4,3},{5,4},{6,5},{7,6},{8,7},{9,8},{10,9},{11,1... | collective-permute-start | bytes 1572872 | tf_op jit(solution)/shard_map/ppermute | solution.py:357
  69.2 2.7 %collective-permute-start.10 = (f32[4,128,128]{2,1,0:T(8,128)S(1)}, f32[4,128,128]{2,1,0:T(8,128)S(1)}, u32[]{:S(2)}, u32[]{:S(2)}) collective-permute-start(f32[4,128,128]{2,1,0:T(8,128)S(1)} %get-tuple-element.46), channel_id=1, source_target_pairs={{32,0},{64,32},{96,64},{128,96},{160,128},{192,160},{224,192},{33,... | collective-permute-start | bytes 786440 | tf_op jit(solution)/shard_map/ppermute | solution.py:357
  71.9 3.7 %collective-permute-done.10.rest_4_ = f32[4,128,128]{2,1,0:T(8,128)S(1)} collective-permute-done((f32[4,128,128]{2,1,0:T(8,128)S(1)}, f32[4,128,128]{2,1,0:T(8,128)S(1)}, u32[]{:S(2)}, u32[]{:S(2)}) %collective-permute-start.10) | collective-permute-done | bytes 262176 | tf_op jit(solution)/shard_map/ppermute | solution.py:357
  76.8 4.1 %collective-permute-done.7.rest_1_ = f32[4,384,128]{2,1,0:T(8,128)S(1)} collective-permute-done((f32[4,384,128]{2,1,0:T(8,128)S(1)}, f32[4,384,128]{2,1,0:T(8,128)S(1)}, u32[]{:S(2)}, u32[]{:S(2)}) %collective-permute-start.7) | collective-permute-done | bytes 786464 | tf_op jit(solution)/shard_map/ppermute | solution.py:357
  80.9 5.2 %collective-permute-done.8.rest_2_ = f32[4,256,128]{2,1,0:T(8,128)S(1)} collective-permute-done((f32[4,256,128]{2,1,0:T(8,128)S(1)}, f32[4,256,128]{2,1,0:T(8,128)S(1)}, u32[]{:S(2)}, u32[]{:S(2)}) %collective-permute-start.8) | collective-permute-done | bytes 524320 | tf_op jit(solution)/shard_map/ppermute | solution.py:357
  86.1 3.8 %collective-permute-done.9.rest_3_ = f32[4,256,128]{2,1,0:T(8,128)S(1)} collective-permute-done((f32[4,256,128]{2,1,0:T(8,128)S(1)}, f32[4,256,128]{2,1,0:T(8,128)S(1)}, u32[]{:S(2)}, u32[]{:S(2)}) %collective-permute-start.9) | collective-permute-done | bytes 524320 | tf_op jit(solution)/shard_map/ppermute | solution.py:357
  89.9 6.6 %shard_map.106 = (f32[4,640,384]{2,1,0:T(8,128)S(1)}, f32[4,640,384]{2,1,0:T(8,128)S(1)}, f32[4,384,128]{2,1,0:T(8,128)S(1)}, f32[4,384,128]{2,1,0:T(8,128)S(1)}...) custom-call(s32[1,1]{1,0:T(1,128)S(6)} %copy.23.count, ...), custom_call_target="tpu_custom_call", output_to_operand_aliasing={{0}: (8, {})} | custom-call | tf_op jit(solution)/shard_map/pallas_call | solution.py:344
  96.5 9.6 %collective-permute-start.11 = (f32[4,128,384]{2,1,0:T(8,128)S(1)}, f32[4,128,384]{2,1,0:T(8,128)S(1)}, u32[]{:S(2)}, u32[]{:S(2)}) collective-permute-start(f32[4,128,384]{2,1,0:T(8,128)S(1)} %get-tuple-element.49), channel_id=1, source_target_pairs={{0,32},{32,64},{64,96},{96,128},{128,160},{160,192},{192,224},{1,3... | collective-permute-start | bytes 2359304 | tf_op jit(solution)/shard_map/ppermute | solution.py:357
  110.0 6.0 %collective-permute-start.14 = (f32[4,384,128]{2,1,0:T(8,128)S(1)}, f32[4,384,128]{2,1,0:T(8,128)S(1)}, u32[]{:S(2)}, u32[]{:S(2)}) collective-permute-start(f32[4,384,128]{2,1,0:T(8,128)S(1)} %get-tuple-element.53), channel_id=1, source_target_pairs={{1,0},{2,1},{3,2},{4,3},{5,4},{6,5},{7,6},{8,7},{9,8},{10,9},{11,1... | collective-permute-start | bytes 2359304 | tf_op jit(solution)/shard_map/ppermute | solution.py:357
  118.9 6.0 %collective-permute-start.16 = (f32[4,256,128]{2,1,0:T(8,128)S(1)}, f32[4,256,128]{2,1,0:T(8,128)S(1)}, u32[]{:S(2)}, u32[]{:S(2)}) collective-permute-start(f32[4,256,128]{2,1,0:T(8,128)S(1)} %get-tuple-element.55), channel_id=1, source_target_pairs={{1,0},{2,1},{3,2},{4,3},{5,4},{6,5},{7,6},{8,7},{9,8},{10,9},{11,1... | collective-permute-start | bytes 1572872 | tf_op jit(solution)/shard_map/ppermute | solution.py:357
  124.9 2.2 %collective-permute-start.17 = (f32[4,128,128]{2,1,0:T(8,128)S(1)}, f32[4,128,128]{2,1,0:T(8,128)S(1)}, u32[]{:S(2)}, u32[]{:S(2)}) collective-permute-start(f32[4,128,128]{2,1,0:T(8,128)S(1)} %get-tuple-element.56), channel_id=1, source_target_pairs={{32,0},{64,32},{96,64},{128,96},{160,128},{192,160},{224,192},{33,... | collective-permute-start | bytes 786440 | tf_op jit(solution)/shard_map/ppermute | solution.py:357
  127.2 3.9 %collective-permute-done.17.rest_4_ = f32[4,128,128]{2,1,0:T(8,128)S(1)} collective-permute-done((f32[4,128,128]{2,1,0:T(8,128)S(1)}, f32[4,128,128]{2,1,0:T(8,128)S(1)}, u32[]{:S(2)}, u32[]{:S(2)}) %collective-permute-start.17) | collective-permute-done | bytes 262176 | tf_op jit(solution)/shard_map/ppermute | solution.py:357
  133.9 9.5 %collective-permute-done.15.rest_2_ = f32[4,256,128]{2,1,0:T(8,128)S(1)} collective-permute-done((f32[4,256,128]{2,1,0:T(8,128)S(1)}, f32[4,256,128]{2,1,0:T(8,128)S(1)}, u32[]{:S(2)}, u32[]{:S(2)}) %collective-permute-start.15) | collective-permute-done | bytes 524320 | tf_op jit(solution)/shard_map/ppermute | solution.py:357
  146.9 6.6 %collective-permute-start.18 = (f32[4,128,128]{2,1,0:T(8,128)S(1)}, f32[4,128,128]{2,1,0:T(8,128)S(1)}, u32[]{:S(2)}, u32[]{:S(2)}) collective-permute-start(f32[4,128,128]{2,1,0:T(8,128)S(1)} %get-tuple-element.61), channel_id=1, source_target_pairs={{0,32},{32,64},{64,96},{96,128},{128,160},{160,192},{192,224},{1,3... | collective-permute-start | bytes 786440 | tf_op jit(solution)/shard_map/ppermute | solution.py:357
  153.5 2.8 %collective-permute-start.22 = (f32[4,128,256]{2,1,0:T(8,128)S(1)}, f32[4,128,256]{2,1,0:T(8,128)S(1)}, u32[]{:S(2)}, u32[]{:S(2)}) collective-permute-start(f32[4,128,256]{2,1,0:T(8,128)S(1)} %get-tuple-element.66), channel_id=1, source_target_pairs={{0,32},{32,64},{64,96},{96,128},{128,160},{160,192},{192,224},{1,3... | collective-permute-start | bytes 1572872 | tf_op jit(solution)/shard_map/ppermute | solution.py:357
  156.3 4.6 %collective-permute-start.20 = (f32[2,384,128]{2,1,0:T(8,128)S(1)}, f32[2,384,128]{2,1,0:T(8,128)S(1)}, u32[]{:S(2)}, u32[]{:S(2)}) collective-permute-start(f32[2,384,128]{2,1,0:T(8,128)S(1)} %get-tuple-element.64), channel_id=1, source_target_pairs={{0,1},{1,2},{2,3},{3,4},{4,5},{5,6},{6,7},{7,8},{8,9},{9,10},{10,1... | collective-permute-start | bytes 1179656 | tf_op jit(solution)/shard_map/ppermute | solution.py:357
  161.0 1.9 collective-permute-start.19
  163.1 5.8 %collective-permute-start.21 = (f32[4,128,128]{2,1,0:T(8,128)S(1)}, f32[4,128,128]{2,1,0:T(8,128)S(1)}, u32[]{:S(2)}, u32[]{:S(2)}) collective-permute-start(f32[4,128,128]{2,1,0:T(8,128)S(1)} %get-tuple-element.65), channel_id=1, source_target_pairs={{0,1},{1,2},{2,3},{3,4},{4,5},{5,6},{6,7},{7,8},{8,9},{9,10},{10,1... | collective-permute-start | bytes 786440 | tf_op jit(solution)/shard_map/ppermute | solution.py:357
  169.0 14.1 %collective-permute-done.20.mid2 = f32[2,384,128]{2,1,0:T(8,128)S(1)} collective-permute-done((f32[2,384,128]{2,1,0:T(8,128)S(1)}, f32[2,384,128]{2,1,0:T(8,128)S(1)}, u32[]{:S(2)}, u32[]{:S(2)}) %collective-permute-start.20) | collective-permute-done | bytes 393248 | tf_op jit(solution)/shard_map/ppermute | solution.py:357
  183.0 8.4 %collective-permute-done.19.mid1 = f32[2,384,128]{2,1,0:T(8,128)S(1)} collective-permute-done((f32[2,384,128]{2,1,0:T(8,128)S(1)}, f32[2,384,128]{2,1,0:T(8,128)S(1)}, u32[]{:S(2)}, u32[]{:S(2)}) %collective-permute-start.19) | collective-permute-done | bytes 393248 | tf_op jit(solution)/shard_map/ppermute | solution.py:357
  191.5 4.9 %collective-permute-done.21.end = f32[4,128,128]{2,1,0:T(8,128)S(1)} collective-permute-done((f32[4,128,128]{2,1,0:T(8,128)S(1)}, f32[4,128,128]{2,1,0:T(8,128)S(1)}, u32[]{:S(2)}, u32[]{:S(2)}) %collective-permute-start.21) | collective-permute-done | bytes 262176 | tf_op jit(solution)/shard_map/ppermute | solution.py:357
  (48 shorter events, 26.1 us)
Async XLA Ops:
  0.0 26.8 %copy-start.5 = (bf16[2,256,256]{2,1,0:T(8,128)(2,1)S(1)}, bf16[2,256,256]{2,1,0:T(8,128)(2,1)}, u32[]{:S(2)}) copy-start(bf16[2,256,256]{2,1,0:T(8,128)(2,1)} %constant.5.clone.order) | copy-start | bytes 786436
  0.0 33.8 %copy-start.1 = (f32[2,2,512,256]{3,2,1,0:T(8,128)S(1)}, f32[2,2,512,256]{3,2,1,0:T(8,128)}, u32[]{:S(2)}) copy-start(f32[2,2,512,256]{3,2,1,0:T(8,128)} %main.3) | copy-start | bytes 6291460
  0.0 26.8 %copy-start.3 = (f32[1,1,4,256,256]{4,3,2,1,0:T(8,128)S(1)}, f32[1,1,4,256,256]{4,3,2,1,0:T(8,128)}, u32[]{:S(2)}) copy-start(f32[1,1,4,256,256]{4,3,2,1,0:T(8,128)} %amp.1) | copy-start | bytes 3145732
  0.0 26.8 %copy-start.4 = (f32[256,256]{1,0:T(8,128)S(1)}, f32[256,256]{1,0:T(8,128)}, u32[]{:S(2)}) copy-start(f32[256,256]{1,0:T(8,128)} %phase.1) | copy-start | bytes 786436
  1.2 13.4 %collective-permute-start = (f32[4,128,128]{2,1,0:T(8,128)S(1)}, f32[4,128,128]{2,1,0:T(8,128)S(1)}, u32[]{:S(2)}, u32[]{:S(2)}) collective-permute-start(f32[4,128,128]{2,1,0:T(8,128)S(1)} %slice.16), channel_id=1, source_target_pairs={{1,0},{2,1},{3,2},{4,3},{5,4},{6,5},{7,6},{8,7},{9,8},{10,9},{11,1... | collective-permute-start | bytes 786440 | tf_op jit(solution)/shard_map/ppermute | solution.py:357
  14.6 19.1 %collective-permute-start.2 = (f32[4,128,384]{2,1,0:T(8,128)S(1)}, f32[4,128,384]{2,1,0:T(8,128)S(1)}, u32[]{:S(2)}, u32[]{:S(2)}) collective-permute-start(f32[4,128,384]{2,1,0:T(8,128)S(1)} %pad_maximum_fusion), channel_id=1, source_target_pairs={{32,0},{64,32},{96,64},{128,96},{160,128},{192,160},{224,192},{33,... | collective-permute-start | bytes 2359304 | tf_op jit(solution)/shard_map/ppermute | solution.py:357
  17.8 16.0 %collective-permute-start.3 = (f32[2,384,128]{2,1,0:T(8,128)S(1)}, f32[2,384,128]{2,1,0:T(8,128)S(1)}, u32[]{:S(2)}, u32[]{:S(2)}) collective-permute-start(f32[2,384,128]{2,1,0:T(8,128)S(1)} %get-tuple-element.67), channel_id=1, source_target_pairs={{1,0},{2,1},{3,2},{4,3},{5,4},{6,5},{7,6},{8,7},{9,8},{10,9},{11,1... | collective-permute-start | bytes 1179656 | tf_op jit(solution)/shard_map/ppermute | solution.py:357
  24.3 17.4 %collective-permute-start.1 = (f32[2,384,128]{2,1,0:T(8,128)S(1)}, f32[2,384,128]{2,1,0:T(8,128)S(1)}, u32[]{:S(2)}, u32[]{:S(2)}) collective-permute-start(f32[2,384,128]{2,1,0:T(8,128)S(1)} %get-tuple-element.68), channel_id=1, source_target_pairs={{1,0},{2,1},{3,2},{4,3},{5,4},{6,5},{7,6},{8,7},{9,8},{10,9},{11,1... | collective-permute-start | bytes 1179656 | tf_op jit(solution)/shard_map/ppermute | solution.py:357
  31.0 2.8 %copy-start = (bf16[2,2,2,256,256]{4,3,2,1,0:T(8,128)(2,1)S(1)}, bf16[2,2,2,256,256]{4,3,2,1,0:T(8,128)(2,1)}, u32[]{:S(2)}) copy-start(bf16[2,2,2,256,256]{4,3,2,1,0:T(8,128)(2,1)} %constant.4.clone.tab) | copy-start | bytes 3145732
  31.1 2.8 %copy-start.2 = (f32[2,256,256]{2,1,0:T(8,128)S(1)}, f32[2,256,256]{2,1,0:T(8,128)}, u32[]{:S(2)}) copy-start(f32[2,256,256]{2,1,0:T(8,128)} %probe.9) | copy-start | bytes 1572868
  31.1 2.8 %copy-start.6 = (s32[1,1,4]{2,1,0:T(1,128)S(1)}, s32[1,1,4]{2,1,0:T(1,128)}, u32[]{:S(2)}) copy-start(s32[1,1,4]{2,1,0:T(1,128)} %orow.9) | copy-start | bytes 52
  31.1 2.8 %copy-start.7 = (s32[1,1,4]{2,1,0:T(1,128)S(1)}, s32[1,1,4]{2,1,0:T(1,128)}, u32[]{:S(2)}) copy-start(s32[1,1,4]{2,1,0:T(1,128)} %ocol.9) | copy-start | bytes 52
  31.1 2.8 %copy-start.8 = (s32[1,1,4]{2,1,0:T(1,128)S(1)}, s32[1,1,4]{2,1,0:T(1,128)}, u32[]{:S(2)}) copy-start(s32[1,1,4]{2,1,0:T(1,128)} %wbatch.9) | copy-start | bytes 52
  42.9 17.4 %collective-permute-start.4 = (f32[4,128,384]{2,1,0:T(8,128)S(1)}, f32[4,128,384]{2,1,0:T(8,128)S(1)}, u32[]{:S(2)}, u32[]{:S(2)}) collective-permute-start(f32[4,128,384]{2,1,0:T(8,128)S(1)} %get-tuple-element.39), channel_id=1, source_target_pairs={{0,32},{32,64},{64,96},{96,128},{128,160},{160,192},{192,224},{1,3... | collective-permute-start | bytes 2359304 | tf_op jit(solution)/shard_map/ppermute | solution.py:357
  44.8 15.5 %collective-permute-start.5 = (f32[4,128,256]{2,1,0:T(8,128)S(1)}, f32[4,128,256]{2,1,0:T(8,128)S(1)}, u32[]{:S(2)}, u32[]{:S(2)}) collective-permute-start(f32[4,128,256]{2,1,0:T(8,128)S(1)} %get-tuple-element.40), channel_id=1, source_target_pairs={{32,0},{64,32},{96,64},{128,96},{160,128},{192,160},{224,192},{33,... | collective-permute-start | bytes 1572872 | tf_op jit(solution)/shard_map/ppermute | solution.py:357
  48.5 28.3 %collective-permute-start.6 = (f32[4,384,128]{2,1,0:T(8,128)S(1)}, f32[4,384,128]{2,1,0:T(8,128)S(1)}, u32[]{:S(2)}, u32[]{:S(2)}) collective-permute-start(f32[4,384,128]{2,1,0:T(8,128)S(1)} %get-tuple-element.42), channel_id=1, source_target_pairs={{0,1},{1,2},{2,3},{3,4},{4,5},{5,6},{6,7},{7,8},{8,9},{9,10},{10,1... | collective-permute-start | bytes 2359304 | tf_op jit(solution)/shard_map/ppermute | solution.py:357
  54.7 26.2 %collective-permute-start.7 = (f32[4,384,128]{2,1,0:T(8,128)S(1)}, f32[4,384,128]{2,1,0:T(8,128)S(1)}, u32[]{:S(2)}, u32[]{:S(2)}) collective-permute-start(f32[4,384,128]{2,1,0:T(8,128)S(1)} %get-tuple-element.43), channel_id=1, source_target_pairs={{1,0},{2,1},{3,2},{4,3},{5,4},{6,5},{7,6},{8,7},{9,8},{10,9},{11,1... | collective-permute-start | bytes 2359304 | tf_op jit(solution)/shard_map/ppermute | solution.py:357
  61.3 24.9 %collective-permute-start.8 = (f32[4,256,128]{2,1,0:T(8,128)S(1)}, f32[4,256,128]{2,1,0:T(8,128)S(1)}, u32[]{:S(2)}, u32[]{:S(2)}) collective-permute-start(f32[4,256,128]{2,1,0:T(8,128)S(1)} %get-tuple-element.44), channel_id=1, source_target_pairs={{0,1},{1,2},{2,3},{3,4},{4,5},{5,6},{6,7},{7,8},{8,9},{9,10},{10,1... | collective-permute-start | bytes 1572872 | tf_op jit(solution)/shard_map/ppermute | solution.py:357
  65.4 24.6 %collective-permute-start.9 = (f32[4,256,128]{2,1,0:T(8,128)S(1)}, f32[4,256,128]{2,1,0:T(8,128)S(1)}, u32[]{:S(2)}, u32[]{:S(2)}) collective-permute-start(f32[4,256,128]{2,1,0:T(8,128)S(1)} %get-tuple-element.45), channel_id=1, source_target_pairs={{1,0},{2,1},{3,2},{4,3},{5,4},{6,5},{7,6},{8,7},{9,8},{10,9},{11,1... | collective-permute-start | bytes 1572872 | tf_op jit(solution)/shard_map/ppermute | solution.py:357
  69.2 6.4 %collective-permute-start.10 = (f32[4,128,128]{2,1,0:T(8,128)S(1)}, f32[4,128,128]{2,1,0:T(8,128)S(1)}, u32[]{:S(2)}, u32[]{:S(2)}) collective-permute-start(f32[4,128,128]{2,1,0:T(8,128)S(1)} %get-tuple-element.46), channel_id=1, source_target_pairs={{32,0},{64,32},{96,64},{128,96},{160,128},{192,160},{224,192},{33,... | collective-permute-start | bytes 786440 | tf_op jit(solution)/shard_map/ppermute | solution.py:357
  96.5 19.5 %collective-permute-start.11 = (f32[4,128,384]{2,1,0:T(8,128)S(1)}, f32[4,128,384]{2,1,0:T(8,128)S(1)}, u32[]{:S(2)}, u32[]{:S(2)}) collective-permute-start(f32[4,128,384]{2,1,0:T(8,128)S(1)} %get-tuple-element.49), channel_id=1, source_target_pairs={{0,32},{32,64},{64,96},{96,128},{128,160},{160,192},{192,224},{1,3... | collective-permute-start | bytes 2359304 | tf_op jit(solution)/shard_map/ppermute | solution.py:357
  106.1 9.9 %collective-permute-start.12 = (f32[4,128,256]{2,1,0:T(8,128)S(1)}, f32[4,128,256]{2,1,0:T(8,128)S(1)}, u32[]{:S(2)}, u32[]{:S(2)}) collective-permute-start(f32[4,128,256]{2,1,0:T(8,128)S(1)} %get-tuple-element.50), channel_id=1, source_target_pairs={{32,0},{64,32},{96,64},{128,96},{160,128},{192,160},{224,192},{33,... | collective-permute-start | bytes 1572872 | tf_op jit(solution)/shard_map/ppermute | solution.py:357
  108.1 24.4 %collective-permute-start.13 = (f32[4,384,128]{2,1,0:T(8,128)S(1)}, f32[4,384,128]{2,1,0:T(8,128)S(1)}, u32[]{:S(2)}, u32[]{:S(2)}) collective-permute-start(f32[4,384,128]{2,1,0:T(8,128)S(1)} %get-tuple-element.52), channel_id=1, source_target_pairs={{0,1},{1,2},{2,3},{3,4},{4,5},{5,6},{6,7},{7,8},{8,9},{9,10},{10,1... | collective-permute-start | bytes 2359304 | tf_op jit(solution)/shard_map/ppermute | solution.py:357
  110.0 24.0 %collective-permute-start.14 = (f32[4,384,128]{2,1,0:T(8,128)S(1)}, f32[4,384,128]{2,1,0:T(8,128)S(1)}, u32[]{:S(2)}, u32[]{:S(2)}) collective-permute-start(f32[4,384,128]{2,1,0:T(8,128)S(1)} %get-tuple-element.53), channel_id=1, source_target_pairs={{1,0},{2,1},{3,2},{4,3},{5,4},{6,5},{7,6},{8,7},{9,8},{10,9},{11,1... | collective-permute-start | bytes 2359304 | tf_op jit(solution)/shard_map/ppermute | solution.py:357
  117.0 26.5 %collective-permute-start.15 = (f32[4,256,128]{2,1,0:T(8,128)S(1)}, f32[4,256,128]{2,1,0:T(8,128)S(1)}, u32[]{:S(2)}, u32[]{:S(2)}) collective-permute-start(f32[4,256,128]{2,1,0:T(8,128)S(1)} %get-tuple-element.54), channel_id=1, source_target_pairs={{0,1},{1,2},{2,3},{3,4},{4,5},{5,6},{6,7},{7,8},{8,9},{9,10},{10,1... | collective-permute-start | bytes 1572872 | tf_op jit(solution)/shard_map/ppermute | solution.py:357
  118.9 25.8 %collective-permute-start.16 = (f32[4,256,128]{2,1,0:T(8,128)S(1)}, f32[4,256,128]{2,1,0:T(8,128)S(1)}, u32[]{:S(2)}, u32[]{:S(2)}) collective-permute-start(f32[4,256,128]{2,1,0:T(8,128)S(1)} %get-tuple-element.55), channel_id=1, source_target_pairs={{1,0},{2,1},{3,2},{4,3},{5,4},{6,5},{7,6},{8,7},{9,8},{10,9},{11,1... | collective-permute-start | bytes 1572872 | tf_op jit(solution)/shard_map/ppermute | solution.py:357
  124.9 6.1 %collective-permute-start.17 = (f32[4,128,128]{2,1,0:T(8,128)S(1)}, f32[4,128,128]{2,1,0:T(8,128)S(1)}, u32[]{:S(2)}, u32[]{:S(2)}) collective-permute-start(f32[4,128,128]{2,1,0:T(8,128)S(1)} %get-tuple-element.56), channel_id=1, source_target_pairs={{32,0},{64,32},{96,64},{128,96},{160,128},{192,160},{224,192},{33,... | collective-permute-start | bytes 786440 | tf_op jit(solution)/shard_map/ppermute | solution.py:357
  146.9 16.0 %collective-permute-start.18 = (f32[4,128,128]{2,1,0:T(8,128)S(1)}, f32[4,128,128]{2,1,0:T(8,128)S(1)}, u32[]{:S(2)}, u32[]{:S(2)}) collective-permute-start(f32[4,128,128]{2,1,0:T(8,128)S(1)} %get-tuple-element.61), channel_id=1, source_target_pairs={{0,32},{32,64},{64,96},{96,128},{128,160},{160,192},{192,224},{1,3... | collective-permute-start | bytes 786440 | tf_op jit(solution)/shard_map/ppermute | solution.py:357
  153.5 37.9 %collective-permute-start.22 = (f32[4,128,256]{2,1,0:T(8,128)S(1)}, f32[4,128,256]{2,1,0:T(8,128)S(1)}, u32[]{:S(2)}, u32[]{:S(2)}) collective-permute-start(f32[4,128,256]{2,1,0:T(8,128)S(1)} %get-tuple-element.66), channel_id=1, source_target_pairs={{0,32},{32,64},{64,96},{96,128},{128,160},{160,192},{192,224},{1,3... | collective-permute-start | bytes 1572872 | tf_op jit(solution)/shard_map/ppermute | solution.py:357
  156.3 26.7 %collective-permute-start.20 = (f32[2,384,128]{2,1,0:T(8,128)S(1)}, f32[2,384,128]{2,1,0:T(8,128)S(1)}, u32[]{:S(2)}, u32[]{:S(2)}) collective-permute-start(f32[2,384,128]{2,1,0:T(8,128)S(1)} %get-tuple-element.64), channel_id=1, source_target_pairs={{0,1},{1,2},{2,3},{3,4},{4,5},{5,6},{6,7},{7,8},{8,9},{9,10},{10,1... | collective-permute-start | bytes 1179656 | tf_op jit(solution)/shard_map/ppermute | solution.py:357
  161.0 30.5 %collective-permute-start.19 = (f32[2,384,128]{2,1,0:T(8,128)S(1)}, f32[2,384,128]{2,1,0:T(8,128)S(1)}, u32[]{:S(2)}, u32[]{:S(2)}) collective-permute-start(f32[2,384,128]{2,1,0:T(8,128)S(1)} %get-tuple-element.63), channel_id=1, source_target_pairs={{0,1},{1,2},{2,3},{3,4},{4,5},{5,6},{6,7},{7,8},{8,9},{9,10},{10,1... | collective-permute-start | bytes 1179656 | tf_op jit(solution)/shard_map/ppermute | solution.py:357
  163.1 33.3 %collective-permute-start.21 = (f32[4,128,128]{2,1,0:T(8,128)S(1)}, f32[4,128,128]{2,1,0:T(8,128)S(1)}, u32[]{:S(2)}, u32[]{:S(2)}) collective-permute-start(f32[4,128,128]{2,1,0:T(8,128)S(1)} %get-tuple-element.65), channel_id=1, source_target_pairs={{0,1},{1,2},{2,3},{3,4},{4,5},{5,6},{6,7},{7,8},{8,9},{9,10},{10,1... | collective-permute-start | bytes 786440 | tf_op jit(solution)/shard_map/ppermute | solution.py:357

commit v3 on v2

--- a/solution.py
+++ b/solution.py
@@ -192,19 +192,16 @@
         state[p, ROWS:, :] = bottom[p]
 
 
-def fold_sides(old, state, mid_l, mid_r, end_l, end_r, core):
-    scale = jnp.where(inside("col"), 0.5, 0.0).astype(f32)
-    drop = jnp.where(inside("row"), 1.0, 0.0).astype(f32)
+def fold_sides(old, state, mid_l, mid_r, above, below):
+    in_c = jnp.where(inside("col"), 1.0, 0.0).astype(f32)
+    in_r = jnp.where(inside("row"), 1.0, 0.0).astype(f32)
+    rows = pl.ds(HALF, ROWS - HALF)
     for p in range(4):
-        for cols, fac, mid, end in (
-            (pl.ds(0, HALF), jnp.float32(0.5), mid_l, end_l),
-            (pl.ds(COLS, HALF), scale, mid_r, end_r),
-        ):
-            state[p, :HALF, cols] = old[p, :HALF, cols] - fac * end[p, :HALF]
-            state[p, HALF:ROWS, cols] = old[p, HALF:ROWS, cols] - fac * mid[p]
-            state[p, ROWS:, cols] = old[p, ROWS:, cols] - (fac * drop) * end[p, HALF:]
-        cols = pl.ds(HALF, HALF)
-        state[p, ROWS:, cols] = old[p, ROWS:, cols] - (0.5 * drop) * core[p]
+        state[p, rows, :HALF] = old[p, rows, :HALF] - 0.5 * mid_l[p]
+        state[p, rows, COLS:] = old[p, rows, COLS:] - (0.5 * in_c) * mid_r[p]
+        for at, fac, near in ((pl.ds(0, HALF), 0.5, above), (pl.ds(ROWS, HALF), 0.5 * in_r, below)):
+            state[p, at, :COLS] = old[p, at, :COLS] - fac * near[p, :, :COLS]
+            state[p, at, COLS:] = old[p, at, COLS:] - (fac * in_c) * near[p, :, COLS:]
 
 
 def windows(batch, stages, count, orow, ocol, wbatch, tab, probe, prop, amp, state, grad, between, mid):
@@ -245,13 +242,11 @@
     lax.fori_loop(0, SLOTS, step, 0)
 
 
-def edges_of(grad, side_l, side_r, top, top_core, bottom):
-    side_l[...] = grad[:, HALF:ROWS, :HALF]
-    side_r[...] = grad[:, HALF:ROWS, COLS:]
-    top[:, :, :HALF] = grad[:, :HALF, :HALF]
-    top[:, :, HALF:] = grad[:, :HALF, COLS:]
-    top_core[...] = grad[:, :HALF, HALF:COLS]
-    bottom[...] = grad[:, ROWS:, :]
+def edges_of(grad, mid_l, mid_r, end_l, end_r):
+    for mid, end, cols in ((mid_l, end_l, pl.ds(0, HALF)), (mid_r, end_r, pl.ds(COLS, HALF))):
+        mid[...] = grad[:, HALF:ROWS, cols]
+        end[:, :HALF, :] = grad[:, :HALF, cols]
+        end[:, HALF:, :] = grad[:, ROWS:, cols]
 
 
 def early_kernel(count, orow, ocol, wbatch, tab, probe, prop, state, between):
@@ -266,7 +261,7 @@
 
 def batch_kernel(batch):
     def run(count, orow, ocol, wbatch, tab, probe, prop, amp, old, *rest):
-        sides, (state, grad), out = rest[:5], rest[5:7], rest[7:]
+        sides, (state, grad), out = rest[:4], rest[4:6], rest[6:]
         fold_sides(old, state, *sides)
         grad[...] = jnp.zeros_like(grad)
         windows(batch, "abc", count, orow, ocol, wbatch, tab, probe, prop, amp, state, grad, None, None)
@@ -276,7 +271,7 @@
 
 
 def final_kernel(count, orow, ocol, wbatch, tab, probe, prop, amp, old, *rest):
-    sides, (state, grad, mid, side_r) = rest[:5], rest[5:]
+    sides, (state, grad, mid, side_r) = rest[:4], rest[4:]
     fold_sides(old, state, *sides)
     grad[...] = jnp.zeros_like(grad)
     windows(BATCHES - 1, "ab", count, orow, ocol, wbatch, tab, probe, prop, amp, state, grad, None, mid)
@@ -290,21 +285,20 @@
     low[...] = grad[:, ROWS:, :COLS]
 
 
-def settle_kernel(state, grad, above, below, out, end_l, end_r):
+def settle_kernel(state, grad, end_l, end_r, out, top, bottom):
     in_r = jnp.where(inside("row"), 0.5, 0.0).astype(f32)
     in_c = jnp.where(inside("col"), 1.0, 0.0).astype(f32)
     h = HALF
     for p in range(4):
-        for at, near, ends in ((0, above, pl.ds(0, h)), (h, None, None), (ROWS, below, pl.ds(h, h))):
-            rows = pl.ds(at, ROWS - h if near is None else h)
+        for at, flat, ends in ((0, top, pl.ds(0, h)), (h, None, None), (ROWS, bottom, pl.ds(h, h))):
+            rows = pl.ds(at, ROWS - h if flat is None else h)
             left, mid, right = grad[p, rows, :h], grad[p, rows, h:COLS], grad[p, rows, COLS:]
-            if near is not None:
-                left = left + near[p, :, :h]
-                right = right + near[p, :, -h:]
-                if at == 0:
-                    mid = mid + near[p, :, h:COLS]
-                end_l[p, ends] = left
-                end_r[p, ends] = right
+            if flat is not None:
+                left = left + end_l[p, ends]
+                right = right + end_r[p, ends]
+                flat[p, :, :h] = left
+                flat[p, :, h:COLS] = mid
+                flat[p, :, COLS:] = right
             scale = in_r if at == ROWS else jnp.float32(0.5)
             out[p, rows, :h] = state[p, rows, :h] - scale * left
             out[p, rows, h:COLS] = state[p, rows, h:COLS] - scale * mid
@@ -374,7 +368,7 @@
     (state,) = call(
         assemble_kernel, (), (transmission, right_top, right_2, bottom, state), [EXT], {4: 0}
     )
-    edges = [MIDS, MIDS, EDGE, CORE, FLAT]
+    edges = [MIDS, MIDS, ENDS, ENDS]
     for b in range(BATCHES - 1):
         common = (tab, probe, prop, amp, state)
         if b == 0:
@@ -383,16 +377,15 @@
             state, grad, *sent = call(
                 batch_kernel(b), scalars, (*common, *parts), [EXT, EXT, *edges], {8: 0}
             )
-        side_l, side_r, top, top_core, bottom = sent
-        mid_l = from_behind(side_r, "col", 1)
-        mid_r = from_behind(side_l, "col", -1)
-        above = from_behind(bottom, "row", 1)
-        below = from_behind(top, "row", -1)
-        core = from_behind(top_core, "row", -1)
-        state, end_l, end_r = call(
-            settle_kernel, (), (state, grad, above, below), [EXT, ENDS, ENDS], {0: 0}
+        mid_l, mid_r, end_l, end_r = sent
+        from_left = from_behind(end_r, "col", 1)
+        from_right = from_behind(end_l, "col", -1)
+        mid_left = from_behind(mid_r, "col", 1)
+        mid_right = from_behind(mid_l, "col", -1)
+        state, top, bottom = call(
+            settle_kernel, (), (state, grad, from_left, from_right), [EXT, FLAT, FLAT], {0: 0}
         )
-        parts = (mid_l, mid_r, from_behind(end_r, "col", 1), from_behind(end_l, "col", -1), core)
+        parts = (mid_left, mid_right, from_behind(bottom, "row", 1), from_behind(top, "row", -1))
     state, grad, mid, side_2 = call(
         final_kernel,
         scalars,
@@ -406,9 +399,9 @@
     )
     mid_1 = from_behind(side_1, "col", 1)
     corner = from_behind(corner, "row", 1)
+    low = from_behind(low, "row", 1)
     main, end_r = call(final_settle_kernel, (), (state, grad, corner), [(4, ROWS, COLS), CORE])
     end = from_behind(end_r, "col", 1)
-    low = from_behind(low, "row", 1)
     return call(last_kernel, (), (main, mid_1, mid_2, end, low), [(2, 2, ROWS, COLS)])[0]
 
 

time: 199 us -> 190 us (0.955)
  the two profiles are of different devices: /device:TPU:12 before, /device:TPU:6 now
where the time goes in v3:
time: 190 us; the launch traced here: 189 us
  starting transfers between devices  103 us (54%)
  waiting for transfers between devices  62.9 us (33%)
  Pallas kernels  18.4 us (10%)
  local copies, waits for them, and re-layouts  3.45 us (2%)
    ppermute x21, starting transfers between devices, from_behind(): return lax.ppermute(array, axis, pairs)  103 us
    ppermute x21, waiting for transfers between devices, from_behind(): return lax.ppermute(array, axis, pairs)  62.9 us
    pallas_call x12, Pallas kernels, call(): pl.pallas_call(kernel, in_specs=[SM] * len(scalars) + [VM] * len(arrays),...  18.4 us
  transfers between devices with their start and end apart: 21, of which 13 were waited for; matrix products, arithmetic and copies ran while one was open for 1% of the time, Pallas kernels for 4%

profile of v3, /device:TPU:6, one launch (start us, length us, event | category | flops | bytes accessed | tf_op | source)
XLA Modules:
  0.0 189.1 jit_solution(6040048356101206280)
XLA Ops:
  1.2 8.2 %collective-permute-start = (f32[4,128,128]{2,1,0:T(8,128)S(1)}, f32[4,128,128]{2,1,0:T(8,128)S(1)}, u32[]{:S(2)}, u32[]{:S(2)}) collective-permute-start(f32[4,128,128]{2,1,0:T(8,128)S(1)} %slice.16), channel_id=1, source_target_pairs={{1,0},{2,1},{3,2},{4,3},{5,4},{6,5},{7,6},{8,7},{9,8},{10,9},{11,1... | collective-permute-start | bytes 786440 | tf_op jit(solution)/shard_map/ppermute | solution.py:351
  10.4 4.5 %collective-permute-done.right_top = f32[4,128,128]{2,1,0:T(8,128)S(1)} collective-permute-done((f32[4,128,128]{2,1,0:T(8,128)S(1)}, f32[4,128,128]{2,1,0:T(8,128)S(1)}, u32[]{:S(2)}, u32[]{:S(2)}) %collective-permute-start) | collective-permute-done | bytes 262176 | tf_op jit(solution)/shard_map/ppermute | solution.py:351
  17.4 6.5 %collective-permute-start.3 = (f32[2,384,128]{2,1,0:T(8,128)S(1)}, f32[2,384,128]{2,1,0:T(8,128)S(1)}, u32[]{:S(2)}, u32[]{:S(2)}) collective-permute-start(f32[2,384,128]{2,1,0:T(8,128)S(1)} %get-tuple-element.63), channel_id=1, source_target_pairs={{1,0},{2,1},{3,2},{4,3},{5,4},{6,5},{7,6},{8,7},{9,8},{10,9},{11,1... | collective-permute-start | bytes 1179656 | tf_op jit(solution)/shard_map/ppermute | solution.py:351
  23.9 1.9 %collective-permute-start.1 = (f32[2,384,128]{2,1,0:T(8,128)S(1)}, f32[2,384,128]{2,1,0:T(8,128)S(1)}, u32[]{:S(2)}, u32[]{:S(2)}) collective-permute-start(f32[2,384,128]{2,1,0:T(8,128)S(1)} %get-tuple-element.64), channel_id=1, source_target_pairs={{1,0},{2,1},{3,2},{4,3},{5,4},{6,5},{7,6},{8,7},{9,8},{10,9},{11,1... | collective-permute-start | bytes 1179656 | tf_op jit(solution)/shard_map/ppermute | solution.py:351
  26.5 4.2 %shard_map.100 = (f32[4,256,256]{2,1,0:T(8,128)S(1)}, f32[2,256,256]{2,1,0:T(8,128)S(1)}) custom-call(f32[1,1,4,256,256]{4,3,2,1,0:T(8,128)S(1)} %copy-done.3, f32[256,256]{1,0:T(8,128)S(1)} %copy-done.4, bf16[2,256,256]{2,1,0:T(8,128)(2,1)S(1)} %copy-done.5), custom_call_target="tpu_custom_call" | custom-call | tf_op jit(solution)/shard_map/pallas_call | solution.py:338
  30.8 2.5 %collective-permute-done.3.right_rest = f32[2,384,128]{2,1,0:T(8,128)S(1)} collective-permute-done((f32[2,384,128]{2,1,0:T(8,128)S(1)}, f32[2,384,128]{2,1,0:T(8,128)S(1)}, u32[]{:S(2)}, u32[]{:S(2)}) %collective-permute-start.3) | collective-permute-done | bytes 393248 | tf_op jit(solution)/shard_map/ppermute | solution.py:351
  34.1 7.6 %collective-permute-done.1.right_rest = f32[2,384,128]{2,1,0:T(8,128)S(1)} collective-permute-done((f32[2,384,128]{2,1,0:T(8,128)S(1)}, f32[2,384,128]{2,1,0:T(8,128)S(1)}, u32[]{:S(2)}, u32[]{:S(2)}) %collective-permute-start.1) | collective-permute-done | bytes 393248 | tf_op jit(solution)/shard_map/ppermute | solution.py:351
  42.9 1.9 %collective-permute-start.4 = (f32[4,256,128]{2,1,0:T(8,128)S(1)}, f32[4,256,128]{2,1,0:T(8,128)S(1)}, u32[]{:S(2)}, u32[]{:S(2)}) collective-permute-start(f32[4,256,128]{2,1,0:T(8,128)S(1)} %get-tuple-element.37), channel_id=1, source_target_pairs={{0,1},{1,2},{2,3},{3,4},{4,5},{5,6},{6,7},{7,8},{8,9},{9,10},{10,1... | collective-permute-start | bytes 1572872 | tf_op jit(solution)/shard_map/ppermute | solution.py:351
  44.8 9.9 %collective-permute-start.5 = (f32[4,256,128]{2,1,0:T(8,128)S(1)}, f32[4,256,128]{2,1,0:T(8,128)S(1)}, u32[]{:S(2)}, u32[]{:S(2)}) collective-permute-start(f32[4,256,128]{2,1,0:T(8,128)S(1)} %get-tuple-element.38), channel_id=1, source_target_pairs={{1,0},{2,1},{3,2},{4,3},{5,4},{6,5},{7,6},{8,7},{9,8},{10,9},{11,1... | collective-permute-start | bytes 1572872 | tf_op jit(solution)/shard_map/ppermute | solution.py:351
  54.7 1.9 %collective-permute-start.6 = (f32[4,384,128]{2,1,0:T(8,128)S(1)}, f32[4,384,128]{2,1,0:T(8,128)S(1)}, u32[]{:S(2)}, u32[]{:S(2)}) collective-permute-start(f32[4,384,128]{2,1,0:T(8,128)S(1)} %get-tuple-element.40), channel_id=1, source_target_pairs={{0,1},{1,2},{2,3},{3,4},{4,5},{5,6},{6,7},{7,8},{8,9},{9,10},{10,1... | collective-permute-start | bytes 2359304 | tf_op jit(solution)/shard_map/ppermute | solution.py:351
  56.6 6.0 %collective-permute-start.7 = (f32[4,384,128]{2,1,0:T(8,128)S(1)}, f32[4,384,128]{2,1,0:T(8,128)S(1)}, u32[]{:S(2)}, u32[]{:S(2)}) collective-permute-start(f32[4,384,128]{2,1,0:T(8,128)S(1)} %get-tuple-element.41), channel_id=1, source_target_pairs={{1,0},{2,1},{3,2},{4,3},{5,4},{6,5},{7,6},{8,7},{9,8},{10,9},{11,1... | collective-permute-start | bytes 2359304 | tf_op jit(solution)/shard_map/ppermute | solution.py:351
  62.7 1.7 collective-permute-done.5.end_r
  65.2 7.3 %collective-permute-start.8 = (f32[4,128,384]{2,1,0:T(8,128)S(1)}, f32[4,128,384]{2,1,0:T(8,128)S(1)}, u32[]{:S(2)}, u32[]{:S(2)}) collective-permute-start(f32[4,128,384]{2,1,0:T(8,128)S(1)} %get-tuple-element.42), channel_id=1, source_target_pairs={{0,32},{32,64},{64,96},{96,128},{128,160},{160,192},{192,224},{1,3... | collective-permute-start | bytes 2359304 | tf_op jit(solution)/shard_map/ppermute | solution.py:351
  74.0 5.5 %collective-permute-done.6.rest_0_ = f32[4,384,128]{2,1,0:T(8,128)S(1)} collective-permute-done((f32[4,384,128]{2,1,0:T(8,128)S(1)}, f32[4,384,128]{2,1,0:T(8,128)S(1)}, u32[]{:S(2)}, u32[]{:S(2)}) %collective-permute-start.6) | collective-permute-done | bytes 786464 | tf_op jit(solution)/shard_map/ppermute | solution.py:351
  79.5 1.7 collective-permute-done.7.rest_1_
  81.2 6.6 %shard_map.106 = (f32[4,640,384]{2,1,0:T(8,128)S(1)}, f32[4,640,384]{2,1,0:T(8,128)S(1)}, f32[4,384,128]{2,1,0:T(8,128)S(1)}, f32[4,384,128]{2,1,0:T(8,128)S(1)}...) custom-call(s32[1,1]{1,0:T(1,128)S(6)} %copy.23.count, ...), custom_call_target="tpu_custom_call", output_to_operand_aliasing={{0}: (8, {})} | custom-call | tf_op jit(solution)/shard_map/pallas_call | solution.py:338
  87.9 1.9 %collective-permute-start.10 = (f32[4,256,128]{2,1,0:T(8,128)S(1)}, f32[4,256,128]{2,1,0:T(8,128)S(1)}, u32[]{:S(2)}, u32[]{:S(2)}) collective-permute-start(f32[4,256,128]{2,1,0:T(8,128)S(1)} %get-tuple-element.46), channel_id=1, source_target_pairs={{0,1},{1,2},{2,3},{3,4},{4,5},{5,6},{6,7},{7,8},{8,9},{9,10},{10,1... | collective-permute-start | bytes 1572872 | tf_op jit(solution)/shard_map/ppermute | solution.py:351
  89.8 6.5 %collective-permute-start.11 = (f32[4,256,128]{2,1,0:T(8,128)S(1)}, f32[4,256,128]{2,1,0:T(8,128)S(1)}, u32[]{:S(2)}, u32[]{:S(2)}) collective-permute-start(f32[4,256,128]{2,1,0:T(8,128)S(1)} %get-tuple-element.47), channel_id=1, source_target_pairs={{1,0},{2,1},{3,2},{4,3},{5,4},{6,5},{7,6},{8,7},{9,8},{10,9},{11,1... | collective-permute-start | bytes 1572872 | tf_op jit(solution)/shard_map/ppermute | solution.py:351
  96.3 1.9 %collective-permute-start.12 = (f32[4,384,128]{2,1,0:T(8,128)S(1)}, f32[4,384,128]{2,1,0:T(8,128)S(1)}, u32[]{:S(2)}, u32[]{:S(2)}) collective-permute-start(f32[4,384,128]{2,1,0:T(8,128)S(1)} %get-tuple-element.49), channel_id=1, source_target_pairs={{0,1},{1,2},{2,3},{3,4},{4,5},{5,6},{6,7},{7,8},{8,9},{9,10},{10,1... | collective-permute-start | bytes 2359304 | tf_op jit(solution)/shard_map/ppermute | solution.py:351
  98.2 6.0 %collective-permute-start.13 = (f32[4,384,128]{2,1,0:T(8,128)S(1)}, f32[4,384,128]{2,1,0:T(8,128)S(1)}, u32[]{:S(2)}, u32[]{:S(2)}) collective-permute-start(f32[4,384,128]{2,1,0:T(8,128)S(1)} %get-tuple-element.50), channel_id=1, source_target_pairs={{1,0},{2,1},{3,2},{4,3},{5,4},{6,5},{7,6},{8,7},{9,8},{10,9},{11,1... | collective-permute-start | bytes 2359304 | tf_op jit(solution)/shard_map/ppermute | solution.py:351
  104.3 2.3 %collective-permute-done.10.end_l = f32[4,256,128]{2,1,0:T(8,128)S(1)} collective-permute-done((f32[4,256,128]{2,1,0:T(8,128)S(1)}, f32[4,256,128]{2,1,0:T(8,128)S(1)}, u32[]{:S(2)}, u32[]{:S(2)}) %collective-permute-start.10) | collective-permute-done | bytes 524320 | tf_op jit(solution)/shard_map/ppermute | solution.py:351
  111.2 11.7 %collective-permute-done.12.rest_0_ = f32[4,384,128]{2,1,0:T(8,128)S(1)} collective-permute-done((f32[4,384,128]{2,1,0:T(8,128)S(1)}, f32[4,384,128]{2,1,0:T(8,128)S(1)}, u32[]{:S(2)}, u32[]{:S(2)}) %collective-permute-start.12) | collective-permute-done | bytes 786464 | tf_op jit(solution)/shard_map/ppermute | solution.py:351
  124.1 1.6 shard_map.108
  126.4 30.2 %collective-permute-start.16 = (f32[4,128,128]{2,1,0:T(8,128)S(1)}, f32[4,128,128]{2,1,0:T(8,128)S(1)}, u32[]{:S(2)}, u32[]{:S(2)}) collective-permute-start(f32[4,128,128]{2,1,0:T(8,128)S(1)} %get-tuple-element.57), channel_id=1, source_target_pairs={{0,32},{32,64},{64,96},{96,128},{128,160},{160,192},{192,224},{1,3... | collective-permute-start | bytes 786440 | tf_op jit(solution)/shard_map/ppermute | solution.py:351
  156.6 1.9 %collective-permute-start.20 = (f32[4,128,256]{2,1,0:T(8,128)S(1)}, f32[4,128,256]{2,1,0:T(8,128)S(1)}, u32[]{:S(2)}, u32[]{:S(2)}) collective-permute-start(f32[4,128,256]{2,1,0:T(8,128)S(1)} %get-tuple-element.62), channel_id=1, source_target_pairs={{0,32},{32,64},{64,96},{96,128},{128,160},{160,192},{192,224},{1,3... | collective-permute-start | bytes 1572872 | tf_op jit(solution)/shard_map/ppermute | solution.py:351
  158.5 1.9 %collective-permute-start.18 = (f32[2,384,128]{2,1,0:T(8,128)S(1)}, f32[2,384,128]{2,1,0:T(8,128)S(1)}, u32[]{:S(2)}, u32[]{:S(2)}) collective-permute-start(f32[2,384,128]{2,1,0:T(8,128)S(1)} %get-tuple-element.60), channel_id=1, source_target_pairs={{0,1},{1,2},{2,3},{3,4},{4,5},{5,6},{6,7},{7,8},{8,9},{9,10},{10,1... | collective-permute-start | bytes 1179656 | tf_op jit(solution)/shard_map/ppermute | solution.py:351
  160.5 1.9 %collective-permute-start.17 = (f32[2,384,128]{2,1,0:T(8,128)S(1)}, f32[2,384,128]{2,1,0:T(8,128)S(1)}, u32[]{:S(2)}, u32[]{:S(2)}) collective-permute-start(f32[2,384,128]{2,1,0:T(8,128)S(1)} %get-tuple-element.59), channel_id=1, source_target_pairs={{0,1},{1,2},{2,3},{3,4},{4,5},{5,6},{6,7},{7,8},{8,9},{9,10},{10,1... | collective-permute-start | bytes 1179656 | tf_op jit(solution)/shard_map/ppermute | solution.py:351
  162.7 1.9 %collective-permute-start.19 = (f32[4,128,128]{2,1,0:T(8,128)S(1)}, f32[4,128,128]{2,1,0:T(8,128)S(1)}, u32[]{:S(2)}, u32[]{:S(2)}) collective-permute-start(f32[4,128,128]{2,1,0:T(8,128)S(1)} %get-tuple-element.61), channel_id=1, source_target_pairs={{0,1},{1,2},{2,3},{3,4},{4,5},{5,6},{6,7},{7,8},{8,9},{9,10},{10,1... | collective-permute-start | bytes 786440 | tf_op jit(solution)/shard_map/ppermute | solution.py:351
  164.6 9.9 %collective-permute-done.18.mid2 = f32[2,384,128]{2,1,0:T(8,128)S(1)} collective-permute-done((f32[2,384,128]{2,1,0:T(8,128)S(1)}, f32[2,384,128]{2,1,0:T(8,128)S(1)}, u32[]{:S(2)}, u32[]{:S(2)}) %collective-permute-start.18) | collective-permute-done | bytes 393248 | tf_op jit(solution)/shard_map/ppermute | solution.py:351
  174.5 8.4 %collective-permute-done.17.mid1 = f32[2,384,128]{2,1,0:T(8,128)S(1)} collective-permute-done((f32[2,384,128]{2,1,0:T(8,128)S(1)}, f32[2,384,128]{2,1,0:T(8,128)S(1)}, u32[]{:S(2)}, u32[]{:S(2)}) %collective-permute-start.17) | collective-permute-done | bytes 393248 | tf_op jit(solution)/shard_map/ppermute | solution.py:351
  183.0 4.6 %collective-permute-done.19.end = f32[4,128,128]{2,1,0:T(8,128)S(1)} collective-permute-done((f32[4,128,128]{2,1,0:T(8,128)S(1)}, f32[4,128,128]{2,1,0:T(8,128)S(1)}, u32[]{:S(2)}, u32[]{:S(2)}) %collective-permute-start.19) | collective-permute-done | bytes 262176 | tf_op jit(solution)/shard_map/ppermute | solution.py:351
  187.6 1.5 shard_map.111
  (44 shorter events, 15.8 us)
Async XLA Ops:
  0.0 26.5 %copy-start.5 = (bf16[2,256,256]{2,1,0:T(8,128)(2,1)S(1)}, bf16[2,256,256]{2,1,0:T(8,128)(2,1)}, u32[]{:S(2)}) copy-start(bf16[2,256,256]{2,1,0:T(8,128)(2,1)} %constant.5.clone.order) | copy-start | bytes 786436
  0.0 33.3 %copy-start.1 = (f32[2,2,512,256]{3,2,1,0:T(8,128)S(1)}, f32[2,2,512,256]{3,2,1,0:T(8,128)}, u32[]{:S(2)}) copy-start(f32[2,2,512,256]{3,2,1,0:T(8,128)} %main.3) | copy-start | bytes 6291460
  0.0 26.5 %copy-start.3 = (f32[1,1,4,256,256]{4,3,2,1,0:T(8,128)S(1)}, f32[1,1,4,256,256]{4,3,2,1,0:T(8,128)}, u32[]{:S(2)}) copy-start(f32[1,1,4,256,256]{4,3,2,1,0:T(8,128)} %amp.1) | copy-start | bytes 3145732
  0.0 26.5 %copy-start.4 = (f32[256,256]{1,0:T(8,128)S(1)}, f32[256,256]{1,0:T(8,128)}, u32[]{:S(2)}) copy-start(f32[256,256]{1,0:T(8,128)} %phase.1) | copy-start | bytes 786436
  1.2 13.7 %collective-permute-start = (f32[4,128,128]{2,1,0:T(8,128)S(1)}, f32[4,128,128]{2,1,0:T(8,128)S(1)}, u32[]{:S(2)}, u32[]{:S(2)}) collective-permute-start(f32[4,128,128]{2,1,0:T(8,128)S(1)} %slice.16), channel_id=1, source_target_pairs={{1,0},{2,1},{3,2},{4,3},{5,4},{6,5},{7,6},{8,7},{9,8},{10,9},{11,1... | collective-permute-start | bytes 786440 | tf_op jit(solution)/shard_map/ppermute | solution.py:351
  14.9 18.3 %collective-permute-start.2 = (f32[4,128,384]{2,1,0:T(8,128)S(1)}, f32[4,128,384]{2,1,0:T(8,128)S(1)}, u32[]{:S(2)}, u32[]{:S(2)}) collective-permute-start(f32[4,128,384]{2,1,0:T(8,128)S(1)} %pad_maximum_fusion), channel_id=1, source_target_pairs={{32,0},{64,32},{96,64},{128,96},{160,128},{192,160},{224,192},{33,... | collective-permute-start | bytes 2359304 | tf_op jit(solution)/shard_map/ppermute | solution.py:351
  17.4 15.8 %collective-permute-start.3 = (f32[2,384,128]{2,1,0:T(8,128)S(1)}, f32[2,384,128]{2,1,0:T(8,128)S(1)}, u32[]{:S(2)}, u32[]{:S(2)}) collective-permute-start(f32[2,384,128]{2,1,0:T(8,128)S(1)} %get-tuple-element.63), channel_id=1, source_target_pairs={{1,0},{2,1},{3,2},{4,3},{5,4},{6,5},{7,6},{8,7},{9,8},{10,9},{11,1... | collective-permute-start | bytes 1179656 | tf_op jit(solution)/shard_map/ppermute | solution.py:351
  23.9 17.8 %collective-permute-start.1 = (f32[2,384,128]{2,1,0:T(8,128)S(1)}, f32[2,384,128]{2,1,0:T(8,128)S(1)}, u32[]{:S(2)}, u32[]{:S(2)}) collective-permute-start(f32[2,384,128]{2,1,0:T(8,128)S(1)} %get-tuple-element.64), channel_id=1, source_target_pairs={{1,0},{2,1},{3,2},{4,3},{5,4},{6,5},{7,6},{8,7},{9,8},{10,9},{11,1... | collective-permute-start | bytes 1179656 | tf_op jit(solution)/shard_map/ppermute | solution.py:351
  30.7 2.7 %copy-start = (bf16[2,2,2,256,256]{4,3,2,1,0:T(8,128)(2,1)S(1)}, bf16[2,2,2,256,256]{4,3,2,1,0:T(8,128)(2,1)}, u32[]{:S(2)}) copy-start(bf16[2,2,2,256,256]{4,3,2,1,0:T(8,128)(2,1)} %constant.4.clone.tab) | copy-start | bytes 3145732
  30.7 2.7 %copy-start.2 = (f32[2,256,256]{2,1,0:T(8,128)S(1)}, f32[2,256,256]{2,1,0:T(8,128)}, u32[]{:S(2)}) copy-start(f32[2,256,256]{2,1,0:T(8,128)} %probe.9) | copy-start | bytes 1572868
  30.7 2.7 %copy-start.6 = (s32[1,1,4]{2,1,0:T(1,128)S(1)}, s32[1,1,4]{2,1,0:T(1,128)}, u32[]{:S(2)}) copy-start(s32[1,1,4]{2,1,0:T(1,128)} %orow.9) | copy-start | bytes 52
  30.8 2.7 %copy-start.7 = (s32[1,1,4]{2,1,0:T(1,128)S(1)}, s32[1,1,4]{2,1,0:T(1,128)}, u32[]{:S(2)}) copy-start(s32[1,1,4]{2,1,0:T(1,128)} %ocol.9) | copy-start | bytes 52
  30.8 2.7 %copy-start.8 = (s32[1,1,4]{2,1,0:T(1,128)S(1)}, s32[1,1,4]{2,1,0:T(1,128)}, u32[]{:S(2)}) copy-start(s32[1,1,4]{2,1,0:T(1,128)} %wbatch.9) | copy-start | bytes 52
  42.9 19.8 %collective-permute-start.4 = (f32[4,256,128]{2,1,0:T(8,128)S(1)}, f32[4,256,128]{2,1,0:T(8,128)S(1)}, u32[]{:S(2)}, u32[]{:S(2)}) collective-permute-start(f32[4,256,128]{2,1,0:T(8,128)S(1)} %get-tuple-element.37), channel_id=1, source_target_pairs={{0,1},{1,2},{2,3},{3,4},{4,5},{5,6},{6,7},{7,8},{8,9},{9,10},{10,1... | collective-permute-start | bytes 1572872 | tf_op jit(solution)/shard_map/ppermute | solution.py:351
  44.8 19.6 %collective-permute-start.5 = (f32[4,256,128]{2,1,0:T(8,128)S(1)}, f32[4,256,128]{2,1,0:T(8,128)S(1)}, u32[]{:S(2)}, u32[]{:S(2)}) collective-permute-start(f32[4,256,128]{2,1,0:T(8,128)S(1)} %get-tuple-element.38), channel_id=1, source_target_pairs={{1,0},{2,1},{3,2},{4,3},{5,4},{6,5},{7,6},{8,7},{9,8},{10,9},{11,1... | collective-permute-start | bytes 1572872 | tf_op jit(solution)/shard_map/ppermute | solution.py:351
  54.7 24.8 %collective-permute-start.6 = (f32[4,384,128]{2,1,0:T(8,128)S(1)}, f32[4,384,128]{2,1,0:T(8,128)S(1)}, u32[]{:S(2)}, u32[]{:S(2)}) collective-permute-start(f32[4,384,128]{2,1,0:T(8,128)S(1)} %get-tuple-element.40), channel_id=1, source_target_pairs={{0,1},{1,2},{2,3},{3,4},{4,5},{5,6},{6,7},{7,8},{8,9},{9,10},{10,1... | collective-permute-start | bytes 2359304 | tf_op jit(solution)/shard_map/ppermute | solution.py:351
  56.6 24.6 %collective-permute-start.7 = (f32[4,384,128]{2,1,0:T(8,128)S(1)}, f32[4,384,128]{2,1,0:T(8,128)S(1)}, u32[]{:S(2)}, u32[]{:S(2)}) collective-permute-start(f32[4,384,128]{2,1,0:T(8,128)S(1)} %get-tuple-element.41), channel_id=1, source_target_pairs={{1,0},{2,1},{3,2},{4,3},{5,4},{6,5},{7,6},{8,7},{9,8},{10,9},{11,1... | collective-permute-start | bytes 2359304 | tf_op jit(solution)/shard_map/ppermute | solution.py:351
  65.2 16.0 %collective-permute-start.8 = (f32[4,128,384]{2,1,0:T(8,128)S(1)}, f32[4,128,384]{2,1,0:T(8,128)S(1)}, u32[]{:S(2)}, u32[]{:S(2)}) collective-permute-start(f32[4,128,384]{2,1,0:T(8,128)S(1)} %get-tuple-element.42), channel_id=1, source_target_pairs={{0,32},{32,64},{64,96},{96,128},{128,160},{160,192},{192,224},{1,3... | collective-permute-start | bytes 2359304 | tf_op jit(solution)/shard_map/ppermute | solution.py:351
  72.5 8.7 %collective-permute-start.9 = (f32[4,128,384]{2,1,0:T(8,128)S(1)}, f32[4,128,384]{2,1,0:T(8,128)S(1)}, u32[]{:S(2)}, u32[]{:S(2)}) collective-permute-start(f32[4,128,384]{2,1,0:T(8,128)S(1)} %get-tuple-element.43), channel_id=1, source_target_pairs={{32,0},{64,32},{96,64},{128,96},{160,128},{192,160},{224,192},{33,... | collective-permute-start | bytes 2359304 | tf_op jit(solution)/shard_map/ppermute | solution.py:351
  87.9 18.7 %collective-permute-start.10 = (f32[4,256,128]{2,1,0:T(8,128)S(1)}, f32[4,256,128]{2,1,0:T(8,128)S(1)}, u32[]{:S(2)}, u32[]{:S(2)}) collective-permute-start(f32[4,256,128]{2,1,0:T(8,128)S(1)} %get-tuple-element.46), channel_id=1, source_target_pairs={{0,1},{1,2},{2,3},{3,4},{4,5},{5,6},{6,7},{7,8},{8,9},{9,10},{10,1... | collective-permute-start | bytes 1572872 | tf_op jit(solution)/shard_map/ppermute | solution.py:351
  89.8 18.0 %collective-permute-start.11 = (f32[4,256,128]{2,1,0:T(8,128)S(1)}, f32[4,256,128]{2,1,0:T(8,128)S(1)}, u32[]{:S(2)}, u32[]{:S(2)}) collective-permute-start(f32[4,256,128]{2,1,0:T(8,128)S(1)} %get-tuple-element.47), channel_id=1, source_target_pairs={{1,0},{2,1},{3,2},{4,3},{5,4},{6,5},{7,6},{8,7},{9,8},{10,9},{11,1... | collective-permute-start | bytes 1572872 | tf_op jit(solution)/shard_map/ppermute | solution.py:351
  96.3 26.6 %collective-permute-start.12 = (f32[4,384,128]{2,1,0:T(8,128)S(1)}, f32[4,384,128]{2,1,0:T(8,128)S(1)}, u32[]{:S(2)}, u32[]{:S(2)}) collective-permute-start(f32[4,384,128]{2,1,0:T(8,128)S(1)} %get-tuple-element.49), channel_id=1, source_target_pairs={{0,1},{1,2},{2,3},{3,4},{4,5},{5,6},{6,7},{7,8},{8,9},{9,10},{10,1... | collective-permute-start | bytes 2359304 | tf_op jit(solution)/shard_map/ppermute | solution.py:351
  98.2 25.9 %collective-permute-start.13 = (f32[4,384,128]{2,1,0:T(8,128)S(1)}, f32[4,384,128]{2,1,0:T(8,128)S(1)}, u32[]{:S(2)}, u32[]{:S(2)}) collective-permute-start(f32[4,384,128]{2,1,0:T(8,128)S(1)} %get-tuple-element.50), channel_id=1, source_target_pairs={{1,0},{2,1},{3,2},{4,3},{5,4},{6,5},{7,6},{8,7},{9,8},{10,9},{11,1... | collective-permute-start | bytes 2359304 | tf_op jit(solution)/shard_map/ppermute | solution.py:351
  108.6 15.5 %collective-permute-start.14 = (f32[4,128,384]{2,1,0:T(8,128)S(1)}, f32[4,128,384]{2,1,0:T(8,128)S(1)}, u32[]{:S(2)}, u32[]{:S(2)}) collective-permute-start(f32[4,128,384]{2,1,0:T(8,128)S(1)} %get-tuple-element.51), channel_id=1, source_target_pairs={{0,32},{32,64},{64,96},{96,128},{128,160},{160,192},{192,224},{1,3... | collective-permute-start | bytes 2359304 | tf_op jit(solution)/shard_map/ppermute | solution.py:351
  109.9 14.2 %collective-permute-start.15 = (f32[4,128,384]{2,1,0:T(8,128)S(1)}, f32[4,128,384]{2,1,0:T(8,128)S(1)}, u32[]{:S(2)}, u32[]{:S(2)}) collective-permute-start(f32[4,128,384]{2,1,0:T(8,128)S(1)} %get-tuple-element.52), channel_id=1, source_target_pairs={{32,0},{64,32},{96,64},{128,96},{160,128},{192,160},{224,192},{33,... | collective-permute-start | bytes 2359304 | tf_op jit(solution)/shard_map/ppermute | solution.py:351
  126.4 36.0 %collective-permute-start.16 = (f32[4,128,128]{2,1,0:T(8,128)S(1)}, f32[4,128,128]{2,1,0:T(8,128)S(1)}, u32[]{:S(2)}, u32[]{:S(2)}) collective-permute-start(f32[4,128,128]{2,1,0:T(8,128)S(1)} %get-tuple-element.57), channel_id=1, source_target_pairs={{0,32},{32,64},{64,96},{96,128},{128,160},{160,192},{192,224},{1,3... | collective-permute-start | bytes 786440 | tf_op jit(solution)/shard_map/ppermute | solution.py:351
  156.6 26.4 %collective-permute-start.20 = (f32[4,128,256]{2,1,0:T(8,128)S(1)}, f32[4,128,256]{2,1,0:T(8,128)S(1)}, u32[]{:S(2)}, u32[]{:S(2)}) collective-permute-start(f32[4,128,256]{2,1,0:T(8,128)S(1)} %get-tuple-element.62), channel_id=1, source_target_pairs={{0,32},{32,64},{64,96},{96,128},{128,160},{160,192},{192,224},{1,3... | collective-permute-start | bytes 1572872 | tf_op jit(solution)/shard_map/ppermute | solution.py:351
  158.5 16.0 %collective-permute-start.18 = (f32[2,384,128]{2,1,0:T(8,128)S(1)}, f32[2,384,128]{2,1,0:T(8,128)S(1)}, u32[]{:S(2)}, u32[]{:S(2)}) collective-permute-start(f32[2,384,128]{2,1,0:T(8,128)S(1)} %get-tuple-element.60), channel_id=1, source_target_pairs={{0,1},{1,2},{2,3},{3,4},{4,5},{5,6},{6,7},{7,8},{8,9},{9,10},{10,1... | collective-permute-start | bytes 1179656 | tf_op jit(solution)/shard_map/ppermute | solution.py:351
  160.5 22.5 %collective-permute-start.17 = (f32[2,384,128]{2,1,0:T(8,128)S(1)}, f32[2,384,128]{2,1,0:T(8,128)S(1)}, u32[]{:S(2)}, u32[]{:S(2)}) collective-permute-start(f32[2,384,128]{2,1,0:T(8,128)S(1)} %get-tuple-element.59), channel_id=1, source_target_pairs={{0,1},{1,2},{2,3},{3,4},{4,5},{5,6},{6,7},{7,8},{8,9},{9,10},{10,1... | collective-permute-start | bytes 1179656 | tf_op jit(solution)/shard_map/ppermute | solution.py:351
  162.7 24.9 %collective-permute-start.19 = (f32[4,128,128]{2,1,0:T(8,128)S(1)}, f32[4,128,128]{2,1,0:T(8,128)S(1)}, u32[]{:S(2)}, u32[]{:S(2)}) collective-permute-start(f32[4,128,128]{2,1,0:T(8,128)S(1)} %get-tuple-element.61), channel_id=1, source_target_pairs={{0,1},{1,2},{2,3},{3,4},{4,5},{5,6},{6,7},{7,8},{8,9},{9,10},{10,1... | collective-permute-start | bytes 786440 | tf_op jit(solution)/shard_map/ppermute | solution.py:351

commit v4 on v3

--- a/solution.py
+++ b/solution.py
@@ -37,11 +37,18 @@
     return np.stack(out).reshape(2, 2, 2, WIN, WIN)
 
 
-def order_matrix():
-    source = np.concatenate([np.arange(0, WIN, 2), np.arange(1, WIN, 2)])
-    m = np.zeros((WIN, WIN), np.float32)
-    m[source, np.arange(WIN)] = 1.0
-    return np.stack([m, m.T]).astype(bf16)
+def order_matrices():
+    rows = lax.broadcasted_iota(jnp.int32, (WIN, WIN), 0)
+    cols = lax.broadcasted_iota(jnp.int32, (WIN, WIN), 1)
+
+    def source(k):
+        return jnp.where(k < HALF, 2 * k, 2 * k - (WIN - 1))
+
+    one, none = jnp.float32(1.0), jnp.float32(0.0)
+    return [
+        jnp.where(rows == source(cols), one, none).astype(bf16),
+        jnp.where(cols == source(rows), one, none).astype(bf16),
+    ]
 
 
 def halves(x):
@@ -50,18 +57,26 @@
     return hi, lo
 
 
+PAIRED = [b for i in range(8) for b in (i, i + 8)]
+NATURAL = [PAIRED.index(b) for b in range(16)]
+
+
+def blocks(x, order):
+    return cc([x[16 * b : 16 * b + 16] for b in order], 0)
+
+
 def dot_r(x, tab, which, trans):
-    hi, lo = halves(x)
+    hi, lo = halves(blocks(x, PAIRED))
     th = tab[which, trans, 0]
     t = cc([th, th, tab[which, trans, 1]], 0)
-    return jnp.dot(cc([hi, lo, hi], 1), t, preferred_element_type=f32)
+    return blocks(jnp.dot(cc([hi, lo, hi], 1), t, preferred_element_type=f32), NATURAL)
 
 
 def dot_l(tab, which, trans, x):
     hi, lo = halves(x)
     th = tab[which, trans, 0]
-    t = cc([th, th, tab[which, trans, 1]], 1)
-    return jnp.dot(t, cc([hi, lo, hi], 0), preferred_element_type=f32)
+    t = blocks(cc([th, th, tab[which, trans, 1]], 1), PAIRED)
+    return blocks(jnp.dot(t, cc([hi, lo, hi], 0), preferred_element_type=f32), NATURAL)
 
 
 def forward_two(z, tab):
@@ -166,7 +181,10 @@
     return y + jnp.dot(m, c, preferred_element_type=f32)
 
 
-def prep_kernel(amp, phase, order, amp_out, prop_out):
+def prep_kernel(amp, phase, amp_out, prop_out, grad):
+    grad[...] = jnp.zeros_like(grad)
+    order = order_matrices()
+
     def step(s, _):
         amp_out[s] = reorder(amp[0, 0, s], order)
         return 0
@@ -253,17 +271,15 @@
     windows(0, "a", count, orow, ocol, wbatch, tab, probe, prop, None, state, None, between, None)
 
 
-def first_kernel(count, orow, ocol, wbatch, tab, probe, prop, amp, state, between, grad, *out):
-    grad[...] = jnp.zeros_like(grad)
+def first_kernel(count, orow, ocol, wbatch, tab, probe, prop, amp, state, between, _, grad, *out):
     windows(0, "bc", count, orow, ocol, wbatch, tab, probe, prop, amp, state, grad, between, None)
     edges_of(grad, *out)
 
 
 def batch_kernel(batch):
     def run(count, orow, ocol, wbatch, tab, probe, prop, amp, old, *rest):
-        sides, (state, grad), out = rest[:4], rest[4:6], rest[6:]
+        sides, (state, grad), out = rest[1:5], rest[5:7], rest[7:]
         fold_sides(old, state, *sides)
-        grad[...] = jnp.zeros_like(grad)
         windows(batch, "abc", count, orow, ocol, wbatch, tab, probe, prop, amp, state, grad, None, None)
         edges_of(grad, *out)
 
@@ -271,9 +287,8 @@
 
 
 def final_kernel(count, orow, ocol, wbatch, tab, probe, prop, amp, old, *rest):
-    sides, (state, grad, mid, side_r) = rest[:4], rest[4:]
+    sides, (state, grad, mid, side_r) = rest[1:5], rest[5:]
     fold_sides(old, state, *sides)
-    grad[...] = jnp.zeros_like(grad)
     windows(BATCHES - 1, "ab", count, orow, ocol, wbatch, tab, probe, prop, amp, state, grad, None, mid)
     side_r[...] = grad[2:, HALF:ROWS, COLS:]
 
@@ -285,24 +300,31 @@
     low[...] = grad[:, ROWS:, :COLS]
 
 
-def settle_kernel(state, grad, end_l, end_r, out, top, bottom):
+def flat_kernel(grad, end_l, end_r, top, bottom):
+    h = HALF
+    for at, flat, ends in ((0, top, pl.ds(0, h)), (ROWS, bottom, pl.ds(h, h))):
+        rows = pl.ds(at, h)
+        flat[:, :, :h] = grad[:, rows, :h] + end_l[:, ends]
+        flat[:, :, h:COLS] = grad[:, rows, h:COLS]
+        flat[:, :, COLS:] = grad[:, rows, COLS:] + end_r[:, ends]
+
+
+def settle_kernel(state, grad, end_l, end_r, out, blank):
     in_r = jnp.where(inside("row"), 0.5, 0.0).astype(f32)
     in_c = jnp.where(inside("col"), 1.0, 0.0).astype(f32)
     h = HALF
     for p in range(4):
-        for at, flat, ends in ((0, top, pl.ds(0, h)), (h, None, None), (ROWS, bottom, pl.ds(h, h))):
-            rows = pl.ds(at, ROWS - h if flat is None else h)
+        for at, ends in ((0, pl.ds(0, h)), (h, None), (ROWS, pl.ds(h, h))):
+            rows = pl.ds(at, ROWS - h if ends is None else h)
             left, mid, right = grad[p, rows, :h], grad[p, rows, h:COLS], grad[p, rows, COLS:]
-            if flat is not None:
+            if ends is not None:
                 left = left + end_l[p, ends]
                 right = right + end_r[p, ends]
-                flat[p, :, :h] = left
-                flat[p, :, h:COLS] = mid
-                flat[p, :, COLS:] = right
             scale = in_r if at == ROWS else jnp.float32(0.5)
             out[p, rows, :h] = state[p, rows, :h] - scale * left
             out[p, rows, h:COLS] = state[p, rows, h:COLS] - scale * mid
             out[p, rows, COLS:] = state[p, rows, COLS:] - (scale * in_c) * right
+            blank[p, rows, :] = jnp.zeros((left.shape[0], EXT_C), f32)
 
 
 def final_settle_kernel(state, grad, corner, out, end_r):
@@ -353,14 +375,15 @@
 
 def body(transmission, probe, phase, amplitude, count, orow, ocol, wbatch):
     tab = jnp.asarray(dft_tables())
-    order = jnp.asarray(order_matrix())
     scalars = (count, orow, ocol, wbatch)
     h = HALF
     planes = transmission.reshape(4, ROWS, COLS)
     right_top = from_behind(planes[:, :h, :h], "col", -1)
     right_1 = from_behind(planes[:2, h:, :h], "col", -1)
     right_2 = from_behind(planes[2:, h:, :h], "col", -1)
-    amp, prop = call(prep_kernel, (), (amplitude, phase, order), [(SLOTS, WIN, WIN), (2, WIN, WIN)])
+    amp, prop, grad = call(
+        prep_kernel, (), (amplitude, phase), [(SLOTS, WIN, WIN), (2, WIN, WIN), EXT]
+    )
     low = cc([planes[:, :h, :], right_top], 2)
     bottom = from_behind(low, "row", -1)
     (state,) = call(assemble_kernel, (), (transmission, right_top, right_1, bottom), [EXT])
@@ -372,26 +395,31 @@
     for b in range(BATCHES - 1):
         common = (tab, probe, prop, amp, state)
         if b == 0:
-            grad, *sent = call(first_kernel, scalars, (*common, between), [EXT, *edges])
+            grad, *sent = call(
+                first_kernel, scalars, (*common, between, grad), [EXT, *edges], {10: 0}
+            )
         else:
             state, grad, *sent = call(
-                batch_kernel(b), scalars, (*common, *parts), [EXT, EXT, *edges], {8: 0}
+                batch_kernel(b), scalars, (*common, grad, *parts), [EXT, EXT, *edges], {8: 0, 9: 1}
             )
         mid_l, mid_r, end_l, end_r = sent
         from_left = from_behind(end_r, "col", 1)
         from_right = from_behind(end_l, "col", -1)
         mid_left = from_behind(mid_r, "col", 1)
         mid_right = from_behind(mid_l, "col", -1)
-        state, top, bottom = call(
-            settle_kernel, (), (state, grad, from_left, from_right), [EXT, FLAT, FLAT], {0: 0}
+        top, bottom = call(flat_kernel, (), (grad, from_left, from_right), [FLAT, FLAT])
+        above = from_behind(bottom, "row", 1)
+        below = from_behind(top, "row", -1)
+        state, grad = call(
+            settle_kernel, (), (state, grad, from_left, from_right), [EXT, EXT], {0: 0, 1: 1}
         )
-        parts = (mid_left, mid_right, from_behind(bottom, "row", 1), from_behind(top, "row", -1))
+        parts = (mid_left, mid_right, above, below)
     state, grad, mid, side_2 = call(
         final_kernel,
         scalars,
-        (tab, probe, prop, amp, state, *parts),
+        (tab, probe, prop, amp, state, grad, *parts),
         [EXT, EXT, PLANES, SIDE],
-        {8: 0},
+        {8: 0, 9: 1},
     )
     mid_2 = from_behind(side_2, "col", 1)
     grad, side_1, corner, low = call(

time: 190 us -> 186 us (0.979)
  waiting for transfers between devices: 62.9 us -> 59 us
  Pallas kernels: 18.4 us -> 20.7 us
  starting transfers between devices: 103 us -> 101 us
    ppermute x21, waiting for transfers between devices: 62.9 us -> 59 us  [from_behind(): return lax.ppermute(array, axis, pairs)]
    ppermute x21, starting transfers between devices: 103 us -> 101 us  [from_behind(): return lax.ppermute(array, axis, pairs)]
    pallas_call x12 -> x14, Pallas kernels: 18.4 us -> 20.7 us  [call(): pl.pallas_call(kernel, in_specs=[SM] * len(scalars) + [VM] * len(arrays),...]
  transfers between devices with their start and end apart: 21 -> 21, of which waited for: 13 -> 14; matrix products, arithmetic and copies ran while one was open for 1% -> 1% of each run, Pallas kernels for 4% -> 5%
where the time goes in v4:
time: 186 us; the launch traced here: 185 us
  starting transfers between devices  101 us (54%)
  waiting for transfers between devices  59 us (32%)
  Pallas kernels  20.7 us (11%)
  local copies, waits for them, and re-layouts  3.45 us (2%)
    ppermute x21, starting transfers between devices, from_behind(): return lax.ppermute(array, axis, pairs)  101 us
    ppermute x21, waiting for transfers between devices, from_behind(): return lax.ppermute(array, axis, pairs)  59 us
    pallas_call x14, Pallas kernels, call(): pl.pallas_call(kernel, in_specs=[SM] * len(scalars) + [VM] * len(arrays),...  20.7 us
  transfers between devices with their start and end apart: 21, of which 14 were waited for; matrix products, arithmetic and copies ran while one was open for 1% of the time, Pallas kernels for 5%

profile of v4, /device:TPU:6, one launch (start us, length us, event | category | flops | bytes accessed | tf_op | source)
XLA Modules:
  0.0 185.3 jit_solution(14845205512422624620)
XLA Ops:
  1.1 8.0 %collective-permute-start = (f32[4,128,128]{2,1,0:T(8,128)S(1)}, f32[4,128,128]{2,1,0:T(8,128)S(1)}, u32[]{:S(2)}, u32[]{:S(2)}) collective-permute-start(f32[4,128,128]{2,1,0:T(8,128)S(1)} %slice.16), channel_id=1, source_target_pairs={{1,0},{2,1},{3,2},{4,3},{5,4},{6,5},{7,6},{8,7},{9,8},{10,9},{11,1... | collective-permute-start | bytes 786440 | tf_op jit(solution)/shard_map/ppermute | solution.py:373
  10.3 4.5 %collective-permute-done.right_top = f32[4,128,128]{2,1,0:T(8,128)S(1)} collective-permute-done((f32[4,128,128]{2,1,0:T(8,128)S(1)}, f32[4,128,128]{2,1,0:T(8,128)S(1)}, u32[]{:S(2)}, u32[]{:S(2)}) %collective-permute-start) | collective-permute-done | bytes 262176 | tf_op jit(solution)/shard_map/ppermute | solution.py:373
  17.3 6.5 %collective-permute-start.3 = (f32[2,384,128]{2,1,0:T(8,128)S(1)}, f32[2,384,128]{2,1,0:T(8,128)S(1)}, u32[]{:S(2)}, u32[]{:S(2)}) collective-permute-start(f32[2,384,128]{2,1,0:T(8,128)S(1)} %get-tuple-element.69), channel_id=1, source_target_pairs={{1,0},{2,1},{3,2},{4,3},{5,4},{6,5},{7,6},{8,7},{9,8},{10,9},{11,1... | collective-permute-start | bytes 1179656 | tf_op jit(solution)/shard_map/ppermute | solution.py:373
  23.8 1.9 %collective-permute-start.1 = (f32[2,384,128]{2,1,0:T(8,128)S(1)}, f32[2,384,128]{2,1,0:T(8,128)S(1)}, u32[]{:S(2)}, u32[]{:S(2)}) collective-permute-start(f32[2,384,128]{2,1,0:T(8,128)S(1)} %get-tuple-element.70), channel_id=1, source_target_pairs={{1,0},{2,1},{3,2},{4,3},{5,4},{6,5},{7,6},{8,7},{9,8},{10,9},{11,1... | collective-permute-start | bytes 1179656 | tf_op jit(solution)/shard_map/ppermute | solution.py:373
  26.4 4.5 %shard_map.91 = (f32[4,256,256]{2,1,0:T(8,128)S(1)}, f32[2,256,256]{2,1,0:T(8,128)S(1)}, f32[4,640,384]{2,1,0:T(8,128)S(1)}) custom-call(f32[1,1,4,256,256]{4,3,2,1,0:T(8,128)S(1)} %copy-done.3, f32[256,256]{1,0:T(8,128)S(1)} %copy-done.4), custom_call_target="tpu_custom_call" | custom-call | tf_op jit(solution)/shard_map/pallas_call | solution.py:360
  31.0 2.1 %collective-permute-done.3.right_rest = f32[2,384,128]{2,1,0:T(8,128)S(1)} collective-permute-done((f32[2,384,128]{2,1,0:T(8,128)S(1)}, f32[2,384,128]{2,1,0:T(8,128)S(1)}, u32[]{:S(2)}, u32[]{:S(2)}) %collective-permute-start.3) | collective-permute-done | bytes 393248 | tf_op jit(solution)/shard_map/ppermute | solution.py:373
  33.9 7.6 %collective-permute-done.1.right_rest = f32[2,384,128]{2,1,0:T(8,128)S(1)} collective-permute-done((f32[2,384,128]{2,1,0:T(8,128)S(1)}, f32[2,384,128]{2,1,0:T(8,128)S(1)}, u32[]{:S(2)}, u32[]{:S(2)}) %collective-permute-start.1) | collective-permute-done | bytes 393248 | tf_op jit(solution)/shard_map/ppermute | solution.py:373
  42.5 1.9 %collective-permute-start.4 = (f32[4,256,128]{2,1,0:T(8,128)S(1)}, f32[4,256,128]{2,1,0:T(8,128)S(1)}, u32[]{:S(2)}, u32[]{:S(2)}) collective-permute-start(f32[4,256,128]{2,1,0:T(8,128)S(1)} %get-tuple-element.41), channel_id=1, source_target_pairs={{0,1},{1,2},{2,3},{3,4},{4,5},{5,6},{6,7},{7,8},{8,9},{9,10},{10,1... | collective-permute-start | bytes 1572872 | tf_op jit(solution)/shard_map/ppermute | solution.py:373
  44.4 9.8 %collective-permute-start.5 = (f32[4,256,128]{2,1,0:T(8,128)S(1)}, f32[4,256,128]{2,1,0:T(8,128)S(1)}, u32[]{:S(2)}, u32[]{:S(2)}) collective-permute-start(f32[4,256,128]{2,1,0:T(8,128)S(1)} %get-tuple-element.42), channel_id=1, source_target_pairs={{1,0},{2,1},{3,2},{4,3},{5,4},{6,5},{7,6},{8,7},{9,8},{10,9},{11,1... | collective-permute-start | bytes 1572872 | tf_op jit(solution)/shard_map/ppermute | solution.py:373
  54.2 1.9 %collective-permute-start.6 = (f32[4,384,128]{2,1,0:T(8,128)S(1)}, f32[4,384,128]{2,1,0:T(8,128)S(1)}, u32[]{:S(2)}, u32[]{:S(2)}) collective-permute-start(f32[4,384,128]{2,1,0:T(8,128)S(1)} %get-tuple-element.45), channel_id=1, source_target_pairs={{0,1},{1,2},{2,3},{3,4},{4,5},{5,6},{6,7},{7,8},{8,9},{9,10},{10,1... | collective-permute-start | bytes 2359304 | tf_op jit(solution)/shard_map/ppermute | solution.py:373
  56.1 6.0 %collective-permute-start.7 = (f32[4,384,128]{2,1,0:T(8,128)S(1)}, f32[4,384,128]{2,1,0:T(8,128)S(1)}, u32[]{:S(2)}, u32[]{:S(2)}) collective-permute-start(f32[4,384,128]{2,1,0:T(8,128)S(1)} %get-tuple-element.46), channel_id=1, source_target_pairs={{1,0},{2,1},{3,2},{4,3},{5,4},{6,5},{7,6},{8,7},{9,8},{10,9},{11,1... | collective-permute-start | bytes 2359304 | tf_op jit(solution)/shard_map/ppermute | solution.py:373
  62.2 1.7 collective-permute-done.5.end_r
  64.2 7.0 %collective-permute-start.8 = (f32[4,128,384]{2,1,0:T(8,128)S(1)}, f32[4,128,384]{2,1,0:T(8,128)S(1)}, u32[]{:S(2)}, u32[]{:S(2)}) collective-permute-start(f32[4,128,384]{2,1,0:T(8,128)S(1)} %get-tuple-element.47), channel_id=1, source_target_pairs={{0,32},{32,64},{64,96},{96,128},{128,160},{160,192},{192,224},{1,3... | collective-permute-start | bytes 2359304 | tf_op jit(solution)/shard_map/ppermute | solution.py:373
  72.7 2.2 %shard_map.96 = (f32[4,640,384]{2,1,0:T(8,128)S(1)}, f32[4,640,384]{2,1,0:T(8,128)S(1)}) custom-call(f32[4,640,384]{2,1,0:T(8,128)S(1)} %shard_map.93.state, f32[4,640,384]{2,1,0:T(8,128)S(1)} %get-tuple-element.40.grad, f32[4,256,128]{2,1,0:T(8,128)S(1)} %collective-permute-done.4.end_l, ...), custom_call_target="tpu_custom_call", output_to_operand_aliasing={{0}: (0, {}), {1}: (1, {})} | custom-call | tf_op jit(solution)/shard_map/pallas_call | solution.py:360
  74.8 4.3 %collective-permute-done.6.rest_1_ = f32[4,384,128]{2,1,0:T(8,128)S(1)} collective-permute-done((f32[4,384,128]{2,1,0:T(8,128)S(1)}, f32[4,384,128]{2,1,0:T(8,128)S(1)}, u32[]{:S(2)}, u32[]{:S(2)}) %collective-permute-start.6) | collective-permute-done | bytes 786464 | tf_op jit(solution)/shard_map/ppermute | solution.py:373
  79.1 1.7 collective-permute-done.7.rest_2_
  80.8 6.1 %shard_map.98 = (f32[4,640,384]{2,1,0:T(8,128)S(1)}, f32[4,640,384]{2,1,0:T(8,128)S(1)}, f32[4,384,128]{2,1,0:T(8,128)S(1)}, f32[4,384,128]{2,1,0:T(8,128)S(1)},...) custom-call(s32[1,1]{1,0:T(1,128)S(6)} %copy.32.count, ...), custom_call_target="tpu_custom_call", output_to_operand_aliasing={{0}: (8, {}), {1}: (9, {})} | custom-call | tf_op jit(solution)/shard_map/pallas_call | solution.py:360
  87.0 1.9 %collective-permute-start.10 = (f32[4,256,128]{2,1,0:T(8,128)S(1)}, f32[4,256,128]{2,1,0:T(8,128)S(1)}, u32[]{:S(2)}, u32[]{:S(2)}) collective-permute-start(f32[4,256,128]{2,1,0:T(8,128)S(1)} %get-tuple-element.51), channel_id=1, source_target_pairs={{0,1},{1,2},{2,3},{3,4},{4,5},{5,6},{6,7},{7,8},{8,9},{9,10},{10,1... | collective-permute-start | bytes 1572872 | tf_op jit(solution)/shard_map/ppermute | solution.py:373
  88.9 6.5 %collective-permute-start.11 = (f32[4,256,128]{2,1,0:T(8,128)S(1)}, f32[4,256,128]{2,1,0:T(8,128)S(1)}, u32[]{:S(2)}, u32[]{:S(2)}) collective-permute-start(f32[4,256,128]{2,1,0:T(8,128)S(1)} %get-tuple-element.52), channel_id=1, source_target_pairs={{1,0},{2,1},{3,2},{4,3},{5,4},{6,5},{7,6},{8,7},{9,8},{10,9},{11,1... | collective-permute-start | bytes 1572872 | tf_op jit(solution)/shard_map/ppermute | solution.py:373
  95.5 1.9 %collective-permute-start.12 = (f32[4,384,128]{2,1,0:T(8,128)S(1)}, f32[4,384,128]{2,1,0:T(8,128)S(1)}, u32[]{:S(2)}, u32[]{:S(2)}) collective-permute-start(f32[4,384,128]{2,1,0:T(8,128)S(1)} %get-tuple-element.55), channel_id=1, source_target_pairs={{0,1},{1,2},{2,3},{3,4},{4,5},{5,6},{6,7},{7,8},{8,9},{9,10},{10,1... | collective-permute-start | bytes 2359304 | tf_op jit(solution)/shard_map/ppermute | solution.py:373
  97.4 6.0 %collective-permute-start.13 = (f32[4,384,128]{2,1,0:T(8,128)S(1)}, f32[4,384,128]{2,1,0:T(8,128)S(1)}, u32[]{:S(2)}, u32[]{:S(2)}) collective-permute-start(f32[4,384,128]{2,1,0:T(8,128)S(1)} %get-tuple-element.56), channel_id=1, source_target_pairs={{1,0},{2,1},{3,2},{4,3},{5,4},{6,5},{7,6},{8,7},{9,8},{10,9},{11,1... | collective-permute-start | bytes 2359304 | tf_op jit(solution)/shard_map/ppermute | solution.py:373
  103.4 2.0 %collective-permute-done.10.end_l = f32[4,256,128]{2,1,0:T(8,128)S(1)} collective-permute-done((f32[4,256,128]{2,1,0:T(8,128)S(1)}, f32[4,256,128]{2,1,0:T(8,128)S(1)}, u32[]{:S(2)}, u32[]{:S(2)}) %collective-permute-start.10) | collective-permute-done | bytes 524320 | tf_op jit(solution)/shard_map/ppermute | solution.py:373
  109.6 2.2 %shard_map.99 = (f32[4,640,384]{2,1,0:T(8,128)S(1)}, f32[4,640,384]{2,1,0:T(8,128)S(1)}) custom-call(f32[4,640,384]{2,1,0:T(8,128)S(1)} %get-tuple-element.49.state, f32[4,640,384]{2,1,0:T(8,128)S(1)} %get-tuple-element.50.grad, f32[4,256,128]{2,1,0:T(8,128)S(1)} %collective-permute-done.10.end_l, ...), custom_call_target="tpu_custom_call", output_to_operand_aliasing={{0}: (0, {}), {1}: (1, {})} | custom-call | tf_op jit(solution)/shard_map/pallas_call | solution.py:360
  111.8 9.6 %collective-permute-done.12.rest_1_ = f32[4,384,128]{2,1,0:T(8,128)S(1)} collective-permute-done((f32[4,384,128]{2,1,0:T(8,128)S(1)}, f32[4,384,128]{2,1,0:T(8,128)S(1)}, u32[]{:S(2)}, u32[]{:S(2)}) %collective-permute-start.12) | collective-permute-done | bytes 786464 | tf_op jit(solution)/shard_map/ppermute | solution.py:373
  124.6 28.2 %collective-permute-start.16 = (f32[4,128,128]{2,1,0:T(8,128)S(1)}, f32[4,128,128]{2,1,0:T(8,128)S(1)}, u32[]{:S(2)}, u32[]{:S(2)}) collective-permute-start(f32[4,128,128]{2,1,0:T(8,128)S(1)} %get-tuple-element.63), channel_id=1, source_target_pairs={{0,32},{32,64},{64,96},{96,128},{128,160},{160,192},{192,224},{1,3... | collective-permute-start | bytes 786440 | tf_op jit(solution)/shard_map/ppermute | solution.py:373
  152.7 1.9 %collective-permute-start.20 = (f32[4,128,256]{2,1,0:T(8,128)S(1)}, f32[4,128,256]{2,1,0:T(8,128)S(1)}, u32[]{:S(2)}, u32[]{:S(2)}) collective-permute-start(f32[4,128,256]{2,1,0:T(8,128)S(1)} %get-tuple-element.68), channel_id=1, source_target_pairs={{0,32},{32,64},{64,96},{96,128},{128,160},{160,192},{192,224},{1,3... | collective-permute-start | bytes 1572872 | tf_op jit(solution)/shard_map/ppermute | solution.py:373
  154.7 1.9 %collective-permute-start.18 = (f32[2,384,128]{2,1,0:T(8,128)S(1)}, f32[2,384,128]{2,1,0:T(8,128)S(1)}, u32[]{:S(2)}, u32[]{:S(2)}) collective-permute-start(f32[2,384,128]{2,1,0:T(8,128)S(1)} %get-tuple-element.66), channel_id=1, source_target_pairs={{0,1},{1,2},{2,3},{3,4},{4,5},{5,6},{6,7},{7,8},{8,9},{9,10},{10,1... | collective-permute-start | bytes 1179656 | tf_op jit(solution)/shard_map/ppermute | solution.py:373
  156.6 1.9 %collective-permute-start.17 = (f32[2,384,128]{2,1,0:T(8,128)S(1)}, f32[2,384,128]{2,1,0:T(8,128)S(1)}, u32[]{:S(2)}, u32[]{:S(2)}) collective-permute-start(f32[2,384,128]{2,1,0:T(8,128)S(1)} %get-tuple-element.65), channel_id=1, source_target_pairs={{0,1},{1,2},{2,3},{3,4},{4,5},{5,6},{6,7},{7,8},{8,9},{9,10},{10,1... | collective-permute-start | bytes 1179656 | tf_op jit(solution)/shard_map/ppermute | solution.py:373
  158.8 1.9 %collective-permute-start.19 = (f32[4,128,128]{2,1,0:T(8,128)S(1)}, f32[4,128,128]{2,1,0:T(8,128)S(1)}, u32[]{:S(2)}, u32[]{:S(2)}) collective-permute-start(f32[4,128,128]{2,1,0:T(8,128)S(1)} %get-tuple-element.67), channel_id=1, source_target_pairs={{0,1},{1,2},{2,3},{3,4},{4,5},{5,6},{6,7},{7,8},{8,9},{9,10},{10,1... | collective-permute-start | bytes 786440 | tf_op jit(solution)/shard_map/ppermute | solution.py:373
  160.7 9.9 %collective-permute-done.18.mid2 = f32[2,384,128]{2,1,0:T(8,128)S(1)} collective-permute-done((f32[2,384,128]{2,1,0:T(8,128)S(1)}, f32[2,384,128]{2,1,0:T(8,128)S(1)}, u32[]{:S(2)}, u32[]{:S(2)}) %collective-permute-start.18) | collective-permute-done | bytes 393248 | tf_op jit(solution)/shard_map/ppermute | solution.py:373
  170.7 8.4 %collective-permute-done.17.mid1 = f32[2,384,128]{2,1,0:T(8,128)S(1)} collective-permute-done((f32[2,384,128]{2,1,0:T(8,128)S(1)}, f32[2,384,128]{2,1,0:T(8,128)S(1)}, u32[]{:S(2)}, u32[]{:S(2)}) %collective-permute-start.17) | collective-permute-done | bytes 393248 | tf_op jit(solution)/shard_map/ppermute | solution.py:373
  179.1 4.6 %collective-permute-done.19.end = f32[4,128,128]{2,1,0:T(8,128)S(1)} collective-permute-done((f32[4,128,128]{2,1,0:T(8,128)S(1)}, f32[4,128,128]{2,1,0:T(8,128)S(1)}, u32[]{:S(2)}, u32[]{:S(2)}) %collective-permute-start.19) | collective-permute-done | bytes 262176 | tf_op jit(solution)/shard_map/ppermute | solution.py:373
  (44 shorter events, 17.4 us)
Async XLA Ops:
  0.0 33.1 %copy-start.1 = (f32[2,2,512,256]{3,2,1,0:T(8,128)S(1)}, f32[2,2,512,256]{3,2,1,0:T(8,128)}, u32[]{:S(2)}) copy-start(f32[2,2,512,256]{3,2,1,0:T(8,128)} %main.3) | copy-start | bytes 6291460
  0.0 26.4 %copy-start.3 = (f32[1,1,4,256,256]{4,3,2,1,0:T(8,128)S(1)}, f32[1,1,4,256,256]{4,3,2,1,0:T(8,128)}, u32[]{:S(2)}) copy-start(f32[1,1,4,256,256]{4,3,2,1,0:T(8,128)} %amp.1) | copy-start | bytes 3145732
  0.0 26.4 %copy-start.4 = (f32[256,256]{1,0:T(8,128)S(1)}, f32[256,256]{1,0:T(8,128)}, u32[]{:S(2)}) copy-start(f32[256,256]{1,0:T(8,128)} %phase.1) | copy-start | bytes 786436
  1.1 13.6 %collective-permute-start = (f32[4,128,128]{2,1,0:T(8,128)S(1)}, f32[4,128,128]{2,1,0:T(8,128)S(1)}, u32[]{:S(2)}, u32[]{:S(2)}) collective-permute-start(f32[4,128,128]{2,1,0:T(8,128)S(1)} %slice.16), channel_id=1, source_target_pairs={{1,0},{2,1},{3,2},{4,3},{5,4},{6,5},{7,6},{8,7},{9,8},{10,9},{11,1... | collective-permute-start | bytes 786440 | tf_op jit(solution)/shard_map/ppermute | solution.py:373
  14.8 18.3 %collective-permute-start.2 = (f32[4,128,384]{2,1,0:T(8,128)S(1)}, f32[4,128,384]{2,1,0:T(8,128)S(1)}, u32[]{:S(2)}, u32[]{:S(2)}) collective-permute-start(f32[4,128,384]{2,1,0:T(8,128)S(1)} %pad_maximum_fusion), channel_id=1, source_target_pairs={{32,0},{64,32},{96,64},{128,96},{160,128},{192,160},{224,192},{33,... | collective-permute-start | bytes 2359304 | tf_op jit(solution)/shard_map/ppermute | solution.py:373
  17.3 15.8 %collective-permute-start.3 = (f32[2,384,128]{2,1,0:T(8,128)S(1)}, f32[2,384,128]{2,1,0:T(8,128)S(1)}, u32[]{:S(2)}, u32[]{:S(2)}) collective-permute-start(f32[2,384,128]{2,1,0:T(8,128)S(1)} %get-tuple-element.69), channel_id=1, source_target_pairs={{1,0},{2,1},{3,2},{4,3},{5,4},{6,5},{7,6},{8,7},{9,8},{10,9},{11,1... | collective-permute-start | bytes 1179656 | tf_op jit(solution)/shard_map/ppermute | solution.py:373
  23.8 17.8 %collective-permute-start.1 = (f32[2,384,128]{2,1,0:T(8,128)S(1)}, f32[2,384,128]{2,1,0:T(8,128)S(1)}, u32[]{:S(2)}, u32[]{:S(2)}) collective-permute-start(f32[2,384,128]{2,1,0:T(8,128)S(1)} %get-tuple-element.70), channel_id=1, source_target_pairs={{1,0},{2,1},{3,2},{4,3},{5,4},{6,5},{7,6},{8,7},{9,8},{10,9},{11,1... | collective-permute-start | bytes 1179656 | tf_op jit(solution)/shard_map/ppermute | solution.py:373
  30.9 2.3 %copy-start = (bf16[2,2,2,256,256]{4,3,2,1,0:T(8,128)(2,1)S(1)}, bf16[2,2,2,256,256]{4,3,2,1,0:T(8,128)(2,1)}, u32[]{:S(2)}) copy-start(bf16[2,2,2,256,256]{4,3,2,1,0:T(8,128)(2,1)} %constant.2.clone.tab) | copy-start | bytes 3145732
  30.9 2.3 %copy-start.2 = (f32[2,256,256]{2,1,0:T(8,128)S(1)}, f32[2,256,256]{2,1,0:T(8,128)}, u32[]{:S(2)}) copy-start(f32[2,256,256]{2,1,0:T(8,128)} %probe.9) | copy-start | bytes 1572868
  30.9 2.3 %copy-start.5 = (s32[1,1,4]{2,1,0:T(1,128)S(1)}, s32[1,1,4]{2,1,0:T(1,128)}, u32[]{:S(2)}) copy-start(s32[1,1,4]{2,1,0:T(1,128)} %orow.9) | copy-start | bytes 52
  30.9 2.3 %copy-start.6 = (s32[1,1,4]{2,1,0:T(1,128)S(1)}, s32[1,1,4]{2,1,0:T(1,128)}, u32[]{:S(2)}) copy-start(s32[1,1,4]{2,1,0:T(1,128)} %ocol.9) | copy-start | bytes 52
  31.0 2.3 %copy-start.7 = (s32[1,1,4]{2,1,0:T(1,128)S(1)}, s32[1,1,4]{2,1,0:T(1,128)}, u32[]{:S(2)}) copy-start(s32[1,1,4]{2,1,0:T(1,128)} %wbatch.9) | copy-start | bytes 52
  42.5 19.8 %collective-permute-start.4 = (f32[4,256,128]{2,1,0:T(8,128)S(1)}, f32[4,256,128]{2,1,0:T(8,128)S(1)}, u32[]{:S(2)}, u32[]{:S(2)}) collective-permute-start(f32[4,256,128]{2,1,0:T(8,128)S(1)} %get-tuple-element.41), channel_id=1, source_target_pairs={{0,1},{1,2},{2,3},{3,4},{4,5},{5,6},{6,7},{7,8},{8,9},{9,10},{10,1... | collective-permute-start | bytes 1572872 | tf_op jit(solution)/shard_map/ppermute | solution.py:373
  44.4 19.6 %collective-permute-start.5 = (f32[4,256,128]{2,1,0:T(8,128)S(1)}, f32[4,256,128]{2,1,0:T(8,128)S(1)}, u32[]{:S(2)}, u32[]{:S(2)}) collective-permute-start(f32[4,256,128]{2,1,0:T(8,128)S(1)} %get-tuple-element.42), channel_id=1, source_target_pairs={{1,0},{2,1},{3,2},{4,3},{5,4},{6,5},{7,6},{8,7},{9,8},{10,9},{11,1... | collective-permute-start | bytes 1572872 | tf_op jit(solution)/shard_map/ppermute | solution.py:373
  54.2 24.9 %collective-permute-start.6 = (f32[4,384,128]{2,1,0:T(8,128)S(1)}, f32[4,384,128]{2,1,0:T(8,128)S(1)}, u32[]{:S(2)}, u32[]{:S(2)}) collective-permute-start(f32[4,384,128]{2,1,0:T(8,128)S(1)} %get-tuple-element.45), channel_id=1, source_target_pairs={{0,1},{1,2},{2,3},{3,4},{4,5},{5,6},{6,7},{7,8},{8,9},{9,10},{10,1... | collective-permute-start | bytes 2359304 | tf_op jit(solution)/shard_map/ppermute | solution.py:373
  56.1 24.7 %collective-permute-start.7 = (f32[4,384,128]{2,1,0:T(8,128)S(1)}, f32[4,384,128]{2,1,0:T(8,128)S(1)}, u32[]{:S(2)}, u32[]{:S(2)}) collective-permute-start(f32[4,384,128]{2,1,0:T(8,128)S(1)} %get-tuple-element.46), channel_id=1, source_target_pairs={{1,0},{2,1},{3,2},{4,3},{5,4},{6,5},{7,6},{8,7},{9,8},{10,9},{11,1... | collective-permute-start | bytes 2359304 | tf_op jit(solution)/shard_map/ppermute | solution.py:373
  64.2 16.7 %collective-permute-start.8 = (f32[4,128,384]{2,1,0:T(8,128)S(1)}, f32[4,128,384]{2,1,0:T(8,128)S(1)}, u32[]{:S(2)}, u32[]{:S(2)}) collective-permute-start(f32[4,128,384]{2,1,0:T(8,128)S(1)} %get-tuple-element.47), channel_id=1, source_target_pairs={{0,32},{32,64},{64,96},{96,128},{128,160},{160,192},{192,224},{1,3... | collective-permute-start | bytes 2359304 | tf_op jit(solution)/shard_map/ppermute | solution.py:373
  71.2 9.6 %collective-permute-start.9 = (f32[4,128,384]{2,1,0:T(8,128)S(1)}, f32[4,128,384]{2,1,0:T(8,128)S(1)}, u32[]{:S(2)}, u32[]{:S(2)}) collective-permute-start(f32[4,128,384]{2,1,0:T(8,128)S(1)} %get-tuple-element.48), channel_id=1, source_target_pairs={{32,0},{64,32},{96,64},{128,96},{160,128},{192,160},{224,192},{33,... | collective-permute-start | bytes 2359304 | tf_op jit(solution)/shard_map/ppermute | solution.py:373
  87.0 18.4 %collective-permute-start.10 = (f32[4,256,128]{2,1,0:T(8,128)S(1)}, f32[4,256,128]{2,1,0:T(8,128)S(1)}, u32[]{:S(2)}, u32[]{:S(2)}) collective-permute-start(f32[4,256,128]{2,1,0:T(8,128)S(1)} %get-tuple-element.51), channel_id=1, source_target_pairs={{0,1},{1,2},{2,3},{3,4},{4,5},{5,6},{6,7},{7,8},{8,9},{9,10},{10,1... | collective-permute-start | bytes 1572872 | tf_op jit(solution)/shard_map/ppermute | solution.py:373
  88.9 17.6 %collective-permute-start.11 = (f32[4,256,128]{2,1,0:T(8,128)S(1)}, f32[4,256,128]{2,1,0:T(8,128)S(1)}, u32[]{:S(2)}, u32[]{:S(2)}) collective-permute-start(f32[4,256,128]{2,1,0:T(8,128)S(1)} %get-tuple-element.52), channel_id=1, source_target_pairs={{1,0},{2,1},{3,2},{4,3},{5,4},{6,5},{7,6},{8,7},{9,8},{10,9},{11,1... | collective-permute-start | bytes 1572872 | tf_op jit(solution)/shard_map/ppermute | solution.py:373
  95.5 25.9 %collective-permute-start.12 = (f32[4,384,128]{2,1,0:T(8,128)S(1)}, f32[4,384,128]{2,1,0:T(8,128)S(1)}, u32[]{:S(2)}, u32[]{:S(2)}) collective-permute-start(f32[4,384,128]{2,1,0:T(8,128)S(1)} %get-tuple-element.55), channel_id=1, source_target_pairs={{0,1},{1,2},{2,3},{3,4},{4,5},{5,6},{6,7},{7,8},{8,9},{9,10},{10,1... | collective-permute-start | bytes 2359304 | tf_op jit(solution)/shard_map/ppermute | solution.py:373
  97.4 25.2 %collective-permute-start.13 = (f32[4,384,128]{2,1,0:T(8,128)S(1)}, f32[4,384,128]{2,1,0:T(8,128)S(1)}, u32[]{:S(2)}, u32[]{:S(2)}) collective-permute-start(f32[4,384,128]{2,1,0:T(8,128)S(1)} %get-tuple-element.56), channel_id=1, source_target_pairs={{1,0},{2,1},{3,2},{4,3},{5,4},{6,5},{7,6},{8,7},{9,8},{10,9},{11,1... | collective-permute-start | bytes 2359304 | tf_op jit(solution)/shard_map/ppermute | solution.py:373
  106.7 15.8 %collective-permute-start.14 = (f32[4,128,384]{2,1,0:T(8,128)S(1)}, f32[4,128,384]{2,1,0:T(8,128)S(1)}, u32[]{:S(2)}, u32[]{:S(2)}) collective-permute-start(f32[4,128,384]{2,1,0:T(8,128)S(1)} %get-tuple-element.57), channel_id=1, source_target_pairs={{0,32},{32,64},{64,96},{96,128},{128,160},{160,192},{192,224},{1,3... | collective-permute-start | bytes 2359304 | tf_op jit(solution)/shard_map/ppermute | solution.py:373
  108.1 14.5 %collective-permute-start.15 = (f32[4,128,384]{2,1,0:T(8,128)S(1)}, f32[4,128,384]{2,1,0:T(8,128)S(1)}, u32[]{:S(2)}, u32[]{:S(2)}) collective-permute-start(f32[4,128,384]{2,1,0:T(8,128)S(1)} %get-tuple-element.58), channel_id=1, source_target_pairs={{32,0},{64,32},{96,64},{128,96},{160,128},{192,160},{224,192},{33,... | collective-permute-start | bytes 2359304 | tf_op jit(solution)/shard_map/ppermute | solution.py:373
  124.6 34.0 %collective-permute-start.16 = (f32[4,128,128]{2,1,0:T(8,128)S(1)}, f32[4,128,128]{2,1,0:T(8,128)S(1)}, u32[]{:S(2)}, u32[]{:S(2)}) collective-permute-start(f32[4,128,128]{2,1,0:T(8,128)S(1)} %get-tuple-element.63), channel_id=1, source_target_pairs={{0,32},{32,64},{64,96},{96,128},{128,160},{160,192},{192,224},{1,3... | collective-permute-start | bytes 786440 | tf_op jit(solution)/shard_map/ppermute | solution.py:373
  152.7 26.4 %collective-permute-start.20 = (f32[4,128,256]{2,1,0:T(8,128)S(1)}, f32[4,128,256]{2,1,0:T(8,128)S(1)}, u32[]{:S(2)}, u32[]{:S(2)}) collective-permute-start(f32[4,128,256]{2,1,0:T(8,128)S(1)} %get-tuple-element.68), channel_id=1, source_target_pairs={{0,32},{32,64},{64,96},{96,128},{128,160},{160,192},{192,224},{1,3... | collective-permute-start | bytes 1572872 | tf_op jit(solution)/shard_map/ppermute | solution.py:373
  154.7 16.0 %collective-permute-start.18 = (f32[2,384,128]{2,1,0:T(8,128)S(1)}, f32[2,384,128]{2,1,0:T(8,128)S(1)}, u32[]{:S(2)}, u32[]{:S(2)}) collective-permute-start(f32[2,384,128]{2,1,0:T(8,128)S(1)} %get-tuple-element.66), channel_id=1, source_target_pairs={{0,1},{1,2},{2,3},{3,4},{4,5},{5,6},{6,7},{7,8},{8,9},{9,10},{10,1... | collective-permute-start | bytes 1179656 | tf_op jit(solution)/shard_map/ppermute | solution.py:373
  156.6 22.5 %collective-permute-start.17 = (f32[2,384,128]{2,1,0:T(8,128)S(1)}, f32[2,384,128]{2,1,0:T(8,128)S(1)}, u32[]{:S(2)}, u32[]{:S(2)}) collective-permute-start(f32[2,384,128]{2,1,0:T(8,128)S(1)} %get-tuple-element.65), channel_id=1, source_target_pairs={{0,1},{1,2},{2,3},{3,4},{4,5},{5,6},{6,7},{7,8},{8,9},{9,10},{10,1... | collective-permute-start | bytes 1179656 | tf_op jit(solution)/shard_map/ppermute | solution.py:373
  158.8 24.9 %collective-permute-start.19 = (f32[4,128,128]{2,1,0:T(8,128)S(1)}, f32[4,128,128]{2,1,0:T(8,128)S(1)}, u32[]{:S(2)}, u32[]{:S(2)}) collective-permute-start(f32[4,128,128]{2,1,0:T(8,128)S(1)} %get-tuple-element.67), channel_id=1, source_target_pairs={{0,1},{1,2},{2,3},{3,4},{4,5},{5,6},{6,7},{7,8},{8,9},{9,10},{10,1... | collective-permute-start | bytes 786440 | tf_op jit(solution)/shard_map/ppermute | solution.py:373

commit v5 on v4

--- a/solution.py
+++ b/solution.py
@@ -210,16 +210,20 @@
         state[p, ROWS:, :] = bottom[p]
 
 
-def fold_sides(old, state, mid_l, mid_r, above, below):
+def fold_sides(old, state, mid_l, mid_r, above, below, core_a, core_b):
     in_c = jnp.where(inside("col"), 1.0, 0.0).astype(f32)
     in_r = jnp.where(inside("row"), 1.0, 0.0).astype(f32)
     rows = pl.ds(HALF, ROWS - HALF)
     for p in range(4):
         state[p, rows, :HALF] = old[p, rows, :HALF] - 0.5 * mid_l[p]
         state[p, rows, COLS:] = old[p, rows, COLS:] - (0.5 * in_c) * mid_r[p]
-        for at, fac, near in ((pl.ds(0, HALF), 0.5, above), (pl.ds(ROWS, HALF), 0.5 * in_r, below)):
-            state[p, at, :COLS] = old[p, at, :COLS] - fac * near[p, :, :COLS]
-            state[p, at, COLS:] = old[p, at, COLS:] - (fac * in_c) * near[p, :, COLS:]
+        for at, fac, near, core in (
+            (pl.ds(0, HALF), 0.5, above, core_a),
+            (pl.ds(ROWS, HALF), 0.5 * in_r, below, core_b),
+        ):
+            state[p, at, :HALF] = old[p, at, :HALF] - fac * near[p, :, :HALF]
+            state[p, at, HALF:COLS] = old[p, at, HALF:COLS] - fac * core[p]
+            state[p, at, COLS:] = old[p, at, COLS:] - (fac * in_c) * near[p, :, HALF:]
 
 
 def windows(batch, stages, count, orow, ocol, wbatch, tab, probe, prop, amp, state, grad, between, mid):
@@ -260,7 +264,9 @@
     lax.fori_loop(0, SLOTS, step, 0)
 
 
-def edges_of(grad, mid_l, mid_r, end_l, end_r):
+def edges_of(grad, mid_l, mid_r, end_l, end_r, top_core, bottom_core):
+    top_core[...] = grad[:, :HALF, HALF:COLS]
+    bottom_core[...] = grad[:, ROWS:, HALF:COLS]
     for mid, end, cols in ((mid_l, end_l, pl.ds(0, HALF)), (mid_r, end_r, pl.ds(COLS, HALF))):
         mid[...] = grad[:, HALF:ROWS, cols]
         end[:, :HALF, :] = grad[:, :HALF, cols]
@@ -278,7 +284,7 @@
 
 def batch_kernel(batch):
     def run(count, orow, ocol, wbatch, tab, probe, prop, amp, old, *rest):
-        sides, (state, grad), out = rest[1:5], rest[5:7], rest[7:]
+        sides, (state, grad), out = rest[1:7], rest[7:9], rest[9:]
         fold_sides(old, state, *sides)
         windows(batch, "abc", count, orow, ocol, wbatch, tab, probe, prop, amp, state, grad, None, None)
         edges_of(grad, *out)
@@ -287,7 +293,7 @@
 
 
 def final_kernel(count, orow, ocol, wbatch, tab, probe, prop, amp, old, *rest):
-    sides, (state, grad, mid, side_r) = rest[1:5], rest[5:]
+    sides, (state, grad, mid, side_r) = rest[1:7], rest[7:]
     fold_sides(old, state, *sides)
     windows(BATCHES - 1, "ab", count, orow, ocol, wbatch, tab, probe, prop, amp, state, grad, None, mid)
     side_r[...] = grad[2:, HALF:ROWS, COLS:]
@@ -305,8 +311,7 @@
     for at, flat, ends in ((0, top, pl.ds(0, h)), (ROWS, bottom, pl.ds(h, h))):
         rows = pl.ds(at, h)
         flat[:, :, :h] = grad[:, rows, :h] + end_l[:, ends]
-        flat[:, :, h:COLS] = grad[:, rows, h:COLS]
-        flat[:, :, COLS:] = grad[:, rows, COLS:] + end_r[:, ends]
+        flat[:, :, h:] = grad[:, rows, COLS:] + end_r[:, ends]
 
 
 def settle_kernel(state, grad, end_l, end_r, out, blank):
@@ -349,7 +354,6 @@
 EXT = (4, EXT_R, EXT_C)
 EDGE = (4, HALF, 2 * HALF)
 CORE = (4, HALF, HALF)
-FLAT = (4, HALF, EXT_C)
 SIDE = (2, ROWS - HALF, HALF)
 PLANES = (SLOTS, 2, WIN, WIN)
 MIDS = (4, ROWS - HALF, HALF)
@@ -391,7 +395,7 @@
     (state,) = call(
         assemble_kernel, (), (transmission, right_top, right_2, bottom, state), [EXT], {4: 0}
     )
-    edges = [MIDS, MIDS, ENDS, ENDS]
+    edges = [MIDS, MIDS, ENDS, ENDS, CORE, CORE]
     for b in range(BATCHES - 1):
         common = (tab, probe, prop, amp, state)
         if b == 0:
@@ -402,18 +406,20 @@
             state, grad, *sent = call(
                 batch_kernel(b), scalars, (*common, grad, *parts), [EXT, EXT, *edges], {8: 0, 9: 1}
             )
-        mid_l, mid_r, end_l, end_r = sent
+        mid_l, mid_r, end_l, end_r, top_core, bottom_core = sent
         from_left = from_behind(end_r, "col", 1)
         from_right = from_behind(end_l, "col", -1)
         mid_left = from_behind(mid_r, "col", 1)
         mid_right = from_behind(mid_l, "col", -1)
-        top, bottom = call(flat_kernel, (), (grad, from_left, from_right), [FLAT, FLAT])
+        core_a = from_behind(bottom_core, "row", 1)
+        core_b = from_behind(top_core, "row", -1)
+        top, bottom = call(flat_kernel, (), (grad, from_left, from_right), [EDGE, EDGE])
         above = from_behind(bottom, "row", 1)
         below = from_behind(top, "row", -1)
         state, grad = call(
             settle_kernel, (), (state, grad, from_left, from_right), [EXT, EXT], {0: 0, 1: 1}
         )
-        parts = (mid_left, mid_right, above, below)
+        parts = (mid_left, mid_right, above, below, core_a, core_b)
     state, grad, mid, side_2 = call(
         final_kernel,
         scalars,

time: 186 us -> 186 us (level)
  waiting for transfers between devices: 59 us -> 51.9 us
  starting transfers between devices: 101 us -> 108 us
    ppermute x21 -> x25, waiting for transfers between devices: 59 us -> 51.9 us  [from_behind(): return lax.ppermute(array, axis, pairs)]
    ppermute x21 -> x25, starting transfers between devices: 101 us -> 108 us  [from_behind(): return lax.ppermute(array, axis, pairs)]
  transfers between devices with their start and end apart: 21 -> 25, of which waited for: 14 -> 11; matrix products, arithmetic and copies ran while one was open for 1% -> 1% of each run, Pallas kernels for 5% -> 5%
where the time goes in v5:
time: 186 us; the launch traced here: 185 us
  starting transfers between devices  108 us (58%)
  waiting for transfers between devices  51.9 us (28%)
  Pallas kernels  20.8 us (11%)
  local copies, waits for them, and re-layouts  3.45 us (2%)
    ppermute x25, starting transfers between devices, from_behind(): return lax.ppermute(array, axis, pairs)  108 us
    ppermute x25, waiting for transfers between devices, from_behind(): return lax.ppermute(array, axis, pairs)  51.9 us
    pallas_call x14, Pallas kernels, call(): pl.pallas_call(kernel, in_specs=[SM] * len(scalars) + [VM] * len(arrays),...  20.8 us
  transfers between devices with their start and end apart: 25, of which 11 were waited for; matrix products, arithmetic and copies ran while one was open for 1% of the time, Pallas kernels for 5%

profile of v5, /device:TPU:6, one launch (start us, length us, event | category | flops | bytes accessed | tf_op | source)
XLA Modules:
  0.0 185.4 jit_solution(7619563985980994434)
XLA Ops:
  1.1 8.0 %collective-permute-start = (f32[4,128,128]{2,1,0:T(8,128)S(1)}, f32[4,128,128]{2,1,0:T(8,128)S(1)}, u32[]{:S(2)}, u32[]{:S(2)}) collective-permute-start(f32[4,128,128]{2,1,0:T(8,128)S(1)} %slice.16), channel_id=1, source_target_pairs={{1,0},{2,1},{3,2},{4,3},{5,4},{6,5},{7,6},{8,7},{9,8},{10,9},{11,1... | collective-permute-start | bytes 786440 | tf_op jit(solution)/shard_map/ppermute | solution.py:377
  10.3 4.5 %collective-permute-done.right_top = f32[4,128,128]{2,1,0:T(8,128)S(1)} collective-permute-done((f32[4,128,128]{2,1,0:T(8,128)S(1)}, f32[4,128,128]{2,1,0:T(8,128)S(1)}, u32[]{:S(2)}, u32[]{:S(2)}) %collective-permute-start) | collective-permute-done | bytes 262176 | tf_op jit(solution)/shard_map/ppermute | solution.py:377
  17.3 6.5 %collective-permute-start.3 = (f32[2,384,128]{2,1,0:T(8,128)S(1)}, f32[2,384,128]{2,1,0:T(8,128)S(1)}, u32[]{:S(2)}, u32[]{:S(2)}) collective-permute-start(f32[2,384,128]{2,1,0:T(8,128)S(1)} %get-tuple-element.77), channel_id=1, source_target_pairs={{1,0},{2,1},{3,2},{4,3},{5,4},{6,5},{7,6},{8,7},{9,8},{10,9},{11,1... | collective-permute-start | bytes 1179656 | tf_op jit(solution)/shard_map/ppermute | solution.py:377
  23.8 1.9 %collective-permute-start.1 = (f32[2,384,128]{2,1,0:T(8,128)S(1)}, f32[2,384,128]{2,1,0:T(8,128)S(1)}, u32[]{:S(2)}, u32[]{:S(2)}) collective-permute-start(f32[2,384,128]{2,1,0:T(8,128)S(1)} %get-tuple-element.78), channel_id=1, source_target_pairs={{1,0},{2,1},{3,2},{4,3},{5,4},{6,5},{7,6},{8,7},{9,8},{10,9},{11,1... | collective-permute-start | bytes 1179656 | tf_op jit(solution)/shard_map/ppermute | solution.py:377
  26.4 4.5 %shard_map.91 = (f32[4,256,256]{2,1,0:T(8,128)S(1)}, f32[2,256,256]{2,1,0:T(8,128)S(1)}, f32[4,640,384]{2,1,0:T(8,128)S(1)}) custom-call(f32[1,1,4,256,256]{4,3,2,1,0:T(8,128)S(1)} %copy-done.3, f32[256,256]{1,0:T(8,128)S(1)} %copy-done.4), custom_call_target="tpu_custom_call" | custom-call | tf_op jit(solution)/shard_map/pallas_call | solution.py:364
  31.0 2.1 %collective-permute-done.3.right_rest = f32[2,384,128]{2,1,0:T(8,128)S(1)} collective-permute-done((f32[2,384,128]{2,1,0:T(8,128)S(1)}, f32[2,384,128]{2,1,0:T(8,128)S(1)}, u32[]{:S(2)}, u32[]{:S(2)}) %collective-permute-start.3) | collective-permute-done | bytes 393248 | tf_op jit(solution)/shard_map/ppermute | solution.py:377
  33.9 7.6 %collective-permute-done.1.right_rest = f32[2,384,128]{2,1,0:T(8,128)S(1)} collective-permute-done((f32[2,384,128]{2,1,0:T(8,128)S(1)}, f32[2,384,128]{2,1,0:T(8,128)S(1)}, u32[]{:S(2)}, u32[]{:S(2)}) %collective-permute-start.1) | collective-permute-done | bytes 393248 | tf_op jit(solution)/shard_map/ppermute | solution.py:377
  42.5 1.9 %collective-permute-start.4 = (f32[4,256,128]{2,1,0:T(8,128)S(1)}, f32[4,256,128]{2,1,0:T(8,128)S(1)}, u32[]{:S(2)}, u32[]{:S(2)}) collective-permute-start(f32[4,256,128]{2,1,0:T(8,128)S(1)} %get-tuple-element.45), channel_id=1, source_target_pairs={{0,1},{1,2},{2,3},{3,4},{4,5},{5,6},{6,7},{7,8},{8,9},{9,10},{10,1... | collective-permute-start | bytes 1572872 | tf_op jit(solution)/shard_map/ppermute | solution.py:377
  44.4 9.8 %collective-permute-start.5 = (f32[4,256,128]{2,1,0:T(8,128)S(1)}, f32[4,256,128]{2,1,0:T(8,128)S(1)}, u32[]{:S(2)}, u32[]{:S(2)}) collective-permute-start(f32[4,256,128]{2,1,0:T(8,128)S(1)} %get-tuple-element.46), channel_id=1, source_target_pairs={{1,0},{2,1},{3,2},{4,3},{5,4},{6,5},{7,6},{8,7},{9,8},{10,9},{11,1... | collective-permute-start | bytes 1572872 | tf_op jit(solution)/shard_map/ppermute | solution.py:377
  54.2 1.9 %collective-permute-start.6 = (f32[4,384,128]{2,1,0:T(8,128)S(1)}, f32[4,384,128]{2,1,0:T(8,128)S(1)}, u32[]{:S(2)}, u32[]{:S(2)}) collective-permute-start(f32[4,384,128]{2,1,0:T(8,128)S(1)} %get-tuple-element.49), channel_id=1, source_target_pairs={{0,1},{1,2},{2,3},{3,4},{4,5},{5,6},{6,7},{7,8},{8,9},{9,10},{10,1... | collective-permute-start | bytes 2359304 | tf_op jit(solution)/shard_map/ppermute | solution.py:377
  56.1 6.0 %collective-permute-start.7 = (f32[4,384,128]{2,1,0:T(8,128)S(1)}, f32[4,384,128]{2,1,0:T(8,128)S(1)}, u32[]{:S(2)}, u32[]{:S(2)}) collective-permute-start(f32[4,384,128]{2,1,0:T(8,128)S(1)} %get-tuple-element.50), channel_id=1, source_target_pairs={{1,0},{2,1},{3,2},{4,3},{5,4},{6,5},{7,6},{8,7},{9,8},{10,9},{11,1... | collective-permute-start | bytes 2359304 | tf_op jit(solution)/shard_map/ppermute | solution.py:377
  62.2 4.5 %collective-permute-start.10 = (f32[4,128,128]{2,1,0:T(8,128)S(1)}, f32[4,128,128]{2,1,0:T(8,128)S(1)}, u32[]{:S(2)}, u32[]{:S(2)}) collective-permute-start(f32[4,128,128]{2,1,0:T(8,128)S(1)} %get-tuple-element.53), channel_id=1, source_target_pairs={{0,32},{32,64},{64,96},{96,128},{128,160},{160,192},{192,224},{1,3... | collective-permute-start | bytes 786440 | tf_op jit(solution)/shard_map/ppermute | solution.py:377
  66.9 4.3 %collective-permute-start.8 = (f32[4,128,256]{2,1,0:T(8,128)S(1)}, f32[4,128,256]{2,1,0:T(8,128)S(1)}, u32[]{:S(2)}, u32[]{:S(2)}) collective-permute-start(f32[4,128,256]{2,1,0:T(8,128)S(1)} %get-tuple-element.51), channel_id=1, source_target_pairs={{0,32},{32,64},{64,96},{96,128},{128,160},{160,192},{192,224},{1,3... | collective-permute-start | bytes 1572872 | tf_op jit(solution)/shard_map/ppermute | solution.py:377
  74.0 2.2 %shard_map.96 = (f32[4,640,384]{2,1,0:T(8,128)S(1)}, f32[4,640,384]{2,1,0:T(8,128)S(1)}) custom-call(f32[4,640,384]{2,1,0:T(8,128)S(1)} %shard_map.93.state, f32[4,640,384]{2,1,0:T(8,128)S(1)} %get-tuple-element.44.grad, f32[4,256,128]{2,1,0:T(8,128)S(1)} %collective-permute-done.4.end_l, ...), custom_call_target="tpu_custom_call", output_to_operand_aliasing={{0}: (0, {}), {1}: (1, {})} | custom-call | tf_op jit(solution)/shard_map/pallas_call | solution.py:364
  76.6 2.6 %collective-permute-done.6.rest_1_ = f32[4,384,128]{2,1,0:T(8,128)S(1)} collective-permute-done((f32[4,384,128]{2,1,0:T(8,128)S(1)}, f32[4,384,128]{2,1,0:T(8,128)S(1)}, u32[]{:S(2)}, u32[]{:S(2)}) %collective-permute-start.6) | collective-permute-done | bytes 786464 | tf_op jit(solution)/shard_map/ppermute | solution.py:377
  80.9 6.2 %shard_map.98 = (f32[4,640,384]{2,1,0:T(8,128)S(1)}, f32[4,640,384]{2,1,0:T(8,128)S(1)}, f32[4,384,128]{2,1,0:T(8,128)S(1)}, f32[4,384,128]{2,1,0:T(8,128)S(1)},...) custom-call(s32[1,1]{1,0:T(1,128)S(6)} %copy.32.count, ...), custom_call_target="tpu_custom_call", output_to_operand_aliasing={{0}: (8, {}), {1}: (9, {})} | custom-call | tf_op jit(solution)/shard_map/pallas_call | solution.py:364
  87.1 1.9 %collective-permute-start.12 = (f32[4,256,128]{2,1,0:T(8,128)S(1)}, f32[4,256,128]{2,1,0:T(8,128)S(1)}, u32[]{:S(2)}, u32[]{:S(2)}) collective-permute-start(f32[4,256,128]{2,1,0:T(8,128)S(1)} %get-tuple-element.57), channel_id=1, source_target_pairs={{0,1},{1,2},{2,3},{3,4},{4,5},{5,6},{6,7},{7,8},{8,9},{9,10},{10,1... | collective-permute-start | bytes 1572872 | tf_op jit(solution)/shard_map/ppermute | solution.py:377
  89.0 6.5 %collective-permute-start.13 = (f32[4,256,128]{2,1,0:T(8,128)S(1)}, f32[4,256,128]{2,1,0:T(8,128)S(1)}, u32[]{:S(2)}, u32[]{:S(2)}) collective-permute-start(f32[4,256,128]{2,1,0:T(8,128)S(1)} %get-tuple-element.58), channel_id=1, source_target_pairs={{1,0},{2,1},{3,2},{4,3},{5,4},{6,5},{7,6},{8,7},{9,8},{10,9},{11,1... | collective-permute-start | bytes 1572872 | tf_op jit(solution)/shard_map/ppermute | solution.py:377
  95.5 1.9 %collective-permute-start.14 = (f32[4,384,128]{2,1,0:T(8,128)S(1)}, f32[4,384,128]{2,1,0:T(8,128)S(1)}, u32[]{:S(2)}, u32[]{:S(2)}) collective-permute-start(f32[4,384,128]{2,1,0:T(8,128)S(1)} %get-tuple-element.61), channel_id=1, source_target_pairs={{0,1},{1,2},{2,3},{3,4},{4,5},{5,6},{6,7},{7,8},{8,9},{9,10},{10,1... | collective-permute-start | bytes 2359304 | tf_op jit(solution)/shard_map/ppermute | solution.py:377
  97.5 6.0 %collective-permute-start.15 = (f32[4,384,128]{2,1,0:T(8,128)S(1)}, f32[4,384,128]{2,1,0:T(8,128)S(1)}, u32[]{:S(2)}, u32[]{:S(2)}) collective-permute-start(f32[4,384,128]{2,1,0:T(8,128)S(1)} %get-tuple-element.62), channel_id=1, source_target_pairs={{1,0},{2,1},{3,2},{4,3},{5,4},{6,5},{7,6},{8,7},{9,8},{10,9},{11,1... | collective-permute-start | bytes 2359304 | tf_op jit(solution)/shard_map/ppermute | solution.py:377
  103.5 2.9 %collective-permute-start.18 = (f32[4,128,128]{2,1,0:T(8,128)S(1)}, f32[4,128,128]{2,1,0:T(8,128)S(1)}, u32[]{:S(2)}, u32[]{:S(2)}) collective-permute-start(f32[4,128,128]{2,1,0:T(8,128)S(1)} %get-tuple-element.65), channel_id=1, source_target_pairs={{0,32},{32,64},{64,96},{96,128},{128,160},{160,192},{192,224},{1,3... | collective-permute-start | bytes 786440 | tf_op jit(solution)/shard_map/ppermute | solution.py:377
  106.8 3.7 %collective-permute-start.16 = (f32[4,128,256]{2,1,0:T(8,128)S(1)}, f32[4,128,256]{2,1,0:T(8,128)S(1)}, u32[]{:S(2)}, u32[]{:S(2)}) collective-permute-start(f32[4,128,256]{2,1,0:T(8,128)S(1)} %get-tuple-element.63), channel_id=1, source_target_pairs={{0,32},{32,64},{64,96},{96,128},{128,160},{160,192},{192,224},{1,3... | collective-permute-start | bytes 1572872 | tf_op jit(solution)/shard_map/ppermute | solution.py:377
  113.4 2.2 %shard_map.99 = (f32[4,640,384]{2,1,0:T(8,128)S(1)}, f32[4,640,384]{2,1,0:T(8,128)S(1)}) custom-call(f32[4,640,384]{2,1,0:T(8,128)S(1)} %get-tuple-element.55.state, f32[4,640,384]{2,1,0:T(8,128)S(1)} %get-tuple-element.56.grad, f32[4,256,128]{2,1,0:T(8,128)S(1)} %collective-permute-done.12.end_l, ...), custom_call_target="tpu_custom_call", output_to_operand_aliasing={{0}: (0, {}), {1}: (1, {})} | custom-call | tf_op jit(solution)/shard_map/pallas_call | solution.py:364
  115.5 9.6 %collective-permute-done.19.rest_6_ = f32[4,128,128]{2,1,0:T(8,128)S(1)} collective-permute-done((f32[4,128,128]{2,1,0:T(8,128)S(1)}, f32[4,128,128]{2,1,0:T(8,128)S(1)}, u32[]{:S(2)}, u32[]{:S(2)}) %collective-permute-start.19) | collective-permute-done | bytes 262176 | tf_op jit(solution)/shard_map/ppermute | solution.py:377
  127.2 25.7 %collective-permute-start.20 = (f32[4,128,128]{2,1,0:T(8,128)S(1)}, f32[4,128,128]{2,1,0:T(8,128)S(1)}, u32[]{:S(2)}, u32[]{:S(2)}) collective-permute-start(f32[4,128,128]{2,1,0:T(8,128)S(1)} %get-tuple-element.71), channel_id=1, source_target_pairs={{0,32},{32,64},{64,96},{96,128},{128,160},{160,192},{192,224},{1,3... | collective-permute-start | bytes 786440 | tf_op jit(solution)/shard_map/ppermute | solution.py:377
  152.9 1.9 %collective-permute-start.24 = (f32[4,128,256]{2,1,0:T(8,128)S(1)}, f32[4,128,256]{2,1,0:T(8,128)S(1)}, u32[]{:S(2)}, u32[]{:S(2)}) collective-permute-start(f32[4,128,256]{2,1,0:T(8,128)S(1)} %get-tuple-element.76), channel_id=1, source_target_pairs={{0,32},{32,64},{64,96},{96,128},{128,160},{160,192},{192,224},{1,3... | collective-permute-start | bytes 1572872 | tf_op jit(solution)/shard_map/ppermute | solution.py:377
  154.8 1.9 %collective-permute-start.22 = (f32[2,384,128]{2,1,0:T(8,128)S(1)}, f32[2,384,128]{2,1,0:T(8,128)S(1)}, u32[]{:S(2)}, u32[]{:S(2)}) collective-permute-start(f32[2,384,128]{2,1,0:T(8,128)S(1)} %get-tuple-element.74), channel_id=1, source_target_pairs={{0,1},{1,2},{2,3},{3,4},{4,5},{5,6},{6,7},{7,8},{8,9},{9,10},{10,1... | collective-permute-start | bytes 1179656 | tf_op jit(solution)/shard_map/ppermute | solution.py:377
  156.7 1.9 %collective-permute-start.21 = (f32[2,384,128]{2,1,0:T(8,128)S(1)}, f32[2,384,128]{2,1,0:T(8,128)S(1)}, u32[]{:S(2)}, u32[]{:S(2)}) collective-permute-start(f32[2,384,128]{2,1,0:T(8,128)S(1)} %get-tuple-element.73), channel_id=1, source_target_pairs={{0,1},{1,2},{2,3},{3,4},{4,5},{5,6},{6,7},{7,8},{8,9},{9,10},{10,1... | collective-permute-start | bytes 1179656 | tf_op jit(solution)/shard_map/ppermute | solution.py:377
  158.9 1.9 %collective-permute-start.23 = (f32[4,128,128]{2,1,0:T(8,128)S(1)}, f32[4,128,128]{2,1,0:T(8,128)S(1)}, u32[]{:S(2)}, u32[]{:S(2)}) collective-permute-start(f32[4,128,128]{2,1,0:T(8,128)S(1)} %get-tuple-element.75), channel_id=1, source_target_pairs={{0,1},{1,2},{2,3},{3,4},{4,5},{5,6},{6,7},{7,8},{8,9},{9,10},{10,1... | collective-permute-start | bytes 786440 | tf_op jit(solution)/shard_map/ppermute | solution.py:377
  160.9 9.9 %collective-permute-done.22.mid2 = f32[2,384,128]{2,1,0:T(8,128)S(1)} collective-permute-done((f32[2,384,128]{2,1,0:T(8,128)S(1)}, f32[2,384,128]{2,1,0:T(8,128)S(1)}, u32[]{:S(2)}, u32[]{:S(2)}) %collective-permute-start.22) | collective-permute-done | bytes 393248 | tf_op jit(solution)/shard_map/ppermute | solution.py:377
  170.8 8.4 %collective-permute-done.21.mid1 = f32[2,384,128]{2,1,0:T(8,128)S(1)} collective-permute-done((f32[2,384,128]{2,1,0:T(8,128)S(1)}, f32[2,384,128]{2,1,0:T(8,128)S(1)}, u32[]{:S(2)}, u32[]{:S(2)}) %collective-permute-start.21) | collective-permute-done | bytes 393248 | tf_op jit(solution)/shard_map/ppermute | solution.py:377
  179.2 4.6 %collective-permute-done.23.end = f32[4,128,128]{2,1,0:T(8,128)S(1)} collective-permute-done((f32[4,128,128]{2,1,0:T(8,128)S(1)}, f32[4,128,128]{2,1,0:T(8,128)S(1)}, u32[]{:S(2)}, u32[]{:S(2)}) %collective-permute-start.23) | collective-permute-done | bytes 262176 | tf_op jit(solution)/shard_map/ppermute | solution.py:377
  (52 shorter events, 18.5 us)
Async XLA Ops:
  0.0 33.1 %copy-start.1 = (f32[2,2,512,256]{3,2,1,0:T(8,128)S(1)}, f32[2,2,512,256]{3,2,1,0:T(8,128)}, u32[]{:S(2)}) copy-start(f32[2,2,512,256]{3,2,1,0:T(8,128)} %main.3) | copy-start | bytes 6291460
  0.0 26.4 %copy-start.3 = (f32[1,1,4,256,256]{4,3,2,1,0:T(8,128)S(1)}, f32[1,1,4,256,256]{4,3,2,1,0:T(8,128)}, u32[]{:S(2)}) copy-start(f32[1,1,4,256,256]{4,3,2,1,0:T(8,128)} %amp.1) | copy-start | bytes 3145732
  0.0 26.4 %copy-start.4 = (f32[256,256]{1,0:T(8,128)S(1)}, f32[256,256]{1,0:T(8,128)}, u32[]{:S(2)}) copy-start(f32[256,256]{1,0:T(8,128)} %phase.1) | copy-start | bytes 786436
  1.1 13.6 %collective-permute-start = (f32[4,128,128]{2,1,0:T(8,128)S(1)}, f32[4,128,128]{2,1,0:T(8,128)S(1)}, u32[]{:S(2)}, u32[]{:S(2)}) collective-permute-start(f32[4,128,128]{2,1,0:T(8,128)S(1)} %slice.16), channel_id=1, source_target_pairs={{1,0},{2,1},{3,2},{4,3},{5,4},{6,5},{7,6},{8,7},{9,8},{10,9},{11,1... | collective-permute-start | bytes 786440 | tf_op jit(solution)/shard_map/ppermute | solution.py:377
  14.8 18.3 %collective-permute-start.2 = (f32[4,128,384]{2,1,0:T(8,128)S(1)}, f32[4,128,384]{2,1,0:T(8,128)S(1)}, u32[]{:S(2)}, u32[]{:S(2)}) collective-permute-start(f32[4,128,384]{2,1,0:T(8,128)S(1)} %pad_maximum_fusion), channel_id=1, source_target_pairs={{32,0},{64,32},{96,64},{128,96},{160,128},{192,160},{224,192},{33,... | collective-permute-start | bytes 2359304 | tf_op jit(solution)/shard_map/ppermute | solution.py:377
  17.3 15.8 %collective-permute-start.3 = (f32[2,384,128]{2,1,0:T(8,128)S(1)}, f32[2,384,128]{2,1,0:T(8,128)S(1)}, u32[]{:S(2)}, u32[]{:S(2)}) collective-permute-start(f32[2,384,128]{2,1,0:T(8,128)S(1)} %get-tuple-element.77), channel_id=1, source_target_pairs={{1,0},{2,1},{3,2},{4,3},{5,4},{6,5},{7,6},{8,7},{9,8},{10,9},{11,1... | collective-permute-start | bytes 1179656 | tf_op jit(solution)/shard_map/ppermute | solution.py:377
  23.8 17.8 %collective-permute-start.1 = (f32[2,384,128]{2,1,0:T(8,128)S(1)}, f32[2,384,128]{2,1,0:T(8,128)S(1)}, u32[]{:S(2)}, u32[]{:S(2)}) collective-permute-start(f32[2,384,128]{2,1,0:T(8,128)S(1)} %get-tuple-element.78), channel_id=1, source_target_pairs={{1,0},{2,1},{3,2},{4,3},{5,4},{6,5},{7,6},{8,7},{9,8},{10,9},{11,1... | collective-permute-start | bytes 1179656 | tf_op jit(solution)/shard_map/ppermute | solution.py:377
  30.9 2.3 %copy-start = (bf16[2,2,2,256,256]{4,3,2,1,0:T(8,128)(2,1)S(1)}, bf16[2,2,2,256,256]{4,3,2,1,0:T(8,128)(2,1)}, u32[]{:S(2)}) copy-start(bf16[2,2,2,256,256]{4,3,2,1,0:T(8,128)(2,1)} %constant.2.clone.tab) | copy-start | bytes 3145732
  30.9 2.3 %copy-start.2 = (f32[2,256,256]{2,1,0:T(8,128)S(1)}, f32[2,256,256]{2,1,0:T(8,128)}, u32[]{:S(2)}) copy-start(f32[2,256,256]{2,1,0:T(8,128)} %probe.9) | copy-start | bytes 1572868
  30.9 2.3 %copy-start.5 = (s32[1,1,4]{2,1,0:T(1,128)S(1)}, s32[1,1,4]{2,1,0:T(1,128)}, u32[]{:S(2)}) copy-start(s32[1,1,4]{2,1,0:T(1,128)} %orow.9) | copy-start | bytes 52
  30.9 2.3 %copy-start.6 = (s32[1,1,4]{2,1,0:T(1,128)S(1)}, s32[1,1,4]{2,1,0:T(1,128)}, u32[]{:S(2)}) copy-start(s32[1,1,4]{2,1,0:T(1,128)} %ocol.9) | copy-start | bytes 52
  42.5 24.2 %collective-permute-start.4 = (f32[4,256,128]{2,1,0:T(8,128)S(1)}, f32[4,256,128]{2,1,0:T(8,128)S(1)}, u32[]{:S(2)}, u32[]{:S(2)}) collective-permute-start(f32[4,256,128]{2,1,0:T(8,128)S(1)} %get-tuple-element.45), channel_id=1, source_target_pairs={{0,1},{1,2},{2,3},{3,4},{4,5},{5,6},{6,7},{7,8},{8,9},{9,10},{10,1... | collective-permute-start | bytes 1572872 | tf_op jit(solution)/shard_map/ppermute | solution.py:377
  44.4 22.3 %collective-permute-start.5 = (f32[4,256,128]{2,1,0:T(8,128)S(1)}, f32[4,256,128]{2,1,0:T(8,128)S(1)}, u32[]{:S(2)}, u32[]{:S(2)}) collective-permute-start(f32[4,256,128]{2,1,0:T(8,128)S(1)} %get-tuple-element.46), channel_id=1, source_target_pairs={{1,0},{2,1},{3,2},{4,3},{5,4},{6,5},{7,6},{8,7},{9,8},{10,9},{11,1... | collective-permute-start | bytes 1572872 | tf_op jit(solution)/shard_map/ppermute | solution.py:377
  54.2 24.9 %collective-permute-start.6 = (f32[4,384,128]{2,1,0:T(8,128)S(1)}, f32[4,384,128]{2,1,0:T(8,128)S(1)}, u32[]{:S(2)}, u32[]{:S(2)}) collective-permute-start(f32[4,384,128]{2,1,0:T(8,128)S(1)} %get-tuple-element.49), channel_id=1, source_target_pairs={{0,1},{1,2},{2,3},{3,4},{4,5},{5,6},{6,7},{7,8},{8,9},{9,10},{10,1... | collective-permute-start | bytes 2359304 | tf_op jit(solution)/shard_map/ppermute | solution.py:377
  56.1 24.7 %collective-permute-start.7 = (f32[4,384,128]{2,1,0:T(8,128)S(1)}, f32[4,384,128]{2,1,0:T(8,128)S(1)}, u32[]{:S(2)}, u32[]{:S(2)}) collective-permute-start(f32[4,384,128]{2,1,0:T(8,128)S(1)} %get-tuple-element.50), channel_id=1, source_target_pairs={{1,0},{2,1},{3,2},{4,3},{5,4},{6,5},{7,6},{8,7},{9,8},{10,9},{11,1... | collective-permute-start | bytes 2359304 | tf_op jit(solution)/shard_map/ppermute | solution.py:377
  62.2 10.3 %collective-permute-start.10 = (f32[4,128,128]{2,1,0:T(8,128)S(1)}, f32[4,128,128]{2,1,0:T(8,128)S(1)}, u32[]{:S(2)}, u32[]{:S(2)}) collective-permute-start(f32[4,128,128]{2,1,0:T(8,128)S(1)} %get-tuple-element.53), channel_id=1, source_target_pairs={{0,32},{32,64},{64,96},{96,128},{128,160},{160,192},{192,224},{1,3... | collective-permute-start | bytes 786440 | tf_op jit(solution)/shard_map/ppermute | solution.py:377
  66.9 14.0 %collective-permute-start.8 = (f32[4,128,256]{2,1,0:T(8,128)S(1)}, f32[4,128,256]{2,1,0:T(8,128)S(1)}, u32[]{:S(2)}, u32[]{:S(2)}) collective-permute-start(f32[4,128,256]{2,1,0:T(8,128)S(1)} %get-tuple-element.51), channel_id=1, source_target_pairs={{0,32},{32,64},{64,96},{96,128},{128,160},{160,192},{192,224},{1,3... | collective-permute-start | bytes 1572872 | tf_op jit(solution)/shard_map/ppermute | solution.py:377
  71.2 9.7 %collective-permute-start.9 = (f32[4,128,256]{2,1,0:T(8,128)S(1)}, f32[4,128,256]{2,1,0:T(8,128)S(1)}, u32[]{:S(2)}, u32[]{:S(2)}) collective-permute-start(f32[4,128,256]{2,1,0:T(8,128)S(1)} %get-tuple-element.52), channel_id=1, source_target_pairs={{32,0},{64,32},{96,64},{128,96},{160,128},{192,160},{224,192},{33,... | collective-permute-start | bytes 1572872 | tf_op jit(solution)/shard_map/ppermute | solution.py:377
  72.5 4.1 %collective-permute-start.11 = (f32[4,128,128]{2,1,0:T(8,128)S(1)}, f32[4,128,128]{2,1,0:T(8,128)S(1)}, u32[]{:S(2)}, u32[]{:S(2)}) collective-permute-start(f32[4,128,128]{2,1,0:T(8,128)S(1)} %get-tuple-element.54), channel_id=1, source_target_pairs={{32,0},{64,32},{96,64},{128,96},{160,128},{192,160},{224,192},{33,... | collective-permute-start | bytes 786440 | tf_op jit(solution)/shard_map/ppermute | solution.py:377
  87.1 19.3 %collective-permute-start.12 = (f32[4,256,128]{2,1,0:T(8,128)S(1)}, f32[4,256,128]{2,1,0:T(8,128)S(1)}, u32[]{:S(2)}, u32[]{:S(2)}) collective-permute-start(f32[4,256,128]{2,1,0:T(8,128)S(1)} %get-tuple-element.57), channel_id=1, source_target_pairs={{0,1},{1,2},{2,3},{3,4},{4,5},{5,6},{6,7},{7,8},{8,9},{9,10},{10,1... | collective-permute-start | bytes 1572872 | tf_op jit(solution)/shard_map/ppermute | solution.py:377
  89.0 17.6 %collective-permute-start.13 = (f32[4,256,128]{2,1,0:T(8,128)S(1)}, f32[4,256,128]{2,1,0:T(8,128)S(1)}, u32[]{:S(2)}, u32[]{:S(2)}) collective-permute-start(f32[4,256,128]{2,1,0:T(8,128)S(1)} %get-tuple-element.58), channel_id=1, source_target_pairs={{1,0},{2,1},{3,2},{4,3},{5,4},{6,5},{7,6},{8,7},{9,8},{10,9},{11,1... | collective-permute-start | bytes 1572872 | tf_op jit(solution)/shard_map/ppermute | solution.py:377
  95.5 29.6 %collective-permute-start.14 = (f32[4,384,128]{2,1,0:T(8,128)S(1)}, f32[4,384,128]{2,1,0:T(8,128)S(1)}, u32[]{:S(2)}, u32[]{:S(2)}) collective-permute-start(f32[4,384,128]{2,1,0:T(8,128)S(1)} %get-tuple-element.61), channel_id=1, source_target_pairs={{0,1},{1,2},{2,3},{3,4},{4,5},{5,6},{6,7},{7,8},{8,9},{9,10},{10,1... | collective-permute-start | bytes 2359304 | tf_op jit(solution)/shard_map/ppermute | solution.py:377
  97.5 27.7 %collective-permute-start.15 = (f32[4,384,128]{2,1,0:T(8,128)S(1)}, f32[4,384,128]{2,1,0:T(8,128)S(1)}, u32[]{:S(2)}, u32[]{:S(2)}) collective-permute-start(f32[4,384,128]{2,1,0:T(8,128)S(1)} %get-tuple-element.62), channel_id=1, source_target_pairs={{1,0},{2,1},{3,2},{4,3},{5,4},{6,5},{7,6},{8,7},{9,8},{10,9},{11,1... | collective-permute-start | bytes 2359304 | tf_op jit(solution)/shard_map/ppermute | solution.py:377
  103.5 8.3 %collective-permute-start.18 = (f32[4,128,128]{2,1,0:T(8,128)S(1)}, f32[4,128,128]{2,1,0:T(8,128)S(1)}, u32[]{:S(2)}, u32[]{:S(2)}) collective-permute-start(f32[4,128,128]{2,1,0:T(8,128)S(1)} %get-tuple-element.65), channel_id=1, source_target_pairs={{0,32},{32,64},{64,96},{96,128},{128,160},{160,192},{192,224},{1,3... | collective-permute-start | bytes 786440 | tf_op jit(solution)/shard_map/ppermute | solution.py:377
  106.8 18.4 %collective-permute-start.16 = (f32[4,128,256]{2,1,0:T(8,128)S(1)}, f32[4,128,256]{2,1,0:T(8,128)S(1)}, u32[]{:S(2)}, u32[]{:S(2)}) collective-permute-start(f32[4,128,256]{2,1,0:T(8,128)S(1)} %get-tuple-element.63), channel_id=1, source_target_pairs={{0,32},{32,64},{64,96},{96,128},{128,160},{160,192},{192,224},{1,3... | collective-permute-start | bytes 1572872 | tf_op jit(solution)/shard_map/ppermute | solution.py:377
  110.5 14.6 %collective-permute-start.17 = (f32[4,128,256]{2,1,0:T(8,128)S(1)}, f32[4,128,256]{2,1,0:T(8,128)S(1)}, u32[]{:S(2)}, u32[]{:S(2)}) collective-permute-start(f32[4,128,256]{2,1,0:T(8,128)S(1)} %get-tuple-element.64), channel_id=1, source_target_pairs={{32,0},{64,32},{96,64},{128,96},{160,128},{192,160},{224,192},{33,... | collective-permute-start | bytes 1572872 | tf_op jit(solution)/shard_map/ppermute | solution.py:377
  111.8 13.3 %collective-permute-start.19 = (f32[4,128,128]{2,1,0:T(8,128)S(1)}, f32[4,128,128]{2,1,0:T(8,128)S(1)}, u32[]{:S(2)}, u32[]{:S(2)}) collective-permute-start(f32[4,128,128]{2,1,0:T(8,128)S(1)} %get-tuple-element.66), channel_id=1, source_target_pairs={{32,0},{64,32},{96,64},{128,96},{160,128},{192,160},{224,192},{33,... | collective-permute-start | bytes 786440 | tf_op jit(solution)/shard_map/ppermute | solution.py:377
  127.2 31.5 %collective-permute-start.20 = (f32[4,128,128]{2,1,0:T(8,128)S(1)}, f32[4,128,128]{2,1,0:T(8,128)S(1)}, u32[]{:S(2)}, u32[]{:S(2)}) collective-permute-start(f32[4,128,128]{2,1,0:T(8,128)S(1)} %get-tuple-element.71), channel_id=1, source_target_pairs={{0,32},{32,64},{64,96},{96,128},{128,160},{160,192},{192,224},{1,3... | collective-permute-start | bytes 786440 | tf_op jit(solution)/shard_map/ppermute | solution.py:377
  152.9 31.0 %collective-permute-start.24 = (f32[4,128,256]{2,1,0:T(8,128)S(1)}, f32[4,128,256]{2,1,0:T(8,128)S(1)}, u32[]{:S(2)}, u32[]{:S(2)}) collective-permute-start(f32[4,128,256]{2,1,0:T(8,128)S(1)} %get-tuple-element.76), channel_id=1, source_target_pairs={{0,32},{32,64},{64,96},{96,128},{128,160},{160,192},{192,224},{1,3... | collective-permute-start | bytes 1572872 | tf_op jit(solution)/shard_map/ppermute | solution.py:377
  154.8 16.0 %collective-permute-start.22 = (f32[2,384,128]{2,1,0:T(8,128)S(1)}, f32[2,384,128]{2,1,0:T(8,128)S(1)}, u32[]{:S(2)}, u32[]{:S(2)}) collective-permute-start(f32[2,384,128]{2,1,0:T(8,128)S(1)} %get-tuple-element.74), channel_id=1, source_target_pairs={{0,1},{1,2},{2,3},{3,4},{4,5},{5,6},{6,7},{7,8},{8,9},{9,10},{10,1... | collective-permute-start | bytes 1179656 | tf_op jit(solution)/shard_map/ppermute | solution.py:377
  156.7 22.5 %collective-permute-start.21 = (f32[2,384,128]{2,1,0:T(8,128)S(1)}, f32[2,384,128]{2,1,0:T(8,128)S(1)}, u32[]{:S(2)}, u32[]{:S(2)}) collective-permute-start(f32[2,384,128]{2,1,0:T(8,128)S(1)} %get-tuple-element.73), channel_id=1, source_target_pairs={{0,1},{1,2},{2,3},{3,4},{4,5},{5,6},{6,7},{7,8},{8,9},{9,10},{10,1... | collective-permute-start | bytes 1179656 | tf_op jit(solution)/shard_map/ppermute | solution.py:377
  158.9 24.9 %collective-permute-start.23 = (f32[4,128,128]{2,1,0:T(8,128)S(1)}, f32[4,128,128]{2,1,0:T(8,128)S(1)}, u32[]{:S(2)}, u32[]{:S(2)}) collective-permute-start(f32[4,128,128]{2,1,0:T(8,128)S(1)} %get-tuple-element.75), channel_id=1, source_target_pairs={{0,1},{1,2},{2,3},{3,4},{4,5},{5,6},{6,7},{7,8},{8,9},{9,10},{10,1... | collective-permute-start | bytes 786440 | tf_op jit(solution)/shard_map/ppermute | solution.py:377
  (1 other events, 2.3 us)

commit v6 on v5

--- a/solution.py
+++ b/solution.py
@@ -199,7 +199,7 @@
     return lax.axis_index(axis) < lax.axis_size(axis) - 1
 
 
-def assemble_kernel(main, right_top, right_rest, bottom, *rest):
+def assemble_kernel(main, right_top, right_rest, bottom, corner, *rest):
     state = rest[-1]
     first = 0 if len(rest) == 1 else 2
     for k in range(2):
@@ -207,7 +207,8 @@
         state[p, :ROWS, :COLS] = main[first // 2, k]
         state[p, :HALF, COLS:] = right_top[p]
         state[p, HALF:ROWS, COLS:] = right_rest[k]
-        state[p, ROWS:, :] = bottom[p]
+        state[p, ROWS:, :COLS] = bottom[p]
+        state[p, ROWS:, COLS:] = corner[p]
 
 
 def fold_sides(old, state, mid_l, mid_r, above, below, core_a, core_b):
@@ -388,12 +389,16 @@
     amp, prop, grad = call(
         prep_kernel, (), (amplitude, phase), [(SLOTS, WIN, WIN), (2, WIN, WIN), EXT]
     )
-    low = cc([planes[:, :h, :], right_top], 2)
-    bottom = from_behind(low, "row", -1)
-    (state,) = call(assemble_kernel, (), (transmission, right_top, right_1, bottom), [EXT])
+    bottom = from_behind(planes[:, :h, :], "row", -1)
+    corner = from_behind(right_top, "row", -1)
+    (state,) = call(assemble_kernel, (), (transmission, right_top, right_1, bottom, corner), [EXT])
     (between,) = call(early_kernel, scalars, (tab, probe, prop, state), [PLANES])
     (state,) = call(
-        assemble_kernel, (), (transmission, right_top, right_2, bottom, state), [EXT], {4: 0}
+        assemble_kernel,
+        (),
+        (transmission, right_top, right_2, bottom, corner, state),
+        [EXT],
+        {5: 0},
     )
     edges = [MIDS, MIDS, ENDS, ENDS, CORE, CORE]
     for b in range(BATCHES - 1):

time: 186 us -> 182 us (0.978)
  waiting for transfers between devices: 51.9 us -> 46.7 us
  local copies, waits for them, and re-layouts: 3.45 us -> 6.72 us
  starting transfers between devices: 108 us -> 105 us
    ppermute x25 -> x26, waiting for transfers between devices: 51.9 us -> 46.7 us  [from_behind(): return lax.ppermute(array, axis, pairs)]
    unnamed x16, local copies, waits for them, and re-layouts: 0.04 us -> 3.32 us
    ppermute x25 -> x26, starting transfers between devices: 108 us -> 105 us  [from_behind(): return lax.ppermute(array, axis, pairs)]
  transfers between devices with their start and end apart: 25 -> 26, of which waited for: 11 -> 8; matrix products, arithmetic and copies ran while one was open for 1% -> 1% of each run, Pallas kernels for 5% -> 6%
where the time goes in v6:
time: 182 us; the launch traced here: 181 us
  starting transfers between devices  105 us (58%)
  waiting for transfers between devices  46.7 us (26%)
  Pallas kernels  20.8 us (11%)
  local copies, waits for them, and re-layouts  6.72 us (4%)
    ppermute x26, starting transfers between devices, from_behind(): return lax.ppermute(array, axis, pairs)  105 us
    ppermute x26, waiting for transfers between devices, from_behind(): return lax.ppermute(array, axis, pairs)  46.7 us
    pallas_call x14, Pallas kernels, call(): pl.pallas_call(kernel, in_specs=[SM] * len(scalars) + [VM] * len(arrays),...  20.8 us
  transfers between devices with their start and end apart: 26, of which 8 were waited for; matrix products, arithmetic and copies ran while one was open for 1% of the time, Pallas kernels for 6%

profile of v6, /device:TPU:6, one launch (start us, length us, event | category | flops | bytes accessed | tf_op | source)
XLA Modules:
  0.0 180.6 jit_solution(1075507362589555122)
XLA Ops:
  1.1 8.0 %collective-permute-start = (f32[4,128,128]{2,1,0:T(8,128)S(1)}, f32[4,128,128]{2,1,0:T(8,128)S(1)}, u32[]{:S(2)}, u32[]{:S(2)}) collective-permute-start(f32[4,128,128]{2,1,0:T(8,128)S(1)} %slice.16), channel_id=1, source_target_pairs={{1,0},{2,1},{3,2},{4,3},{5,4},{6,5},{7,6},{8,7},{9,8},{10,9},{11,1... | collective-permute-start | bytes 786440 | tf_op jit(solution)/shard_map/ppermute | solution.py:378
  12.8 2.9 %collective-permute-start.4 = (f32[2,384,128]{2,1,0:T(8,128)S(1)}, f32[2,384,128]{2,1,0:T(8,128)S(1)}, u32[]{:S(2)}, u32[]{:S(2)}) collective-permute-start(f32[2,384,128]{2,1,0:T(8,128)S(1)} %get-tuple-element.77), channel_id=1, source_target_pairs={{1,0},{2,1},{3,2},{4,3},{5,4},{6,5},{7,6},{8,7},{9,8},{10,9},{11,1... | collective-permute-start | bytes 1179656 | tf_op jit(solution)/shard_map/ppermute | solution.py:378
  15.7 2.9 %collective-permute-start.1 = (f32[2,384,128]{2,1,0:T(8,128)S(1)}, f32[2,384,128]{2,1,0:T(8,128)S(1)}, u32[]{:S(2)}, u32[]{:S(2)}) collective-permute-start(f32[2,384,128]{2,1,0:T(8,128)S(1)} %get-tuple-element.78), channel_id=1, source_target_pairs={{1,0},{2,1},{3,2},{4,3},{5,4},{6,5},{7,6},{8,7},{9,8},{10,9},{11,1... | collective-permute-start | bytes 1179656 | tf_op jit(solution)/shard_map/ppermute | solution.py:378
  22.7 4.5 %shard_map.91 = (f32[4,256,256]{2,1,0:T(8,128)S(1)}, f32[2,256,256]{2,1,0:T(8,128)S(1)}, f32[4,640,384]{2,1,0:T(8,128)S(1)}) custom-call(f32[1,1,4,256,256]{4,3,2,1,0:T(8,128)S(1)} %copy-done.3, f32[256,256]{1,0:T(8,128)S(1)} %copy-done.4), custom_call_target="tpu_custom_call" | custom-call | tf_op jit(solution)/shard_map/pallas_call | solution.py:365
  29.2 5.7 %collective-permute-done.1.right_rest = f32[2,384,128]{2,1,0:T(8,128)S(1)} collective-permute-done((f32[2,384,128]{2,1,0:T(8,128)S(1)}, f32[2,384,128]{2,1,0:T(8,128)S(1)}, u32[]{:S(2)}, u32[]{:S(2)}) %collective-permute-start.1) | collective-permute-done | bytes 393248 | tf_op jit(solution)/shard_map/ppermute | solution.py:378
  35.9 1.9 %collective-permute-start.5 = (f32[4,256,128]{2,1,0:T(8,128)S(1)}, f32[4,256,128]{2,1,0:T(8,128)S(1)}, u32[]{:S(2)}, u32[]{:S(2)}) collective-permute-start(f32[4,256,128]{2,1,0:T(8,128)S(1)} %get-tuple-element.45), channel_id=1, source_target_pairs={{0,1},{1,2},{2,3},{3,4},{4,5},{5,6},{6,7},{7,8},{8,9},{9,10},{10,1... | collective-permute-start | bytes 1572872 | tf_op jit(solution)/shard_map/ppermute | solution.py:378
  37.8 8.3 %collective-permute-start.6 = (f32[4,256,128]{2,1,0:T(8,128)S(1)}, f32[4,256,128]{2,1,0:T(8,128)S(1)}, u32[]{:S(2)}, u32[]{:S(2)}) collective-permute-start(f32[4,256,128]{2,1,0:T(8,128)S(1)} %get-tuple-element.46), channel_id=1, source_target_pairs={{1,0},{2,1},{3,2},{4,3},{5,4},{6,5},{7,6},{8,7},{9,8},{10,9},{11,1... | collective-permute-start | bytes 1572872 | tf_op jit(solution)/shard_map/ppermute | solution.py:378
  46.1 1.9 %collective-permute-start.7 = (f32[4,384,128]{2,1,0:T(8,128)S(1)}, f32[4,384,128]{2,1,0:T(8,128)S(1)}, u32[]{:S(2)}, u32[]{:S(2)}) collective-permute-start(f32[4,384,128]{2,1,0:T(8,128)S(1)} %get-tuple-element.49), channel_id=1, source_target_pairs={{0,1},{1,2},{2,3},{3,4},{4,5},{5,6},{6,7},{7,8},{8,9},{9,10},{10,1... | collective-permute-start | bytes 2359304 | tf_op jit(solution)/shard_map/ppermute | solution.py:378
  48.0 6.0 %collective-permute-start.8 = (f32[4,384,128]{2,1,0:T(8,128)S(1)}, f32[4,384,128]{2,1,0:T(8,128)S(1)}, u32[]{:S(2)}, u32[]{:S(2)}) collective-permute-start(f32[4,384,128]{2,1,0:T(8,128)S(1)} %get-tuple-element.50), channel_id=1, source_target_pairs={{1,0},{2,1},{3,2},{4,3},{5,4},{6,5},{7,6},{8,7},{9,8},{10,9},{11,1... | collective-permute-start | bytes 2359304 | tf_op jit(solution)/shard_map/ppermute | solution.py:378
  54.1 4.5 %collective-permute-start.11 = (f32[4,128,128]{2,1,0:T(8,128)S(1)}, f32[4,128,128]{2,1,0:T(8,128)S(1)}, u32[]{:S(2)}, u32[]{:S(2)}) collective-permute-start(f32[4,128,128]{2,1,0:T(8,128)S(1)} %get-tuple-element.53), channel_id=1, source_target_pairs={{0,32},{32,64},{64,96},{96,128},{128,160},{160,192},{192,224},{1,3... | collective-permute-start | bytes 786440 | tf_op jit(solution)/shard_map/ppermute | solution.py:378
  58.8 4.3 %collective-permute-start.9 = (f32[4,128,256]{2,1,0:T(8,128)S(1)}, f32[4,128,256]{2,1,0:T(8,128)S(1)}, u32[]{:S(2)}, u32[]{:S(2)}) collective-permute-start(f32[4,128,256]{2,1,0:T(8,128)S(1)} %get-tuple-element.51), channel_id=1, source_target_pairs={{0,32},{32,64},{64,96},{96,128},{128,160},{160,192},{192,224},{1,3... | collective-permute-start | bytes 1572872 | tf_op jit(solution)/shard_map/ppermute | solution.py:378
  65.9 2.2 %shard_map.96 = (f32[4,640,384]{2,1,0:T(8,128)S(1)}, f32[4,640,384]{2,1,0:T(8,128)S(1)}) custom-call(f32[4,640,384]{2,1,0:T(8,128)S(1)} %shard_map.93.state, f32[4,640,384]{2,1,0:T(8,128)S(1)} %get-tuple-element.44.grad, f32[4,256,128]{2,1,0:T(8,128)S(1)} %collective-permute-done.5.end_l, ...), custom_call_target="tpu_custom_call", output_to_operand_aliasing={{0}: (0, {}), {1}: (1, {})} | custom-call | tf_op jit(solution)/shard_map/pallas_call | solution.py:365
  68.4 2.6 %collective-permute-done.7.rest_1_ = f32[4,384,128]{2,1,0:T(8,128)S(1)} collective-permute-done((f32[4,384,128]{2,1,0:T(8,128)S(1)}, f32[4,384,128]{2,1,0:T(8,128)S(1)}, u32[]{:S(2)}, u32[]{:S(2)}) %collective-permute-start.7) | collective-permute-done | bytes 786464 | tf_op jit(solution)/shard_map/ppermute | solution.py:378
  71.0 1.7 collective-permute-done.8.rest_2_
  72.8 6.2 %shard_map.98 = (f32[4,640,384]{2,1,0:T(8,128)S(1)}, f32[4,640,384]{2,1,0:T(8,128)S(1)}, f32[4,384,128]{2,1,0:T(8,128)S(1)}, f32[4,384,128]{2,1,0:T(8,128)S(1)},...) custom-call(s32[1,1]{1,0:T(1,128)S(6)} %copy.32.count, ...), custom_call_target="tpu_custom_call", output_to_operand_aliasing={{0}: (8, {}), {1}: (9, {})} | custom-call | tf_op jit(solution)/shard_map/pallas_call | solution.py:365
  79.0 1.9 %collective-permute-start.13 = (f32[4,256,128]{2,1,0:T(8,128)S(1)}, f32[4,256,128]{2,1,0:T(8,128)S(1)}, u32[]{:S(2)}, u32[]{:S(2)}) collective-permute-start(f32[4,256,128]{2,1,0:T(8,128)S(1)} %get-tuple-element.57), channel_id=1, source_target_pairs={{0,1},{1,2},{2,3},{3,4},{4,5},{5,6},{6,7},{7,8},{8,9},{9,10},{10,1... | collective-permute-start | bytes 1572872 | tf_op jit(solution)/shard_map/ppermute | solution.py:378
  80.9 6.5 %collective-permute-start.14 = (f32[4,256,128]{2,1,0:T(8,128)S(1)}, f32[4,256,128]{2,1,0:T(8,128)S(1)}, u32[]{:S(2)}, u32[]{:S(2)}) collective-permute-start(f32[4,256,128]{2,1,0:T(8,128)S(1)} %get-tuple-element.58), channel_id=1, source_target_pairs={{1,0},{2,1},{3,2},{4,3},{5,4},{6,5},{7,6},{8,7},{9,8},{10,9},{11,1... | collective-permute-start | bytes 1572872 | tf_op jit(solution)/shard_map/ppermute | solution.py:378
  87.4 1.9 %collective-permute-start.15 = (f32[4,384,128]{2,1,0:T(8,128)S(1)}, f32[4,384,128]{2,1,0:T(8,128)S(1)}, u32[]{:S(2)}, u32[]{:S(2)}) collective-permute-start(f32[4,384,128]{2,1,0:T(8,128)S(1)} %get-tuple-element.61), channel_id=1, source_target_pairs={{0,1},{1,2},{2,3},{3,4},{4,5},{5,6},{6,7},{7,8},{8,9},{9,10},{10,1... | collective-permute-start | bytes 2359304 | tf_op jit(solution)/shard_map/ppermute | solution.py:378
  89.3 6.0 %collective-permute-start.16 = (f32[4,384,128]{2,1,0:T(8,128)S(1)}, f32[4,384,128]{2,1,0:T(8,128)S(1)}, u32[]{:S(2)}, u32[]{:S(2)}) collective-permute-start(f32[4,384,128]{2,1,0:T(8,128)S(1)} %get-tuple-element.62), channel_id=1, source_target_pairs={{1,0},{2,1},{3,2},{4,3},{5,4},{6,5},{7,6},{8,7},{9,8},{10,9},{11,1... | collective-permute-start | bytes 2359304 | tf_op jit(solution)/shard_map/ppermute | solution.py:378
  95.4 3.7 %collective-permute-start.19 = (f32[4,128,128]{2,1,0:T(8,128)S(1)}, f32[4,128,128]{2,1,0:T(8,128)S(1)}, u32[]{:S(2)}, u32[]{:S(2)}) collective-permute-start(f32[4,128,128]{2,1,0:T(8,128)S(1)} %get-tuple-element.65), channel_id=1, source_target_pairs={{0,32},{32,64},{64,96},{96,128},{128,160},{160,192},{192,224},{1,3... | collective-permute-start | bytes 786440 | tf_op jit(solution)/shard_map/ppermute | solution.py:378
  99.2 3.6 %collective-permute-start.17 = (f32[4,128,256]{2,1,0:T(8,128)S(1)}, f32[4,128,256]{2,1,0:T(8,128)S(1)}, u32[]{:S(2)}, u32[]{:S(2)}) collective-permute-start(f32[4,128,256]{2,1,0:T(8,128)S(1)} %get-tuple-element.63), channel_id=1, source_target_pairs={{0,32},{32,64},{64,96},{96,128},{128,160},{160,192},{192,224},{1,3... | collective-permute-start | bytes 1572872 | tf_op jit(solution)/shard_map/ppermute | solution.py:378
  105.6 2.2 %shard_map.99 = (f32[4,640,384]{2,1,0:T(8,128)S(1)}, f32[4,640,384]{2,1,0:T(8,128)S(1)}) custom-call(f32[4,640,384]{2,1,0:T(8,128)S(1)} %get-tuple-element.55.state, f32[4,640,384]{2,1,0:T(8,128)S(1)} %get-tuple-element.56.grad, f32[4,256,128]{2,1,0:T(8,128)S(1)} %collective-permute-done.13.end_l, ...), custom_call_target="tpu_custom_call", output_to_operand_aliasing={{0}: (0, {}), {1}: (1, {})} | custom-call | tf_op jit(solution)/shard_map/pallas_call | solution.py:365
  107.8 13.2 %collective-permute-done.20.rest_6_ = f32[4,128,128]{2,1,0:T(8,128)S(1)} collective-permute-done((f32[4,128,128]{2,1,0:T(8,128)S(1)}, f32[4,128,128]{2,1,0:T(8,128)S(1)}, u32[]{:S(2)}, u32[]{:S(2)}) %collective-permute-start.20) | collective-permute-done | bytes 262176 | tf_op jit(solution)/shard_map/ppermute | solution.py:378
  123.1 25.0 %collective-permute-start.21 = (f32[4,128,128]{2,1,0:T(8,128)S(1)}, f32[4,128,128]{2,1,0:T(8,128)S(1)}, u32[]{:S(2)}, u32[]{:S(2)}) collective-permute-start(f32[4,128,128]{2,1,0:T(8,128)S(1)} %get-tuple-element.71), channel_id=1, source_target_pairs={{0,32},{32,64},{64,96},{96,128},{128,160},{160,192},{192,224},{1,3... | collective-permute-start | bytes 786440 | tf_op jit(solution)/shard_map/ppermute | solution.py:378
  148.1 1.9 %collective-permute-start.25 = (f32[4,128,256]{2,1,0:T(8,128)S(1)}, f32[4,128,256]{2,1,0:T(8,128)S(1)}, u32[]{:S(2)}, u32[]{:S(2)}) collective-permute-start(f32[4,128,256]{2,1,0:T(8,128)S(1)} %get-tuple-element.76), channel_id=1, source_target_pairs={{0,32},{32,64},{64,96},{96,128},{128,160},{160,192},{192,224},{1,3... | collective-permute-start | bytes 1572872 | tf_op jit(solution)/shard_map/ppermute | solution.py:378
  150.0 1.9 %collective-permute-start.23 = (f32[2,384,128]{2,1,0:T(8,128)S(1)}, f32[2,384,128]{2,1,0:T(8,128)S(1)}, u32[]{:S(2)}, u32[]{:S(2)}) collective-permute-start(f32[2,384,128]{2,1,0:T(8,128)S(1)} %get-tuple-element.74), channel_id=1, source_target_pairs={{0,1},{1,2},{2,3},{3,4},{4,5},{5,6},{6,7},{7,8},{8,9},{9,10},{10,1... | collective-permute-start | bytes 1179656 | tf_op jit(solution)/shard_map/ppermute | solution.py:378
  152.0 1.9 %collective-permute-start.22 = (f32[2,384,128]{2,1,0:T(8,128)S(1)}, f32[2,384,128]{2,1,0:T(8,128)S(1)}, u32[]{:S(2)}, u32[]{:S(2)}) collective-permute-start(f32[2,384,128]{2,1,0:T(8,128)S(1)} %get-tuple-element.73), channel_id=1, source_target_pairs={{0,1},{1,2},{2,3},{3,4},{4,5},{5,6},{6,7},{7,8},{8,9},{9,10},{10,1... | collective-permute-start | bytes 1179656 | tf_op jit(solution)/shard_map/ppermute | solution.py:378
  154.2 1.9 %collective-permute-start.24 = (f32[4,128,128]{2,1,0:T(8,128)S(1)}, f32[4,128,128]{2,1,0:T(8,128)S(1)}, u32[]{:S(2)}, u32[]{:S(2)}) collective-permute-start(f32[4,128,128]{2,1,0:T(8,128)S(1)} %get-tuple-element.75), channel_id=1, source_target_pairs={{0,1},{1,2},{2,3},{3,4},{4,5},{5,6},{6,7},{7,8},{8,9},{9,10},{10,1... | collective-permute-start | bytes 786440 | tf_op jit(solution)/shard_map/ppermute | solution.py:378
  156.1 9.9 %collective-permute-done.23.mid2 = f32[2,384,128]{2,1,0:T(8,128)S(1)} collective-permute-done((f32[2,384,128]{2,1,0:T(8,128)S(1)}, f32[2,384,128]{2,1,0:T(8,128)S(1)}, u32[]{:S(2)}, u32[]{:S(2)}) %collective-permute-start.23) | collective-permute-done | bytes 393248 | tf_op jit(solution)/shard_map/ppermute | solution.py:378
  166.0 8.4 %collective-permute-done.22.mid1 = f32[2,384,128]{2,1,0:T(8,128)S(1)} collective-permute-done((f32[2,384,128]{2,1,0:T(8,128)S(1)}, f32[2,384,128]{2,1,0:T(8,128)S(1)}, u32[]{:S(2)}, u32[]{:S(2)}) %collective-permute-start.22) | collective-permute-done | bytes 393248 | tf_op jit(solution)/shard_map/ppermute | solution.py:378
  174.4 4.6 %collective-permute-done.24.end = f32[4,128,128]{2,1,0:T(8,128)S(1)} collective-permute-done((f32[4,128,128]{2,1,0:T(8,128)S(1)}, f32[4,128,128]{2,1,0:T(8,128)S(1)}, u32[]{:S(2)}, u32[]{:S(2)}) %collective-permute-start.24) | collective-permute-done | bytes 262176 | tf_op jit(solution)/shard_map/ppermute | solution.py:378
  179.1 1.5 shard_map.104
  (53 shorter events, 19.6 us)
Async XLA Ops:
  0.0 27.3 %copy-start.1 = (f32[2,2,512,256]{3,2,1,0:T(8,128)S(1)}, f32[2,2,512,256]{3,2,1,0:T(8,128)}, u32[]{:S(2)}) copy-start(f32[2,2,512,256]{3,2,1,0:T(8,128)} %main.3) | copy-start | bytes 6291460
  1.1 17.5 %collective-permute-start = (f32[4,128,128]{2,1,0:T(8,128)S(1)}, f32[4,128,128]{2,1,0:T(8,128)S(1)}, u32[]{:S(2)}, u32[]{:S(2)}) collective-permute-start(f32[4,128,128]{2,1,0:T(8,128)S(1)} %slice.16), channel_id=1, source_target_pairs={{1,0},{2,1},{3,2},{4,3},{5,4},{6,5},{7,6},{8,7},{9,8},{10,9},{11,1... | collective-permute-start | bytes 786440 | tf_op jit(solution)/shard_map/ppermute | solution.py:378
  10.3 17.1 %collective-permute-start.2 = (f32[4,128,256]{2,1,0:T(8,128)S(1)}, f32[4,128,256]{2,1,0:T(8,128)S(1)}, u32[]{:S(2)}, u32[]{:S(2)}) collective-permute-start(f32[4,128,256]{2,1,0:T(8,128)S(1)} %slice.18), channel_id=1, source_target_pairs={{32,0},{64,32},{96,64},{128,96},{160,128},{192,160},{224,192},{33,... | collective-permute-start | bytes 1572872 | tf_op jit(solution)/shard_map/ppermute | solution.py:378
  12.8 14.6 %collective-permute-start.4 = (f32[2,384,128]{2,1,0:T(8,128)S(1)}, f32[2,384,128]{2,1,0:T(8,128)S(1)}, u32[]{:S(2)}, u32[]{:S(2)}) collective-permute-start(f32[2,384,128]{2,1,0:T(8,128)S(1)} %get-tuple-element.77), channel_id=1, source_target_pairs={{1,0},{2,1},{3,2},{4,3},{5,4},{6,5},{7,6},{8,7},{9,8},{10,9},{11,1... | collective-permute-start | bytes 1179656 | tf_op jit(solution)/shard_map/ppermute | solution.py:378
  15.7 19.2 %collective-permute-start.1 = (f32[2,384,128]{2,1,0:T(8,128)S(1)}, f32[2,384,128]{2,1,0:T(8,128)S(1)}, u32[]{:S(2)}, u32[]{:S(2)}) collective-permute-start(f32[2,384,128]{2,1,0:T(8,128)S(1)} %get-tuple-element.78), channel_id=1, source_target_pairs={{1,0},{2,1},{3,2},{4,3},{5,4},{6,5},{7,6},{8,7},{9,8},{10,9},{11,1... | collective-permute-start | bytes 1179656 | tf_op jit(solution)/shard_map/ppermute | solution.py:378
  18.6 8.7 %collective-permute-start.3 = (f32[4,128,128]{2,1,0:T(8,128)S(1)}, f32[4,128,128]{2,1,0:T(8,128)S(1)}, u32[]{:S(2)}, u32[]{:S(2)}) collective-permute-start(f32[4,128,128]{2,1,0:T(8,128)S(1)} %collective-permute-done.right_top), channel_id=1, source_target_pairs={{32,0},{64,32},{96,64},{128,96},{160,128},{192,160},{224,192},{33,... | collective-permute-start | bytes 786440 | tf_op jit(solution)/shard_map/ppermute | solution.py:378
  27.3 1.2 copy-start
  27.3 1.3 copy-start.2
  27.3 1.3 copy-start.5
  27.3 1.3 copy-start.6
  27.3 1.3 copy-start.7
  35.9 22.7 %collective-permute-start.5 = (f32[4,256,128]{2,1,0:T(8,128)S(1)}, f32[4,256,128]{2,1,0:T(8,128)S(1)}, u32[]{:S(2)}, u32[]{:S(2)}) collective-permute-start(f32[4,256,128]{2,1,0:T(8,128)S(1)} %get-tuple-element.45), channel_id=1, source_target_pairs={{0,1},{1,2},{2,3},{3,4},{4,5},{5,6},{6,7},{7,8},{8,9},{9,10},{10,1... | collective-permute-start | bytes 1572872 | tf_op jit(solution)/shard_map/ppermute | solution.py:378
  37.8 20.8 %collective-permute-start.6 = (f32[4,256,128]{2,1,0:T(8,128)S(1)}, f32[4,256,128]{2,1,0:T(8,128)S(1)}, u32[]{:S(2)}, u32[]{:S(2)}) collective-permute-start(f32[4,256,128]{2,1,0:T(8,128)S(1)} %get-tuple-element.46), channel_id=1, source_target_pairs={{1,0},{2,1},{3,2},{4,3},{5,4},{6,5},{7,6},{8,7},{9,8},{10,9},{11,1... | collective-permute-start | bytes 1572872 | tf_op jit(solution)/shard_map/ppermute | solution.py:378
  46.1 24.9 %collective-permute-start.7 = (f32[4,384,128]{2,1,0:T(8,128)S(1)}, f32[4,384,128]{2,1,0:T(8,128)S(1)}, u32[]{:S(2)}, u32[]{:S(2)}) collective-permute-start(f32[4,384,128]{2,1,0:T(8,128)S(1)} %get-tuple-element.49), channel_id=1, source_target_pairs={{0,1},{1,2},{2,3},{3,4},{4,5},{5,6},{6,7},{7,8},{8,9},{9,10},{10,1... | collective-permute-start | bytes 2359304 | tf_op jit(solution)/shard_map/ppermute | solution.py:378
  48.0 24.7 %collective-permute-start.8 = (f32[4,384,128]{2,1,0:T(8,128)S(1)}, f32[4,384,128]{2,1,0:T(8,128)S(1)}, u32[]{:S(2)}, u32[]{:S(2)}) collective-permute-start(f32[4,384,128]{2,1,0:T(8,128)S(1)} %get-tuple-element.50), channel_id=1, source_target_pairs={{1,0},{2,1},{3,2},{4,3},{5,4},{6,5},{7,6},{8,7},{9,8},{10,9},{11,1... | collective-permute-start | bytes 2359304 | tf_op jit(solution)/shard_map/ppermute | solution.py:378
  54.1 10.3 %collective-permute-start.11 = (f32[4,128,128]{2,1,0:T(8,128)S(1)}, f32[4,128,128]{2,1,0:T(8,128)S(1)}, u32[]{:S(2)}, u32[]{:S(2)}) collective-permute-start(f32[4,128,128]{2,1,0:T(8,128)S(1)} %get-tuple-element.53), channel_id=1, source_target_pairs={{0,32},{32,64},{64,96},{96,128},{128,160},{160,192},{192,224},{1,3... | collective-permute-start | bytes 786440 | tf_op jit(solution)/shard_map/ppermute | solution.py:378
  58.8 14.0 %collective-permute-start.9 = (f32[4,128,256]{2,1,0:T(8,128)S(1)}, f32[4,128,256]{2,1,0:T(8,128)S(1)}, u32[]{:S(2)}, u32[]{:S(2)}) collective-permute-start(f32[4,128,256]{2,1,0:T(8,128)S(1)} %get-tuple-element.51), channel_id=1, source_target_pairs={{0,32},{32,64},{64,96},{96,128},{128,160},{160,192},{192,224},{1,3... | collective-permute-start | bytes 1572872 | tf_op jit(solution)/shard_map/ppermute | solution.py:378
  63.1 9.7 %collective-permute-start.10 = (f32[4,128,256]{2,1,0:T(8,128)S(1)}, f32[4,128,256]{2,1,0:T(8,128)S(1)}, u32[]{:S(2)}, u32[]{:S(2)}) collective-permute-start(f32[4,128,256]{2,1,0:T(8,128)S(1)} %get-tuple-element.52), channel_id=1, source_target_pairs={{32,0},{64,32},{96,64},{128,96},{160,128},{192,160},{224,192},{33,... | collective-permute-start | bytes 1572872 | tf_op jit(solution)/shard_map/ppermute | solution.py:378
  64.4 4.1 %collective-permute-start.12 = (f32[4,128,128]{2,1,0:T(8,128)S(1)}, f32[4,128,128]{2,1,0:T(8,128)S(1)}, u32[]{:S(2)}, u32[]{:S(2)}) collective-permute-start(f32[4,128,128]{2,1,0:T(8,128)S(1)} %get-tuple-element.54), channel_id=1, source_target_pairs={{32,0},{64,32},{96,64},{128,96},{160,128},{192,160},{224,192},{33,... | collective-permute-start | bytes 786440 | tf_op jit(solution)/shard_map/ppermute | solution.py:378
  79.0 20.1 %collective-permute-start.13 = (f32[4,256,128]{2,1,0:T(8,128)S(1)}, f32[4,256,128]{2,1,0:T(8,128)S(1)}, u32[]{:S(2)}, u32[]{:S(2)}) collective-permute-start(f32[4,256,128]{2,1,0:T(8,128)S(1)} %get-tuple-element.57), channel_id=1, source_target_pairs={{0,1},{1,2},{2,3},{3,4},{4,5},{5,6},{6,7},{7,8},{8,9},{9,10},{10,1... | collective-permute-start | bytes 1572872 | tf_op jit(solution)/shard_map/ppermute | solution.py:378
  80.9 18.2 %collective-permute-start.14 = (f32[4,256,128]{2,1,0:T(8,128)S(1)}, f32[4,256,128]{2,1,0:T(8,128)S(1)}, u32[]{:S(2)}, u32[]{:S(2)}) collective-permute-start(f32[4,256,128]{2,1,0:T(8,128)S(1)} %get-tuple-element.58), channel_id=1, source_target_pairs={{1,0},{2,1},{3,2},{4,3},{5,4},{6,5},{7,6},{8,7},{9,8},{10,9},{11,1... | collective-permute-start | bytes 1572872 | tf_op jit(solution)/shard_map/ppermute | solution.py:378
  87.4 33.6 %collective-permute-start.15 = (f32[4,384,128]{2,1,0:T(8,128)S(1)}, f32[4,384,128]{2,1,0:T(8,128)S(1)}, u32[]{:S(2)}, u32[]{:S(2)}) collective-permute-start(f32[4,384,128]{2,1,0:T(8,128)S(1)} %get-tuple-element.61), channel_id=1, source_target_pairs={{0,1},{1,2},{2,3},{3,4},{4,5},{5,6},{6,7},{7,8},{8,9},{9,10},{10,1... | collective-permute-start | bytes 2359304 | tf_op jit(solution)/shard_map/ppermute | solution.py:378
  89.3 31.7 %collective-permute-start.16 = (f32[4,384,128]{2,1,0:T(8,128)S(1)}, f32[4,384,128]{2,1,0:T(8,128)S(1)}, u32[]{:S(2)}, u32[]{:S(2)}) collective-permute-start(f32[4,384,128]{2,1,0:T(8,128)S(1)} %get-tuple-element.62), channel_id=1, source_target_pairs={{1,0},{2,1},{3,2},{4,3},{5,4},{6,5},{7,6},{8,7},{9,8},{10,9},{11,1... | collective-permute-start | bytes 2359304 | tf_op jit(solution)/shard_map/ppermute | solution.py:378
  95.4 8.7 %collective-permute-start.19 = (f32[4,128,128]{2,1,0:T(8,128)S(1)}, f32[4,128,128]{2,1,0:T(8,128)S(1)}, u32[]{:S(2)}, u32[]{:S(2)}) collective-permute-start(f32[4,128,128]{2,1,0:T(8,128)S(1)} %get-tuple-element.65), channel_id=1, source_target_pairs={{0,32},{32,64},{64,96},{96,128},{128,160},{160,192},{192,224},{1,3... | collective-permute-start | bytes 786440 | tf_op jit(solution)/shard_map/ppermute | solution.py:378
  99.2 21.8 %collective-permute-start.17 = (f32[4,128,256]{2,1,0:T(8,128)S(1)}, f32[4,128,256]{2,1,0:T(8,128)S(1)}, u32[]{:S(2)}, u32[]{:S(2)}) collective-permute-start(f32[4,128,256]{2,1,0:T(8,128)S(1)} %get-tuple-element.63), channel_id=1, source_target_pairs={{0,32},{32,64},{64,96},{96,128},{128,160},{160,192},{192,224},{1,3... | collective-permute-start | bytes 1572872 | tf_op jit(solution)/shard_map/ppermute | solution.py:378
  102.8 18.2 %collective-permute-start.18 = (f32[4,128,256]{2,1,0:T(8,128)S(1)}, f32[4,128,256]{2,1,0:T(8,128)S(1)}, u32[]{:S(2)}, u32[]{:S(2)}) collective-permute-start(f32[4,128,256]{2,1,0:T(8,128)S(1)} %get-tuple-element.64), channel_id=1, source_target_pairs={{32,0},{64,32},{96,64},{128,96},{160,128},{192,160},{224,192},{33,... | collective-permute-start | bytes 1572872 | tf_op jit(solution)/shard_map/ppermute | solution.py:378
  104.1 16.9 %collective-permute-start.20 = (f32[4,128,128]{2,1,0:T(8,128)S(1)}, f32[4,128,128]{2,1,0:T(8,128)S(1)}, u32[]{:S(2)}, u32[]{:S(2)}) collective-permute-start(f32[4,128,128]{2,1,0:T(8,128)S(1)} %get-tuple-element.66), channel_id=1, source_target_pairs={{32,0},{64,32},{96,64},{128,96},{160,128},{192,160},{224,192},{33,... | collective-permute-start | bytes 786440 | tf_op jit(solution)/shard_map/ppermute | solution.py:378
  123.1 30.8 %collective-permute-start.21 = (f32[4,128,128]{2,1,0:T(8,128)S(1)}, f32[4,128,128]{2,1,0:T(8,128)S(1)}, u32[]{:S(2)}, u32[]{:S(2)}) collective-permute-start(f32[4,128,128]{2,1,0:T(8,128)S(1)} %get-tuple-element.71), channel_id=1, source_target_pairs={{0,32},{32,64},{64,96},{96,128},{128,160},{160,192},{192,224},{1,3... | collective-permute-start | bytes 786440 | tf_op jit(solution)/shard_map/ppermute | solution.py:378
  148.1 31.0 %collective-permute-start.25 = (f32[4,128,256]{2,1,0:T(8,128)S(1)}, f32[4,128,256]{2,1,0:T(8,128)S(1)}, u32[]{:S(2)}, u32[]{:S(2)}) collective-permute-start(f32[4,128,256]{2,1,0:T(8,128)S(1)} %get-tuple-element.76), channel_id=1, source_target_pairs={{0,32},{32,64},{64,96},{96,128},{128,160},{160,192},{192,224},{1,3... | collective-permute-start | bytes 1572872 | tf_op jit(solution)/shard_map/ppermute | solution.py:378
  150.0 16.0 %collective-permute-start.23 = (f32[2,384,128]{2,1,0:T(8,128)S(1)}, f32[2,384,128]{2,1,0:T(8,128)S(1)}, u32[]{:S(2)}, u32[]{:S(2)}) collective-permute-start(f32[2,384,128]{2,1,0:T(8,128)S(1)} %get-tuple-element.74), channel_id=1, source_target_pairs={{0,1},{1,2},{2,3},{3,4},{4,5},{5,6},{6,7},{7,8},{8,9},{9,10},{10,1... | collective-permute-start | bytes 1179656 | tf_op jit(solution)/shard_map/ppermute | solution.py:378
  152.0 22.5 %collective-permute-start.22 = (f32[2,384,128]{2,1,0:T(8,128)S(1)}, f32[2,384,128]{2,1,0:T(8,128)S(1)}, u32[]{:S(2)}, u32[]{:S(2)}) collective-permute-start(f32[2,384,128]{2,1,0:T(8,128)S(1)} %get-tuple-element.73), channel_id=1, source_target_pairs={{0,1},{1,2},{2,3},{3,4},{4,5},{5,6},{6,7},{7,8},{8,9},{9,10},{10,1... | collective-permute-start | bytes 1179656 | tf_op jit(solution)/shard_map/ppermute | solution.py:378
  154.2 24.9 %collective-permute-start.24 = (f32[4,128,128]{2,1,0:T(8,128)S(1)}, f32[4,128,128]{2,1,0:T(8,128)S(1)}, u32[]{:S(2)}, u32[]{:S(2)}) collective-permute-start(f32[4,128,128]{2,1,0:T(8,128)S(1)} %get-tuple-element.75), channel_id=1, source_target_pairs={{0,1},{1,2},{2,3},{3,4},{4,5},{5,6},{6,7},{7,8},{8,9},{9,10},{10,1... | collective-permute-start | bytes 786440 | tf_op jit(solution)/shard_map/ppermute | solution.py:378
  (2 other events, 2.2 us)
